TPU v7x, 256 devices: a whole 4x4x8 slice. The times are simulated.
256 devices in a mesh: island: 4 (over x), fsdp: 64 (over y, z, core).
Axes of the slice: x: 4, y: 4, z: 8, core: 2. Of those that a mesh axis runs over, the one named last changes fastest.
Arguments:
- pseudo_grad: bfloat16 [4, 14336, 4096], P('island', 'fsdp'), may hold values from -110 to 110
- error_buffer: bfloat16 [4, 14336, 4096], P('island', 'fsdp'), may hold values from -3 to 3
- basis_init: float32 [4096, 64], replicated, may hold values from -6 to 6
- params: float32 [14336, 4096], P(('fsdp', 'island')), may hold values from -6 to 6
- momentum: float32 [14336, 4096], P(('fsdp', 'island')), may hold values from -6 to 6
Outputs:
- new_error: bfloat16 [4, 14336, 4096], P('island', 'fsdp')
- new_params: float32 [14336, 4096], P(('fsdp', 'island'))
- new_momentum: float32 [14336, 4096], P(('fsdp', 'island'))
All inputs are finite; a program needn't handle non-finite values.
Results may differ from a plain program's by a relative error of at most 0.0051.
Values sent between devices are 32-bit elements; how exact they have to be, the bound alone decides.
No kernel may reach another device: no remote copies, remote signals or barrier semaphores. Data moves between devices by JAX's collectives and lax.ppermute only.
A program may use at most 64 MiB of HBM per device.

v0:
```python
import jax
import jax.numpy as jnp
from jax import lax
from jax.experimental import pallas as pl
from jax.experimental.pallas import tpu as pltpu
from jax.sharding import Mesh, PartitionSpec as P

ITERS = 4
STEP = 4
momentum_coef = 0.9
outer_rate = 0.7
ROW = ("y", "z")


def dot(a, b, ca, cb):
    return lax.dot_general(
        a,
        b,
        (((ca,), (cb,)), ((), ())),
        precision=lax.Precision.HIGHEST,
        preferred_element_type=jnp.float32,
    )


def ring(n, step):
    return [(i, (i + step) % n) for i in range(n)]


def island_parts(v):
    return [v] + [lax.ppermute(v, "x", ring(4, s)) for s in (1, 2, 3)]


def island_sum(v):
    a, b, c, d = island_parts(v)
    return (a + c) + (b + d)


def factor_kernel(gram_ref, out_ref, work):
    n = gram_ref.shape[0]
    lane = lax.broadcasted_iota(jnp.int32, (n, 2 * n), 1)
    row_of = lax.broadcasted_iota(jnp.int32, (n, 2 * n), 0)
    work[:, :n] = gram_ref[...]
    work[:, n:] = jnp.where(lane[:, :n] == row_of[:, :n], 1.0, 0.0)
    below, across = row_of[:, :1], lane[:1]

    def pick(v, lanes, at):
        return jnp.sum(jnp.where(lanes == at, v, 0.0), axis=1, keepdims=True)

    def eliminate(step, carry):
        first = STEP * step
        state = work[...]
        rows = [work[pl.ds(first + i, 1), :] for i in range(STEP)]
        cols = [pick(state, lane, first + i) for i in range(STEP)]
        block = {
            (i, k): pick(rows[i], across, first + k) for i in range(STEP) for k in range(i, STEP)
        }
        for i in range(STEP):
            scale = 1.0 / block[i, i]
            for k in range(i + 1, STEP):
                ratio = block[i, k] * scale
                rows[k] = rows[k] - ratio * rows[i]
                cols[k] = cols[k] - ratio * cols[i]
                for m in range(k, STEP):
                    block[k, m] = block[k, m] - ratio * block[i, m]
            weight = jnp.where(below > first + i, cols[i] * scale, 0.0)
            state = state - weight * rows[i]
        work[...] = state
        return carry

    lax.fori_loop(0, n // STEP, eliminate, 0)
    state = work[...]
    pivots = jnp.sum(jnp.where(lane == row_of, state, 0.0), axis=1, keepdims=True)
    out_ref[...] = state[:, n:] * lax.rsqrt(pivots)


def inverse_factor(gram):
    n = gram.shape[0]
    return pl.pallas_call(
        factor_kernel,
        out_shape=jax.ShapeDtypeStruct((n, n), jnp.float32),
        scratch_shapes=[pltpu.VMEM((n, 2 * n), jnp.float32)],
        cost_estimate=pl.CostEstimate(
            flops=16 * 1024 * 1024, bytes_accessed=16 * 1024 * 1024, transcendentals=0
        ),
        name="factor",
    )(gram)


def tiles(v):
    r, w = v.shape
    return v.reshape(r // 8, 8, w // 128, 128).transpose(0, 2, 1, 3).reshape(-1, 8, 128)


def untile(v, r, w):
    return v.reshape(r // 8, w // 128, 8, 128).transpose(0, 2, 1, 3).reshape(r, w)


def swap(v):
    return lax.ppermute(v, "c", ring(2, 1))


def row_sum(near, far, inverse=None):
    near = near + swap(far)
    parts = tiles(near)
    own = jnp.sum(lax.all_to_all(parts, ROW, 0, 0), axis=0)
    full = lax.all_to_all(jnp.broadcast_to(own, parts.shape), ROW, 0, 0)
    near = untile(full, *near.shape)
    if inverse is not None:
        near = dot(inverse, near, 1, 0)
    return jnp.concatenate([near, swap(near)], axis=1)


def combine_kernel(island_ref, core_ref, grad_ref, buffer_ref, top_ref, bottom_ref):
    both = grad_ref[...].astype(jnp.float32) + buffer_ref[...].astype(jnp.float32)
    combined = both.astype(jnp.bfloat16).astype(jnp.float32)
    split = top_ref.shape[0]
    top_ref[...] = combined[:split]
    bottom_ref[...] = combined[split:]


def combine_block(island, core, grad, buffer, width):
    rows = grad.shape[0]
    half = width // 2
    spec = pl.BlockSpec((rows, half), lambda h, i, c: (0, 2 * i[0] + lax.rem(c[0] + h, 2)))
    piece = pl.BlockSpec((rows // 2, half), lambda h, i, c: (0, h))
    shape = jax.ShapeDtypeStruct((rows // 2, width), jnp.float32)
    return pl.pallas_call(
        combine_kernel,
        out_shape=(shape, shape),
        grid_spec=pltpu.PrefetchScalarGridSpec(
            num_scalar_prefetch=2,
            grid=(2,),
            in_specs=[spec, spec],
            out_specs=(piece, piece),
        ),
        cost_estimate=pl.CostEstimate(
            flops=rows * width, bytes_accessed=rows * width * 8, transcendentals=0
        ),
        name="combine",
    )(island.reshape(1), core.reshape(1), grad, buffer)


def low_high(v):
    high = v.astype(jnp.bfloat16)
    return high, (v - high.astype(jnp.float32)).astype(jnp.bfloat16)


def finish_kernel(me_ref, core_ref, left_ref, *refs):
    right_refs, rest = refs[:4], refs[4:]
    grad_ref, buffer_ref, params_ref, momentum_ref = rest[:4]
    error_out, params_out, momentum_out, left4, mine4, right = rest[4:]
    step = pl.program_id(0)
    half = right.shape[1] // 2
    quarter = params_ref.shape[0]

    @pl.when(step == 0)
    def _():
        high, low = low_high(left_ref[...])
        left4[...] = jnp.concatenate([high, high, low, low], axis=1)
        own = pl.ds(pl.multiple_of(me_ref[0] * quarter, 8), quarter)
        high, low = low_high(left_ref[own, :])
        mine4[...] = jnp.concatenate([high, high, low, low], axis=1)

    near = pl.multiple_of(core_ref[0] * half, half)
    far = pl.multiple_of((1 - core_ref[0]) * half, half)
    for s in range(4):

        @pl.when(step == s)
        def _(s=s):
            right[:, :half] = right_refs[s][:, pl.ds(near, half)]
            right[:, half:] = right_refs[s][:, pl.ds(far, half)]

    high, low = low_high(right[...])
    right4 = jnp.concatenate([high, low, high, low], axis=0)
    approx = jnp.dot(left4[...], right4, preferred_element_type=jnp.float32)
    both = grad_ref[...].astype(jnp.float32) + buffer_ref[...].astype(jnp.float32)
    combined = both.astype(jnp.bfloat16).astype(jnp.float32)
    error_out[...] = (combined - approx).astype(jnp.bfloat16)
    mine = jnp.dot(mine4[...], right4, preferred_element_type=jnp.float32)
    moved = momentum_coef * momentum_ref[...] + mine
    momentum_out[...] = moved
    params_out[...] = params_ref[...] - outer_rate * (mine + momentum_coef * moved)


def finish(me, core, left, rights, grad, buffer, params, momentum):
    rows, _ = grad.shape
    quarter = params.shape[0]
    rank, width = rights[0].shape
    islands = len(rights)

    def block(n):
        return pl.BlockSpec((n, width), lambda s, m, c: (0, lax.rem(m[0] + islands - s, islands)))

    def whole(a):
        return pl.BlockSpec(a.shape, lambda s, m, c: (0, 0))

    state = jax.ShapeDtypeStruct(params.shape, jnp.float32)
    return pl.pallas_call(
        finish_kernel,
        out_shape=(jax.ShapeDtypeStruct(grad.shape, jnp.bfloat16), state, state),
        grid_spec=pltpu.PrefetchScalarGridSpec(
            num_scalar_prefetch=2,
            grid=(islands,),
            in_specs=[whole(left)]
            + [whole(r) for r in rights]
            + [block(rows), block(rows), block(quarter), block(quarter)],
            out_specs=(block(rows), block(quarter), block(quarter)),
            scratch_shapes=[
                pltpu.VMEM((rows, 4 * rank), jnp.bfloat16),
                pltpu.VMEM((quarter, 4 * rank), jnp.bfloat16),
                pltpu.VMEM((rank, width), jnp.float32),
            ],
        ),
        name="finish",
    )(me.reshape(1), core.reshape(1), left, *rights, grad, buffer, params, momentum)


def start_sketch(basis, combined):
    rank = basis.shape[1]
    rest, pieces = basis, []
    for _ in range(3):
        piece = lax.reduce_precision(rest, exponent_bits=8, mantissa_bits=7)
        pieces.append(piece.astype(jnp.bfloat16))
        rest = rest - piece
    wide = lax.dot_general(
        jnp.concatenate(pieces, axis=1),
        combined.astype(jnp.bfloat16),
        (((0,), (1,)), ((), ())),
        preferred_element_type=jnp.float32,
    )
    return wide[2 * rank :] + wide[rank : 2 * rank] + wide[:rank]


def hop(v, pairs):
    return lax.ppermute(v, "x", pairs)


def shards(pseudo_grad, error_buffer, basis_init, params, momentum):
    grad, buffer = pseudo_grad[0], error_buffer[0]
    rows, cols = grad.shape
    islands = lax.axis_size("x")
    me = lax.axis_index("x")
    core = lax.axis_index("c")
    width = cols // islands
    half = width // 2

    blocks = {
        s: combine_block(lax.rem(me + s, islands), core, grad, buffer, width)
        for s in (2, 1, 3, 0)
    }
    up, down = ring(islands, 1), ring(islands, -1)
    relay_up = hop(blocks[2][0], up)
    relay_down = hop(blocks[2][1], down)
    from_below = hop(blocks[1][1], up)
    from_above = hop(blocks[3][0], down)
    top_below = hop(blocks[1][0] + relay_up, up)
    bottom_above = hop(blocks[3][1] + relay_down, down)
    total = jnp.concatenate(
        [
            (blocks[0][0] + from_above) + top_below,
            (blocks[0][1] + from_below) + bottom_above,
        ],
        axis=0,
    )

    both = grad.astype(jnp.float32) + buffer.astype(jnp.float32)
    combined = lax.reduce_precision(both, exponent_bits=8, mantissa_bits=7)
    part = start_sketch(basis_init, combined)
    image = island_sum(part)
    basis = lax.dynamic_slice_in_dim(basis_init, me * width, width, 0)
    basis = jnp.where(core == 0, basis, jnp.roll(basis, half, axis=0)).T
    near, far = total[:, :half], total[:, half:]
    right = row_sum(dot(image, near, 1, 0), dot(image, far, 1, 0))
    for _ in range(1, ITERS):
        part = jnp.concatenate([dot(right, total, 1, 1), dot(basis, right, 1, 1)], axis=1)
        summed = island_sum(part)
        image, gram = summed[:, :rows], summed[:, rows:]
        raw = dot(image, near, 1, 0), dot(image, far, 1, 0)
        inverse = inverse_factor(gram)
        basis = dot(inverse, right, 1, 0)
        right = row_sum(*raw, inverse)
    gram = island_sum(dot(basis, right, 1, 1))
    rights = island_parts(right)
    last = inverse_factor(gram)
    sketch = dot(last, dot(inverse, image, 1, 0), 1, 0)
    left = dot(sketch, last, 0, 0) * (1.0 / islands)
    new_error, new_params, new_momentum = finish(
        me, core, left, rights, grad, buffer, params, momentum
    )
    return (new_error[None], new_params, new_momentum)


def solution(mesh):
    fine = Mesh(mesh.devices.reshape(4, 4, 8, 2), ("x", "y", "z", "c"))
    block = P("x", ROW + ("c",), None)
    state = P(ROW + ("c", "x"), None)
    return jax.shard_map(
        shards,
        mesh=fine,
        in_specs=(block, block, P(), state, state),
        out_specs=(block, state, state),
        check_vma=False,
    )
```

profile of v0, /device:TPU:2, one launch (start us, length us, event | category | flops | bytes accessed | tf_op | source)
XLA Modules:
  0.0 246.9 jit_solution(17139844086695550614)
XLA Ops:
  0.6 2.2 combine.7
  5.1 2.2 combine.6
  9.9 2.2 combine.5
  12.1 2.8 %fusion = f32[192,224]{1,0:T(8,128)S(1)} fusion(bf16[4096,64]{0,1:T(8,128)(2,1)} %get-tuple-element.26, bf16[4096,64]{0,1:T(8,128)(2,1)} %get-tuple-element.27, bf16[4096,64]{0,1:T(8,128)(2,1)} %get-tuple-element.25, bf16[1,224,4096]{2,1,0:T(8,128)(2,1)S(1)} %copy-done, bf16[1,224,4096]{2,1,0:T(8,128)(2,1)} %param.5), kind=kOutput, calls=%fused_computation.1 | convolution fusion | flops 361627648 | bytes 5414912 | tf_op jit(solution)/shard_map/dot_general | solution.py:225
  24.7 2.1 combine.4
  29.3 5.0 %collective-permute-done.2 = f32[64,224]{1,0:T(8,128)} collective-permute-done((f32[64,224]{1,0:T(8,128)}, f32[64,224]{1,0:T(8,128)}, u32[]{:S(2)}, u32[]{:S(2)}) %collective-permute-start.2) | collective-permute-done | bytes 57376 | tf_op jit(solution)/shard_map/ppermute | solution.py:30
  36.6 5.8 %collective-permute-done.3 = f32[112,1024]{1,0:T(8,128)S(1)} collective-permute-done((f32[112,1024]{1,0:T(8,128)}, f32[112,1024]{1,0:T(8,128)S(1)}, u32[]{:S(2)}, u32[]{:S(2)}) %collective-permute-start.3) | collective-permute-done | bytes 458784 | tf_op jit(solution)/shard_map/ppermute | solution.py:235
  45.2 21.5 %all_to_all.40 = f32[32,8,128]{2,1,0:T(8,128)S(1)} all-to-all(f32[32,8,128]{2,1,0:T(8,128)S(1)} %bitcast.101), channel_id=1, replica_groups=mesh['x'=4,'y'=4,'z'=8,'c'=2] {'y','z'}, dimensions={0} | all-to-all | bytes 262144 | tf_op jit(solution)/shard_map/all_to_all | solution.py:105
  66.8 13.9 %all_to_all.41 = f32[32,8,128]{2,1,0:T(8,128)S(1)} all-to-all(f32[32,8,128]{2,1,0:T(8,128)S(1)} %broadcast_in_dim.15), channel_id=1, replica_groups=mesh['x'=4,'y'=4,'z'=8,'c'=2] {'y','z'}, dimensions={0} | all-to-all | bytes 262144 | tf_op jit(solution)/shard_map/all_to_all | solution.py:106
  83.5 2.7 %collective-permute-start.12 = (f32[64,288]{1,0:T(8,128)S(1)}, f32[64,288]{1,0:T(8,128)S(1)}, u32[]{:S(2)}, u32[]{:S(2)}) collective-permute-start(f32[64,288]{1,0:T(8,128)S(1)} %pad_maximum_fusion.17), channel_id=1, source_target_pairs={{0,64},{64,128},{128,192},{192,0},{1,65},{65,129},{129,193},{193,1... | collective-permute-start | bytes 221192 | tf_op jit(solution)/shard_map/ppermute | solution.py:30
  87.4 2.8 %collective-permute-start.11 = (f32[64,288]{1,0:T(8,128)S(1)}, f32[64,288]{1,0:T(8,128)S(1)}, u32[]{:S(2)}, u32[]{:S(2)}) collective-permute-start(f32[64,288]{1,0:T(8,128)S(1)} %pad_maximum_fusion.17), channel_id=1, source_target_pairs={{0,128},{64,192},{128,0},{192,64},{1,129},{65,193},{129,1},{193,65... | collective-permute-start | bytes 221192 | tf_op jit(solution)/shard_map/ppermute | solution.py:30
  91.5 3.3 %collective-permute-done.11 = f32[64,288]{1,0:T(8,128)S(1)} collective-permute-done((f32[64,288]{1,0:T(8,128)S(1)}, f32[64,288]{1,0:T(8,128)S(1)}, u32[]{:S(2)}, u32[]{:S(2)}) %collective-permute-start.11) | collective-permute-done | bytes 73760 | tf_op jit(solution)/shard_map/ppermute | solution.py:30
  97.1 14.1 %all_to_all.42 = f32[32,8,128]{2,1,0:T(8,128)S(1)} all-to-all(f32[32,8,128]{2,1,0:T(8,128)S(1)} %bitcast.103), channel_id=1, replica_groups=mesh['x'=4,'y'=4,'z'=8,'c'=2] {'y','z'}, dimensions={0} | all-to-all | bytes 262144 | tf_op jit(solution)/shard_map/all_to_all | solution.py:105
  111.9 3.9 %all-to-all-start.3 = ((f32[32,8,128]{2,1,0:T(8,128)}), f32[32,8,128]{2,1,0:T(8,128)S(1)}, u32[]{:S(2)}, u32[]{:S(2)}) async-start(f32[32,8,128]{2,1,0:T(8,128)} %broadcast_in_dim.16), calls=%async_computation.3 | async-start | bytes 262144 | tf_op jit(solution)/shard_map/all_to_all | solution.py:106
  116.5 3.8 %factor.4 = f32[64,64]{1,0:T(8,128)} custom-call(f32[64,64]{1,0:T(8,128)} %slice.61.gram_ref), custom_call_target="tpu_custom_call" | custom-call | flops 16777216 | bytes 16777216 | tf_op jit(solution)/shard_map/factor/pallas_call | solution.py:78
  120.3 6.0 %all-to-all-done.3 = f32[32,8,128]{2,1,0:T(8,128)S(1)} async-done(((f32[32,8,128]{2,1,0:T(8,128)}), f32[32,8,128]{2,1,0:T(8,128)S(1)}, u32[]{:S(2)}, u32[]{:S(2)}) %all-to-all-start.3) | async-done | bytes 131104 | tf_op jit(solution)/shard_map/all_to_all | solution.py:106
  132.2 2.4 collective-permute-start.16
  136.2 3.3 %collective-permute-done.16 = f32[64,288]{1,0:T(8,128)S(1)} collective-permute-done((f32[64,288]{1,0:T(8,128)S(1)}, f32[64,288]{1,0:T(8,128)S(1)}, u32[]{:S(2)}, u32[]{:S(2)}) %collective-permute-start.16) | collective-permute-done | bytes 73760 | tf_op jit(solution)/shard_map/ppermute | solution.py:30
  141.8 14.2 %all_to_all.43 = f32[32,8,128]{2,1,0:T(8,128)S(1)} all-to-all(f32[32,8,128]{2,1,0:T(8,128)S(1)} %bitcast.104), channel_id=1, replica_groups=mesh['x'=4,'y'=4,'z'=8,'c'=2] {'y','z'}, dimensions={0} | all-to-all | bytes 262144 | tf_op jit(solution)/shard_map/all_to_all | solution.py:105
  156.7 3.9 %all-to-all-start.5 = ((f32[32,8,128]{2,1,0:T(8,128)}), f32[32,8,128]{2,1,0:T(8,128)S(1)}, u32[]{:S(2)}, u32[]{:S(2)}) async-start(f32[32,8,128]{2,1,0:T(8,128)} %broadcast_in_dim.17), calls=%async_computation.5 | async-start | bytes 262144 | tf_op jit(solution)/shard_map/all_to_all | solution.py:106
  161.3 3.8 %factor.5 = f32[64,64]{1,0:T(8,128)} custom-call(f32[64,64]{1,0:T(8,128)} %slice.63.gram_ref), custom_call_target="tpu_custom_call" | custom-call | flops 16777216 | bytes 16777216 | tf_op jit(solution)/shard_map/factor/pallas_call | solution.py:78
  165.1 6.0 %all-to-all-done.5 = f32[32,8,128]{2,1,0:T(8,128)S(1)} async-done(((f32[32,8,128]{2,1,0:T(8,128)}), f32[32,8,128]{2,1,0:T(8,128)S(1)}, u32[]{:S(2)}, u32[]{:S(2)}) %all-to-all-start.5) | async-done | bytes 131104 | tf_op jit(solution)/shard_map/all_to_all | solution.py:106
  177.3 2.7 %collective-permute-start.21 = (f32[64,288]{1,0:T(8,128)S(1)}, f32[64,288]{1,0:T(8,128)S(1)}, u32[]{:S(2)}, u32[]{:S(2)}) collective-permute-start(f32[64,288]{1,0:T(8,128)S(1)} %pad_maximum_fusion.19), channel_id=1, source_target_pairs={{0,128},{64,192},{128,0},{192,64},{1,129},{65,193},{129,1},{193,65... | collective-permute-start | bytes 221192 | tf_op jit(solution)/shard_map/ppermute | solution.py:30
  181.5 3.3 %collective-permute-done.21 = f32[64,288]{1,0:T(8,128)S(1)} collective-permute-done((f32[64,288]{1,0:T(8,128)S(1)}, f32[64,288]{1,0:T(8,128)S(1)}, u32[]{:S(2)}, u32[]{:S(2)}) %collective-permute-start.21) | collective-permute-done | bytes 73760 | tf_op jit(solution)/shard_map/ppermute | solution.py:30
  187.1 14.2 %all_to_all.44 = f32[32,8,128]{2,1,0:T(8,128)S(1)} all-to-all(f32[32,8,128]{2,1,0:T(8,128)S(1)} %bitcast.102), channel_id=1, replica_groups=mesh['x'=4,'y'=4,'z'=8,'c'=2] {'y','z'}, dimensions={0} | all-to-all | bytes 262144 | tf_op jit(solution)/shard_map/all_to_all | solution.py:105
  202.0 3.9 %all-to-all-start.7 = ((f32[32,8,128]{2,1,0:T(8,128)}), f32[32,8,128]{2,1,0:T(8,128)S(1)}, u32[]{:S(2)}, u32[]{:S(2)}) async-start(f32[32,8,128]{2,1,0:T(8,128)} %broadcast_in_dim.18), calls=%async_computation.7 | async-start | bytes 262144 | tf_op jit(solution)/shard_map/all_to_all | solution.py:106
  206.6 3.8 %factor.6 = f32[64,64]{1,0:T(8,128)} custom-call(f32[64,64]{1,0:T(8,128)} %slice.65.gram_ref), custom_call_target="tpu_custom_call" | custom-call | flops 16777216 | bytes 16777216 | tf_op jit(solution)/shard_map/factor/pallas_call | solution.py:78
  211.5 4.9 %all-to-all-done.7 = f32[32,8,128]{2,1,0:T(8,128)S(1)} async-done(((f32[32,8,128]{2,1,0:T(8,128)}), f32[32,8,128]{2,1,0:T(8,128)S(1)}, u32[]{:S(2)}, u32[]{:S(2)}) %all-to-all-start.7) | async-done | bytes 131104 | tf_op jit(solution)/shard_map/all_to_all | solution.py:106
  221.3 3.7 %collective-permute-start.26 = (f32[64,64]{1,0:T(8,128)S(1)}, f32[64,64]{1,0:T(8,128)S(1)}, u32[]{:S(2)}, u32[]{:S(2)}) collective-permute-start(f32[64,64]{1,0:T(8,128)S(1)} %fusion.47), channel_id=1, source_target_pairs={{0,128},{64,192},{128,0},{192,64},{1,129},{65,193},{129,1},{193,65... | collective-permute-start | bytes 49160 | tf_op jit(solution)/shard_map/ppermute | solution.py:30
  228.4 3.8 %factor.7 = f32[64,64]{1,0:T(8,128)} custom-call(f32[64,64]{1,0:T(8,128)} %add_add_fusion.6.gram_ref), custom_call_target="tpu_custom_call" | custom-call | flops 16777216 | bytes 16777216 | tf_op jit(solution)/shard_map/factor/pallas_call | solution.py:78
  234.9 3.5 %collective-permute-done.31.refs_3_ = f32[64,1024]{1,0:T(8,128)S(1)} collective-permute-done((f32[64,1024]{1,0:T(8,128)S(1)}, f32[64,1024]{1,0:T(8,128)S(1)}, u32[]{:S(2)}, u32[]{:S(2)}) %collective-permute-start.31) | collective-permute-done | bytes 262176 | tf_op jit(solution)/shard_map/ppermute | solution.py:30
  240.8 6.0 %finish.1 = (bf16[224,4096]{1,0:T(8,128)(2,1)}, f32[56,4096]{1,0:T(8,128)}, f32[56,4096]{1,0:T(8,128)}) custom-call(s32[1]{0:T(128)} %bitcast.me_ref, s32[1]{0:T(128)} %bitcast.1.core_ref, f32[224,64]{1,0:T(8,128)} %convolution_multiply_fusion.left_ref, f32[64,1024]{1,0:T(8,128)} %copy-done.2, f32[64,1024]{1,0:T(8,128)} %copy-done.9, f32[64,1024]{1,0:T(8,128)} %copy-done.8, ...), custom_call_target="tpu_custom_call" | custom-call | tf_op jit(solution)/shard_map/finish/pallas_call | solution.py:198
  (125 shorter events, 68.3 us)
Async XLA Ops:
  2.8 19.8 %collective-permute-start.4 = (f32[112,1024]{1,0:T(8,128)}, f32[112,1024]{1,0:T(8,128)}, u32[]{:S(2)}, u32[]{:S(2)}) collective-permute-start(f32[112,1024]{1,0:T(8,128)} %get-tuple-element.17), channel_id=1, source_target_pairs={{0,64},{64,128},{128,192},{192,0},{1,65},{65,129},{129,193},{193,1... | collective-permute-start | bytes 1376264 | tf_op jit(solution)/shard_map/ppermute | solution.py:235
  4.3 12.3 %collective-permute-start.7 = (f32[112,1024]{1,0:T(8,128)}, f32[112,1024]{1,0:T(8,128)}, u32[]{:S(2)}, u32[]{:S(2)}) collective-permute-start(f32[112,1024]{1,0:T(8,128)} %get-tuple-element.21), channel_id=1, source_target_pairs={{0,192},{64,0},{128,64},{192,128},{1,193},{65,1},{129,65},{193,129... | collective-permute-start | bytes 1376264 | tf_op jit(solution)/shard_map/ppermute | solution.py:235
  7.3 29.2 %collective-permute-start.6 = (f32[112,1024]{1,0:T(8,128)}, f32[112,1024]{1,0:T(8,128)S(1)}, u32[]{:S(2)}, u32[]{:S(2)}) collective-permute-start(f32[112,1024]{1,0:T(8,128)} %get-tuple-element.19), channel_id=1, source_target_pairs={{0,64},{64,128},{128,192},{192,0},{1,65},{65,129},{129,193},{193,1... | collective-permute-start | bytes 1376264 | tf_op jit(solution)/shard_map/ppermute | solution.py:235
  18.4 18.1 %collective-permute-start.8 = (f32[112,1024]{1,0:T(8,128)}, f32[112,1024]{1,0:T(8,128)S(1)}, u32[]{:S(2)}, u32[]{:S(2)}) collective-permute-start(f32[112,1024]{1,0:T(8,128)} %add.109), channel_id=1, source_target_pairs={{0,192},{64,0},{128,64},{192,128},{1,193},{65,1},{129,65},{193,129... | collective-permute-start | bytes 1376264 | tf_op jit(solution)/shard_map/ppermute | solution.py:235
  19.6 8.4 %collective-permute-start.1 = (f32[64,224]{1,0:T(8,128)}, f32[64,224]{1,0:T(8,128)}, u32[]{:S(2)}, u32[]{:S(2)}) collective-permute-start(f32[64,224]{1,0:T(8,128)} %slice_add_fusion), channel_id=1, source_target_pairs={{0,64},{64,128},{128,192},{192,0},{1,65},{65,129},{129,193},{193,1... | collective-permute-start | bytes 172040 | tf_op jit(solution)/shard_map/ppermute | solution.py:30
  21.1 13.2 %collective-permute-start.2 = (f32[64,224]{1,0:T(8,128)}, f32[64,224]{1,0:T(8,128)}, u32[]{:S(2)}, u32[]{:S(2)}) collective-permute-start(f32[64,224]{1,0:T(8,128)} %slice_add_fusion), channel_id=1, source_target_pairs={{0,192},{64,0},{128,64},{192,128},{1,193},{65,1},{129,65},{193,129... | collective-permute-start | bytes 172040 | tf_op jit(solution)/shard_map/ppermute | solution.py:30
  22.6 13.0 %collective-permute-start = (f32[64,224]{1,0:T(8,128)}, f32[64,224]{1,0:T(8,128)}, u32[]{:S(2)}, u32[]{:S(2)}) collective-permute-start(f32[64,224]{1,0:T(8,128)} %slice_add_fusion), channel_id=1, source_target_pairs={{0,128},{64,192},{128,0},{192,64},{1,129},{65,193},{129,1},{193,65... | collective-permute-start | bytes 172040 | tf_op jit(solution)/shard_map/ppermute | solution.py:30
  28.0 14.4 %collective-permute-start.3 = (f32[112,1024]{1,0:T(8,128)}, f32[112,1024]{1,0:T(8,128)S(1)}, u32[]{:S(2)}, u32[]{:S(2)}) collective-permute-start(f32[112,1024]{1,0:T(8,128)} %get-tuple-element.15), channel_id=1, source_target_pairs={{0,192},{64,0},{128,64},{192,128},{1,193},{65,1},{129,65},{193,129... | collective-permute-start | bytes 1376264 | tf_op jit(solution)/shard_map/ppermute | solution.py:235
  34.3 8.5 %collective-permute-start.5 = (f32[112,1024]{1,0:T(8,128)S(1)}, f32[112,1024]{1,0:T(8,128)S(1)}, u32[]{:S(2)}, u32[]{:S(2)}) collective-permute-start(f32[112,1024]{1,0:T(8,128)S(1)} %add.106), channel_id=1, source_target_pairs={{0,64},{64,128},{128,192},{192,0},{1,65},{65,129},{129,193},{193,1... | collective-permute-start | bytes 1376264 | tf_op jit(solution)/shard_map/ppermute | solution.py:235
  43.3 1.4 collective-permute-start.9
  83.5 6.9 %collective-permute-start.12 = (f32[64,288]{1,0:T(8,128)S(1)}, f32[64,288]{1,0:T(8,128)S(1)}, u32[]{:S(2)}, u32[]{:S(2)}) collective-permute-start(f32[64,288]{1,0:T(8,128)S(1)} %pad_maximum_fusion.17), channel_id=1, source_target_pairs={{0,64},{64,128},{128,192},{192,0},{1,65},{65,129},{129,193},{193,1... | collective-permute-start | bytes 221192 | tf_op jit(solution)/shard_map/ppermute | solution.py:30
  86.2 5.3 %collective-permute-start.13 = (f32[64,288]{1,0:T(8,128)S(1)}, f32[64,288]{1,0:T(8,128)S(1)}, u32[]{:S(2)}, u32[]{:S(2)}) collective-permute-start(f32[64,288]{1,0:T(8,128)S(1)} %pad_maximum_fusion.17), channel_id=1, source_target_pairs={{0,192},{64,0},{128,64},{192,128},{1,193},{65,1},{129,65},{193,129... | collective-permute-start | bytes 221192 | tf_op jit(solution)/shard_map/ppermute | solution.py:30
  87.4 7.4 %collective-permute-start.11 = (f32[64,288]{1,0:T(8,128)S(1)}, f32[64,288]{1,0:T(8,128)S(1)}, u32[]{:S(2)}, u32[]{:S(2)}) collective-permute-start(f32[64,288]{1,0:T(8,128)S(1)} %pad_maximum_fusion.17), channel_id=1, source_target_pairs={{0,128},{64,192},{128,0},{192,64},{1,129},{65,193},{129,1},{193,65... | collective-permute-start | bytes 221192 | tf_op jit(solution)/shard_map/ppermute | solution.py:30
  95.3 1.4 collective-permute-start.14
  111.9 14.3 %all-to-all-start.3 = ((f32[32,8,128]{2,1,0:T(8,128)}), f32[32,8,128]{2,1,0:T(8,128)S(1)}, u32[]{:S(2)}, u32[]{:S(2)}) async-start(f32[32,8,128]{2,1,0:T(8,128)} %broadcast_in_dim.16), calls=%async_computation.3 | async-start | bytes 262144 | tf_op jit(solution)/shard_map/all_to_all | solution.py:106
  127.3 1.4 collective-permute-start.15
  130.1 5.2 %collective-permute-start.17 = (f32[64,288]{1,0:T(8,128)S(1)}, f32[64,288]{1,0:T(8,128)S(1)}, u32[]{:S(2)}, u32[]{:S(2)}) collective-permute-start(f32[64,288]{1,0:T(8,128)S(1)} %pad_maximum_fusion.18), channel_id=1, source_target_pairs={{0,64},{64,128},{128,192},{192,0},{1,65},{65,129},{129,193},{193,1... | collective-permute-start | bytes 221192 | tf_op jit(solution)/shard_map/ppermute | solution.py:30
  130.2 5.9 %collective-permute-start.18 = (f32[64,288]{1,0:T(8,128)S(1)}, f32[64,288]{1,0:T(8,128)S(1)}, u32[]{:S(2)}, u32[]{:S(2)}) collective-permute-start(f32[64,288]{1,0:T(8,128)S(1)} %pad_maximum_fusion.18), channel_id=1, source_target_pairs={{0,192},{64,0},{128,64},{192,128},{1,193},{65,1},{129,65},{193,129... | collective-permute-start | bytes 221192 | tf_op jit(solution)/shard_map/ppermute | solution.py:30
  132.2 7.2 %collective-permute-start.16 = (f32[64,288]{1,0:T(8,128)S(1)}, f32[64,288]{1,0:T(8,128)S(1)}, u32[]{:S(2)}, u32[]{:S(2)}) collective-permute-start(f32[64,288]{1,0:T(8,128)S(1)} %pad_maximum_fusion.18), channel_id=1, source_target_pairs={{0,128},{64,192},{128,0},{192,64},{1,129},{65,193},{129,1},{193,65... | collective-permute-start | bytes 221192 | tf_op jit(solution)/shard_map/ppermute | solution.py:30
  156.7 14.3 %all-to-all-start.5 = ((f32[32,8,128]{2,1,0:T(8,128)}), f32[32,8,128]{2,1,0:T(8,128)S(1)}, u32[]{:S(2)}, u32[]{:S(2)}) async-start(f32[32,8,128]{2,1,0:T(8,128)} %broadcast_in_dim.17), calls=%async_computation.5 | async-start | bytes 262144 | tf_op jit(solution)/shard_map/all_to_all | solution.py:106
  172.1 1.7 collective-permute-start.20
  175.2 5.3 %collective-permute-start.22 = (f32[64,288]{1,0:T(8,128)S(1)}, f32[64,288]{1,0:T(8,128)S(1)}, u32[]{:S(2)}, u32[]{:S(2)}) collective-permute-start(f32[64,288]{1,0:T(8,128)S(1)} %pad_maximum_fusion.19), channel_id=1, source_target_pairs={{0,64},{64,128},{128,192},{192,0},{1,65},{65,129},{129,193},{193,1... | collective-permute-start | bytes 221192 | tf_op jit(solution)/shard_map/ppermute | solution.py:30
  175.3 6.2 %collective-permute-start.23 = (f32[64,288]{1,0:T(8,128)S(1)}, f32[64,288]{1,0:T(8,128)S(1)}, u32[]{:S(2)}, u32[]{:S(2)}) collective-permute-start(f32[64,288]{1,0:T(8,128)S(1)} %pad_maximum_fusion.19), channel_id=1, source_target_pairs={{0,192},{64,0},{128,64},{192,128},{1,193},{65,1},{129,65},{193,129... | collective-permute-start | bytes 221192 | tf_op jit(solution)/shard_map/ppermute | solution.py:30
  177.3 7.5 %collective-permute-start.21 = (f32[64,288]{1,0:T(8,128)S(1)}, f32[64,288]{1,0:T(8,128)S(1)}, u32[]{:S(2)}, u32[]{:S(2)}) collective-permute-start(f32[64,288]{1,0:T(8,128)S(1)} %pad_maximum_fusion.19), channel_id=1, source_target_pairs={{0,128},{64,192},{128,0},{192,64},{1,129},{65,193},{129,1},{193,65... | collective-permute-start | bytes 221192 | tf_op jit(solution)/shard_map/ppermute | solution.py:30
  202.0 14.3 %all-to-all-start.7 = ((f32[32,8,128]{2,1,0:T(8,128)}), f32[32,8,128]{2,1,0:T(8,128)S(1)}, u32[]{:S(2)}, u32[]{:S(2)}) async-start(f32[32,8,128]{2,1,0:T(8,128)} %broadcast_in_dim.18), calls=%async_computation.7 | async-start | bytes 262144 | tf_op jit(solution)/shard_map/all_to_all | solution.py:106
  217.4 1.4 collective-permute-start.25
  219.2 6.9 %collective-permute-start.28 = (f32[64,64]{1,0:T(8,128)S(1)}, f32[64,64]{1,0:T(8,128)S(1)}, u32[]{:S(2)}, u32[]{:S(2)}) collective-permute-start(f32[64,64]{1,0:T(8,128)S(1)} %fusion.47), channel_id=1, source_target_pairs={{0,192},{64,0},{128,64},{192,128},{1,193},{65,1},{129,65},{193,129... | collective-permute-start | bytes 49160 | tf_op jit(solution)/shard_map/ppermute | solution.py:30
  221.0 6.7 %collective-permute-start.27 = (f32[64,64]{1,0:T(8,128)S(1)}, f32[64,64]{1,0:T(8,128)S(1)}, u32[]{:S(2)}, u32[]{:S(2)}) collective-permute-start(f32[64,64]{1,0:T(8,128)S(1)} %fusion.47), channel_id=1, source_target_pairs={{0,64},{64,128},{128,192},{192,0},{1,65},{65,129},{129,193},{193,1... | collective-permute-start | bytes 49160 | tf_op jit(solution)/shard_map/ppermute | solution.py:30
  221.3 6.5 %collective-permute-start.26 = (f32[64,64]{1,0:T(8,128)S(1)}, f32[64,64]{1,0:T(8,128)S(1)}, u32[]{:S(2)}, u32[]{:S(2)}) collective-permute-start(f32[64,64]{1,0:T(8,128)S(1)} %fusion.47), channel_id=1, source_target_pairs={{0,128},{64,192},{128,0},{192,64},{1,129},{65,193},{129,1},{193,65... | collective-permute-start | bytes 49160 | tf_op jit(solution)/shard_map/ppermute | solution.py:30
  225.1 13.3 %collective-permute-start.31 = (f32[64,1024]{1,0:T(8,128)S(1)}, f32[64,1024]{1,0:T(8,128)S(1)}, u32[]{:S(2)}, u32[]{:S(2)}) collective-permute-start(f32[64,1024]{1,0:T(8,128)S(1)} %pad_maximum_fusion.7.refs_0_), channel_id=1, source_target_pairs={{0,192},{64,0},{128,64},{192,128},{1,193},{65,1},{129,65},{193,129... | collective-permute-start | bytes 786440 | tf_op jit(solution)/shard_map/ppermute | solution.py:30
  225.2 13.2 %collective-permute-start.30 = (f32[64,1024]{1,0:T(8,128)S(1)}, f32[64,1024]{1,0:T(8,128)S(1)}, u32[]{:S(2)}, u32[]{:S(2)}) collective-permute-start(f32[64,1024]{1,0:T(8,128)S(1)} %pad_maximum_fusion.7.refs_0_), channel_id=1, source_target_pairs={{0,128},{64,192},{128,0},{192,64},{1,129},{65,193},{129,1},{193,65... | collective-permute-start | bytes 786440 | tf_op jit(solution)/shard_map/ppermute | solution.py:30
  226.1 14.0 %collective-permute-start.29 = (f32[64,1024]{1,0:T(8,128)S(1)}, f32[64,1024]{1,0:T(8,128)S(1)}, u32[]{:S(2)}, u32[]{:S(2)}) collective-permute-start(f32[64,1024]{1,0:T(8,128)S(1)} %pad_maximum_fusion.7.refs_0_), channel_id=1, source_target_pairs={{0,64},{64,128},{128,192},{192,0},{1,65},{65,129},{129,193},{193,1... | collective-permute-start | bytes 786440 | tf_op jit(solution)/shard_map/ppermute | solution.py:30
  (13 other events, 61.5 us)
where the time goes:
time: 250 us; the launch traced here: 247 us
  blocking collectives  78 us (31%)
  waiting for transfers between devices  57.4 us (23%)
  starting transfers between devices  47.8 us (19%)
  Pallas kernels  29.9 us (12%)
  matrix products  20.4 us (8%)
  other arithmetic  7.43 us (3%)
  local copies, waits for them, and re-layouts  4.85 us (2%)
    all_to_all x4, blocking collectives, row_sum(): own = jnp.sum(lax.all_to_all(parts, ROW, 0, 0), axis=0)  64.1 us
    ppermute x18, starting transfers between devices, island_parts(): return [v] + [lax.ppermute(v, 'x', ring(4, s)) for s in (1, 2, 3)]  29.6 us
    ppermute x18, waiting for transfers between devices, island_parts(): return [v] + [lax.ppermute(v, 'x', ring(4, s)) for s in (1, 2, 3)]  25.3 us
    dot_general x24, matrix products, dot(): lax.dot_general(a, b, (((ca,), (cb,)), ((), ())), precision=lax.Precision...  17.6 us
    all_to_all x3, waiting for transfers between devices, row_sum(): full = lax.all_to_all(jnp.broadcast_to(own, parts.shape), ROW, 0, 0)  16.8 us
    pallas_call x4, Pallas kernels, inverse_factor(): pl.pallas_call(factor_kernel, out_shape=jax.ShapeDtypeStruct((n, n), jnp....  15.2 us
    all_to_all x1, blocking collectives, row_sum(): full = lax.all_to_all(jnp.broadcast_to(own, parts.shape), ROW, 0, 0)  13.9 us
    all_to_all x3, starting transfers between devices, row_sum(): full = lax.all_to_all(jnp.broadcast_to(own, parts.shape), ROW, 0, 0)  11.6 us
  transfers between devices with their start and end apart: 35, of which 27 were waited for; matrix products, arithmetic and copies ran while one was open for 7% of the time, Pallas kernels for 9%

commit v1 on v0

--- a/solution.py
+++ b/solution.py
@@ -35,11 +35,11 @@
     return (a + c) + (b + d)
 
 
-def factor_kernel(gram_ref, out_ref, work):
-    n = gram_ref.shape[0]
+def factor_into(gram, work):
+    n = gram.shape[0]
     lane = lax.broadcasted_iota(jnp.int32, (n, 2 * n), 1)
     row_of = lax.broadcasted_iota(jnp.int32, (n, 2 * n), 0)
-    work[:, :n] = gram_ref[...]
+    work[:, :n] = gram
     work[:, n:] = jnp.where(lane[:, :n] == row_of[:, :n], 1.0, 0.0)
     below, across = row_of[:, :1], lane[:1]
 
@@ -70,7 +70,11 @@
     lax.fori_loop(0, n // STEP, eliminate, 0)
     state = work[...]
     pivots = jnp.sum(jnp.where(lane == row_of, state, 0.0), axis=1, keepdims=True)
-    out_ref[...] = state[:, n:] * lax.rsqrt(pivots)
+    return state[:, n:] * lax.rsqrt(pivots)
+
+
+def factor_kernel(gram_ref, out_ref, work):
+    out_ref[...] = factor_into(gram_ref[...], work)
 
 
 def inverse_factor(gram):
@@ -99,15 +103,12 @@
     return lax.ppermute(v, "c", ring(2, 1))
 
 
-def row_sum(near, far, inverse=None):
+def row_sum(near, far):
     near = near + swap(far)
     parts = tiles(near)
     own = jnp.sum(lax.all_to_all(parts, ROW, 0, 0), axis=0)
     full = lax.all_to_all(jnp.broadcast_to(own, parts.shape), ROW, 0, 0)
-    near = untile(full, *near.shape)
-    if inverse is not None:
-        near = dot(inverse, near, 1, 0)
-    return jnp.concatenate([near, swap(near)], axis=1)
+    return untile(full, *near.shape)
 
 
 def combine_kernel(island_ref, core_ref, grad_ref, buffer_ref, top_ref, bottom_ref):
@@ -145,36 +146,41 @@
     return high, (v - high.astype(jnp.float32)).astype(jnp.bfloat16)
 
 
-def finish_kernel(me_ref, core_ref, left_ref, *refs):
-    right_refs, rest = refs[:4], refs[4:]
-    grad_ref, buffer_ref, params_ref, momentum_ref = rest[:4]
-    error_out, params_out, momentum_out, left4, mine4, right = rest[4:]
+def finish_kernel(me_ref, core_ref, gram_ref, sketch_ref, combined_ref, *refs):
+    near_refs, far_refs, rest = refs[:4], refs[4:8], refs[8:]
+    params_ref, momentum_ref, error_out, params_out, momentum_out = rest[:5]
+    left4, mine4, right, left, work = rest[5:]
     step = pl.program_id(0)
-    half = right.shape[1] // 2
+    width = right.shape[1]
+    half = width // 2
     quarter = params_ref.shape[0]
+    islands = len(near_refs)
 
     @pl.when(step == 0)
     def _():
-        high, low = low_high(left_ref[...])
+        last = factor_into(gram_ref[...], work)
+        left[...] = dot(dot(last, sketch_ref[...], 1, 0), last, 0, 0) * (1.0 / islands)
+        high, low = low_high(left[...])
         left4[...] = jnp.concatenate([high, high, low, low], axis=1)
         own = pl.ds(pl.multiple_of(me_ref[0] * quarter, 8), quarter)
-        high, low = low_high(left_ref[own, :])
+        high, low = low_high(left[own, :])
         mine4[...] = jnp.concatenate([high, high, low, low], axis=1)
 
     near = pl.multiple_of(core_ref[0] * half, half)
     far = pl.multiple_of((1 - core_ref[0]) * half, half)
-    for s in range(4):
+    for s in range(islands):
 
         @pl.when(step == s)
         def _(s=s):
-            right[:, :half] = right_refs[s][:, pl.ds(near, half)]
-            right[:, half:] = right_refs[s][:, pl.ds(far, half)]
+            right[:, pl.ds(near, half)] = near_refs[s][...]
+            right[:, pl.ds(far, half)] = far_refs[s][...]
 
     high, low = low_high(right[...])
     right4 = jnp.concatenate([high, low, high, low], axis=0)
     approx = jnp.dot(left4[...], right4, preferred_element_type=jnp.float32)
-    both = grad_ref[...].astype(jnp.float32) + buffer_ref[...].astype(jnp.float32)
-    combined = both.astype(jnp.bfloat16).astype(jnp.float32)
+    island = lax.rem(me_ref[0] + islands - step, islands)
+    columns = pl.ds(pl.multiple_of(island * width, width), width)
+    combined = combined_ref[:, columns].astype(jnp.float32)
     error_out[...] = (combined - approx).astype(jnp.bfloat16)
     mine = jnp.dot(mine4[...], right4, preferred_element_type=jnp.float32)
     moved = momentum_coef * momentum_ref[...] + mine
@@ -182,37 +188,36 @@
     params_out[...] = params_ref[...] - outer_rate * (mine + momentum_coef * moved)
 
 
-def finish(me, core, left, rights, grad, buffer, params, momentum):
-    rows, _ = grad.shape
+def finish(me, core, gram, sketch, combined, nears, fars, params, momentum):
+    rows, cols = combined.shape
     quarter = params.shape[0]
-    rank, width = rights[0].shape
-    islands = len(rights)
+    rank, half = nears[0].shape
+    islands = len(nears)
+    width = 2 * half
 
     def block(n):
         return pl.BlockSpec((n, width), lambda s, m, c: (0, lax.rem(m[0] + islands - s, islands)))
 
-    def whole(a):
-        return pl.BlockSpec(a.shape, lambda s, m, c: (0, 0))
-
+    whole = pl.BlockSpec(memory_space=pltpu.VMEM)
     state = jax.ShapeDtypeStruct(params.shape, jnp.float32)
     return pl.pallas_call(
         finish_kernel,
-        out_shape=(jax.ShapeDtypeStruct(grad.shape, jnp.bfloat16), state, state),
+        out_shape=(jax.ShapeDtypeStruct((rows, cols), jnp.bfloat16), state, state),
         grid_spec=pltpu.PrefetchScalarGridSpec(
             num_scalar_prefetch=2,
             grid=(islands,),
-            in_specs=[whole(left)]
-            + [whole(r) for r in rights]
-            + [block(rows), block(rows), block(quarter), block(quarter)],
+            in_specs=[whole] * (3 + 2 * islands) + [block(quarter), block(quarter)],
             out_specs=(block(rows), block(quarter), block(quarter)),
             scratch_shapes=[
                 pltpu.VMEM((rows, 4 * rank), jnp.bfloat16),
                 pltpu.VMEM((quarter, 4 * rank), jnp.bfloat16),
                 pltpu.VMEM((rank, width), jnp.float32),
+                pltpu.VMEM((rows, rank), jnp.float32),
+                pltpu.VMEM((rank, 2 * rank), jnp.float32),
             ],
         ),
         name="finish",
-    )(me.reshape(1), core.reshape(1), left, *rights, grad, buffer, params, momentum)
+    )(me.reshape(1), core.reshape(1), gram, sketch, combined, *nears, *fars, params, momentum)
 
 
 def start_sketch(basis, combined):
@@ -224,7 +229,7 @@
         rest = rest - piece
     wide = lax.dot_general(
         jnp.concatenate(pieces, axis=1),
-        combined.astype(jnp.bfloat16),
+        combined,
         (((0,), (1,)), ((), ())),
         preferred_element_type=jnp.float32,
     )
@@ -238,6 +243,7 @@
 def shards(pseudo_grad, error_buffer, basis_init, params, momentum):
     grad, buffer = pseudo_grad[0], error_buffer[0]
     rows, cols = grad.shape
+    rank = basis_init.shape[1]
     islands = lax.axis_size("x")
     me = lax.axis_index("x")
     core = lax.axis_index("c")
@@ -265,27 +271,53 @@
 
     both = grad.astype(jnp.float32) + buffer.astype(jnp.float32)
     combined = lax.reduce_precision(both, exponent_bits=8, mantissa_bits=7)
+    combined = lax.optimization_barrier(combined.astype(jnp.bfloat16))
     part = start_sketch(basis_init, combined)
     image = island_sum(part)
     basis = lax.dynamic_slice_in_dim(basis_init, me * width, width, 0)
     basis = jnp.where(core == 0, basis, jnp.roll(basis, half, axis=0)).T
-    near, far = total[:, :half], total[:, half:]
-    right = row_sum(dot(image, near, 1, 0), dot(image, far, 1, 0))
-    for _ in range(1, ITERS):
-        part = jnp.concatenate([dot(right, total, 1, 1), dot(basis, right, 1, 1)], axis=1)
+    side = rank // 2
+
+    def gram_half(basis, right):
+        own = lax.dynamic_slice_in_dim(basis, core * side, side, 0)
+        return dot(right, own, 1, 1)
+
+    def gram_whole(own):
+        other = swap(own)
+        first, second = jnp.where(core == 0, own, other), jnp.where(core == 0, other, own)
+        return jnp.concatenate([first, second], axis=1)
+
+    def raw_sum(image):
+        return row_sum(dot(image, total[:, :half], 1, 0), dot(image, total[:, half:], 1, 0))
+
+    near = raw_sum(image)
+
+    def sweep(_, carry):
+        near, basis = carry[:2]
+        far = swap(near)
+        right = jnp.concatenate([near, far], axis=1)
+        part = jnp.concatenate([dot(right, total, 1, 1), gram_half(basis, right)], axis=1)
         summed = island_sum(part)
-        image, gram = summed[:, :rows], summed[:, rows:]
-        raw = dot(image, near, 1, 0), dot(image, far, 1, 0)
-        inverse = inverse_factor(gram)
+        image = summed[:, :rows]
+        raw = raw_sum(image)
+        inverse = inverse_factor(gram_whole(summed[:, rows:]))
         basis = dot(inverse, right, 1, 0)
-        right = row_sum(*raw, inverse)
+        near = dot(inverse, raw, 1, 0)
+        return near, basis, image, inverse
+
+    square = jnp.zeros((rank, rank), jnp.float32)
+    near, basis, image, inverse = lax.fori_loop(
+        1, ITERS, sweep, (near, basis, jnp.zeros_like(image), square)
+    )
+    nears = island_parts(near)
+    far = swap(near)
+    others = swap(jnp.stack(nears[1:]))
+    fars = [far] + [others[i] for i in range(islands - 1)]
+    right = jnp.concatenate([near, fars[0]], axis=1)
     gram = island_sum(dot(basis, right, 1, 1))
-    rights = island_parts(right)
-    last = inverse_factor(gram)
-    sketch = dot(last, dot(inverse, image, 1, 0), 1, 0)
-    left = dot(sketch, last, 0, 0) * (1.0 / islands)
+    sketch = dot(inverse, image, 1, 0)
     new_error, new_params, new_momentum = finish(
-        me, core, left, rights, grad, buffer, params, momentum
+        me, core, gram, sketch, combined, nears, fars, params, momentum
     )
     return (new_error[None], new_params, new_momentum)
 

time: 250 us -> 246 us (0.984)
  blocking collectives: 78 us -> 0 us
  waiting for transfers between devices: 57.4 us -> 102 us
  starting transfers between devices: 47.8 us -> 79.7 us
  matrix products: 20.4 us -> 15.9 us
  other arithmetic: 7.43 us -> 11.9 us
  Pallas kernels: 29.9 us -> 27 us
    all_to_all x5 -> x0, blocking collectives: 78 us -> none  [the longest x4 64.1 us: row_sum(): own = jnp.sum(lax.all_to_all(parts, ROW, 0, 0), axis=0)]
    all_to_all x0 -> x4, waiting for transfers between devices: none -> 39.1 us  [row_sum(): own = jnp.sum(lax.all_to_all(parts, ROW, 0, 0), axis=0)]
    all_to_all x0 -> x4, starting transfers between devices: none -> 23.1 us  [row_sum(): own = jnp.sum(lax.all_to_all(parts, ROW, 0, 0), axis=0)]
    ppermute x18, waiting for transfers between devices: 25.3 us -> 12.6 us  [island_parts(): return [v] + [lax.ppermute(v, 'x', ring(4, s)) for s in (1, 2, 3)]]
    all_to_all x3 -> x4, waiting for transfers between devices: 16.8 us -> 28.6 us  [row_sum(): full = lax.all_to_all(jnp.broadcast_to(own, parts.shape), ROW, 0, 0)]
    pallas_call x4 -> x3, Pallas kernels: 15.2 us -> 9.5 us  [inverse_factor(): pl.pallas_call(factor_kernel, out_shape=jax.ShapeDtypeStruct((n, n), jnp....]
    ppermute x8 -> x12, waiting for transfers between devices: 7.45 us -> 12.5 us  [swap(): return lax.ppermute(v, 'c', ring(2, 1))]
    all_to_all x3 -> x4, starting transfers between devices: 11.6 us -> 15.6 us  [row_sum(): full = lax.all_to_all(jnp.broadcast_to(own, parts.shape), ROW, 0, 0)]
  transfers between devices with their start and end apart: 35 -> 44, of which waited for: 27 -> 33; matrix products, arithmetic and copies ran while one was open for 7% -> 7% of each run, Pallas kernels for 9% -> 7%
where the time goes in v1:
time: 246 us; the launch traced here: 242 us
  waiting for transfers between devices  102 us (41%)
  starting transfers between devices  79.7 us (32%)
  Pallas kernels  27 us (11%)
  matrix products  15.9 us (6%)
  other arithmetic  11.9 us (5%)
  local copies, waits for them, and re-layouts  3.81 us (2%)
    all_to_all x4, waiting for transfers between devices, row_sum(): own = jnp.sum(lax.all_to_all(parts, ROW, 0, 0), axis=0)  39.1 us
    ppermute x18, starting transfers between devices, island_parts(): return [v] + [lax.ppermute(v, 'x', ring(4, s)) for s in (1, 2, 3)]  31.2 us
    all_to_all x4, waiting for transfers between devices, row_sum(): full = lax.all_to_all(jnp.broadcast_to(own, parts.shape), ROW, 0, 0)  28.6 us
    all_to_all x4, starting transfers between devices, row_sum(): own = jnp.sum(lax.all_to_all(parts, ROW, 0, 0), axis=0)  23.1 us
    all_to_all x4, starting transfers between devices, row_sum(): full = lax.all_to_all(jnp.broadcast_to(own, parts.shape), ROW, 0, 0)  15.6 us
    dot_general x22, matrix products, dot(): lax.dot_general(a, b, (((ca,), (cb,)), ((), ())), precision=lax.Precision...  13.7 us
    ppermute x18, waiting for transfers between devices, island_parts(): return [v] + [lax.ppermute(v, 'x', ring(4, s)) for s in (1, 2, 3)]  12.6 us
    ppermute x12, waiting for transfers between devices, swap(): return lax.ppermute(v, 'c', ring(2, 1))  12.5 us
  transfers between devices with their start and end apart: 44, of which 33 were waited for; matrix products, arithmetic and copies ran while one was open for 7% of the time, Pallas kernels for 7%

profile of v1, /device:TPU:2, one launch (start us, length us, event | category | flops | bytes accessed | tf_op | source)
XLA Modules:
  0.0 241.8 jit_solution(9612570536180415374)
XLA Ops:
  2.8 2.2 collective-permute-start.9
  9.3 3.4 %reduce-precision_convert_fusion.combined_ref = bf16[224,4096]{1,0:T(8,128)(2,1)} fusion(bf16[1,224,4096]{2,1,0:T(8,128)(2,1)S(1)} %copy-done, bf16[1,224,4096]{2,1,0:T(8,128)(2,1)} %param.7), kind=kLoop, calls=%fused_computation.14 | loop fusion | flops 4587520 | bytes 5505024 | tf_op jit(solution)/shard_map/convert_element_type | solution.py:274
  23.2 2.4 collective-permute-done.13
  25.6 3.7 %collective-permute-start.6 = (f32[64,224]{1,0:T(8,128)S(1)}, f32[64,224]{1,0:T(8,128)S(1)}, u32[]{:S(2)}, u32[]{:S(2)}) collective-permute-start(f32[64,224]{1,0:T(8,128)S(1)} %slice_add_fusion), channel_id=1, source_target_pairs={{0,128},{64,192},{128,0},{192,64},{1,129},{65,193},{129,1},{193,65... | collective-permute-start | bytes 172040 | tf_op jit(solution)/shard_map/ppermute | solution.py:30
  34.5 3.7 %collective-permute-start.14 = (f32[112,1024]{1,0:T(8,128)S(1)}, f32[112,1024]{1,0:T(8,128)S(1)}, u32[]{:S(2)}, u32[]{:S(2)}) collective-permute-start(f32[112,1024]{1,0:T(8,128)S(1)} %add.103), channel_id=1, source_target_pairs={{0,192},{64,0},{128,64},{192,128},{1,193},{65,1},{129,65},{193,129... | collective-permute-start | bytes 1376264 | tf_op jit(solution)/shard_map/ppermute | solution.py:240
  39.4 6.6 %collective-permute-done.12 = f32[112,1024]{1,0:T(8,128)S(1)} collective-permute-done((f32[112,1024]{1,0:T(8,128)S(1)}, f32[112,1024]{1,0:T(8,128)S(1)}, u32[]{:S(2)}, u32[]{:S(2)}) %collective-permute-start.12) | collective-permute-done | bytes 458784 | tf_op jit(solution)/shard_map/ppermute | solution.py:240
  49.0 11.5 %all-to-all-start.2 = ((f32[32,8,128]{2,1,0:T(8,128)}), f32[32,8,128]{2,1,0:T(8,128)S(1)}, u32[]{:S(2)}, u32[]{:S(2)}) async-start(f32[32,8,128]{2,1,0:T(8,128)} %bitcast.16), calls=%async_computation.2 | async-start | bytes 262144 | tf_op jit(solution)/shard_map/all_to_all | solution.py:109
  60.5 10.6 %all-to-all-done.2 = f32[32,8,128]{2,1,0:T(8,128)S(1)} async-done(((f32[32,8,128]{2,1,0:T(8,128)}), f32[32,8,128]{2,1,0:T(8,128)S(1)}, u32[]{:S(2)}, u32[]{:S(2)}) %all-to-all-start.2) | async-done | bytes 131104 | tf_op jit(solution)/shard_map/all_to_all | solution.py:109
  71.8 4.0 %all-to-all-start.3 = ((f32[32,8,128]{2,1,0:T(8,128)}), f32[32,8,128]{2,1,0:T(8,128)S(1)}, u32[]{:S(2)}, u32[]{:S(2)}) async-start(f32[32,8,128]{2,1,0:T(8,128)} %broadcast_in_dim.17), calls=%async_computation.3 | async-start | bytes 262144 | tf_op jit(solution)/shard_map/all_to_all | solution.py:110
  76.0 10.1 %all-to-all-done.3 = f32[32,8,128]{2,1,0:T(8,128)S(1)} async-done(((f32[32,8,128]{2,1,0:T(8,128)}), f32[32,8,128]{2,1,0:T(8,128)S(1)}, u32[]{:S(2)}, u32[]{:S(2)}) %all-to-all-start.3) | async-done | bytes 131104 | tf_op jit(solution)/shard_map/all_to_all | solution.py:110
  86.1 132.1 %while.18 = (s32[]{:T(128)}, f32[64,512]{1,0:T(8,128)S(1)}, f32[64,1024]{1,0:T(8,128)S(1)}, f32[64,224]{1,0:T(8,128)}, f32[64,64]{1,0:T(8,128)}, /*index=5*/pred...) while((s32[]{:T(128)}, f32[64,512]{1,0:T(8,128)S(1)}, f32[64,1024]{1,0:T(8,128)S(1)}, ...), condition=%wide.region_3.4_spmd, body=%wide.region_1.3_spmd.sunk | while | flops 469916672 | bytes 24994260 | solution.py:309
  88.9 4.8 %collective-permute-start.3 = (f32[64,256]{1,0:T(8,128)S(1)}, f32[64,256]{1,0:T(8,128)S(1)}, u32[]{:S(2)}, u32[]{:S(2)}) collective-permute-start(f32[64,256]{1,0:T(8,128)S(1)} %pad_maximum_fusion.6), channel_id=1, source_target_pairs={{0,128},{64,192},{128,0},{192,64},{1,129},{65,193},{129,1},{193,65... | collective-permute-start | bytes 196616 | tf_op jit(solution)/shard_map/while/body/eval_jaxpr/ppermute | solution.py:30
  100.9 3.9 %all-to-all-start = ((f32[32,8,128]{2,1,0:T(8,128)}), f32[32,8,128]{2,1,0:T(8,128)S(1)}, u32[]{:S(2)}, u32[]{:S(2)}) async-start(f32[32,8,128]{2,1,0:T(8,128)} %bitcast.80), calls=%async_computation | async-start | bytes 262144 | tf_op jit(solution)/shard_map/while/body/eval_jaxpr/all_to_all | solution.py:109
  106.2 9.5 %all-to-all-done = f32[32,8,128]{2,1,0:T(8,128)S(1)} async-done(((f32[32,8,128]{2,1,0:T(8,128)}), f32[32,8,128]{2,1,0:T(8,128)S(1)}, u32[]{:S(2)}, u32[]{:S(2)}) %all-to-all-start) | async-done | bytes 131104 | tf_op jit(solution)/shard_map/while/body/eval_jaxpr/all_to_all | solution.py:109
  116.4 3.9 %all-to-all-start.1 = ((f32[32,8,128]{2,1,0:T(8,128)}), f32[32,8,128]{2,1,0:T(8,128)S(1)}, u32[]{:S(2)}, u32[]{:S(2)}) async-start(f32[32,8,128]{2,1,0:T(8,128)} %broadcast_in_dim.22), calls=%async_computation.1 | async-start | bytes 262144 | tf_op jit(solution)/shard_map/while/body/eval_jaxpr/all_to_all | solution.py:110
  121.0 3.2 %factor.3 = f32[64,64]{1,0:T(8,128)S(1)} custom-call(f32[64,64]{1,0:T(8,128)} %pad_maximum_fusion.7.gram_ref), custom_call_target="tpu_custom_call" | custom-call | flops 16777216 | bytes 16777216 | tf_op jit(solution)/shard_map/while/body/eval_jaxpr/factor/pallas_call | solution.py:82
  124.5 6.2 %all-to-all-done.1 = f32[32,8,128]{2,1,0:T(8,128)S(1)} async-done(((f32[32,8,128]{2,1,0:T(8,128)}), f32[32,8,128]{2,1,0:T(8,128)S(1)}, u32[]{:S(2)}, u32[]{:S(2)}) %all-to-all-start.1) | async-done | bytes 131104 | tf_op jit(solution)/shard_map/while/body/eval_jaxpr/all_to_all | solution.py:110
  133.8 2.6 %collective-permute-start.3 = (f32[64,256]{1,0:T(8,128)S(1)}, f32[64,256]{1,0:T(8,128)S(1)}, u32[]{:S(2)}, u32[]{:S(2)}) collective-permute-start(f32[64,256]{1,0:T(8,128)S(1)} %pad_maximum_fusion.6), channel_id=1, source_target_pairs={{0,128},{64,192},{128,0},{192,64},{1,129},{65,193},{129,1},{193,65... | collective-permute-start | bytes 196616 | tf_op jit(solution)/shard_map/while/body/eval_jaxpr/ppermute | solution.py:30
  145.2 3.9 %all-to-all-start = ((f32[32,8,128]{2,1,0:T(8,128)}), f32[32,8,128]{2,1,0:T(8,128)S(1)}, u32[]{:S(2)}, u32[]{:S(2)}) async-start(f32[32,8,128]{2,1,0:T(8,128)} %bitcast.80), calls=%async_computation | async-start | bytes 262144 | tf_op jit(solution)/shard_map/while/body/eval_jaxpr/all_to_all | solution.py:109
  150.5 9.5 %all-to-all-done = f32[32,8,128]{2,1,0:T(8,128)S(1)} async-done(((f32[32,8,128]{2,1,0:T(8,128)}), f32[32,8,128]{2,1,0:T(8,128)S(1)}, u32[]{:S(2)}, u32[]{:S(2)}) %all-to-all-start) | async-done | bytes 131104 | tf_op jit(solution)/shard_map/while/body/eval_jaxpr/all_to_all | solution.py:109
  160.7 3.9 %all-to-all-start.1 = ((f32[32,8,128]{2,1,0:T(8,128)}), f32[32,8,128]{2,1,0:T(8,128)S(1)}, u32[]{:S(2)}, u32[]{:S(2)}) async-start(f32[32,8,128]{2,1,0:T(8,128)} %broadcast_in_dim.22), calls=%async_computation.1 | async-start | bytes 262144 | tf_op jit(solution)/shard_map/while/body/eval_jaxpr/all_to_all | solution.py:110
  165.2 3.2 %factor.3 = f32[64,64]{1,0:T(8,128)S(1)} custom-call(f32[64,64]{1,0:T(8,128)} %pad_maximum_fusion.7.gram_ref), custom_call_target="tpu_custom_call" | custom-call | flops 16777216 | bytes 16777216 | tf_op jit(solution)/shard_map/while/body/eval_jaxpr/factor/pallas_call | solution.py:82
  168.8 6.2 %all-to-all-done.1 = f32[32,8,128]{2,1,0:T(8,128)S(1)} async-done(((f32[32,8,128]{2,1,0:T(8,128)}), f32[32,8,128]{2,1,0:T(8,128)S(1)}, u32[]{:S(2)}, u32[]{:S(2)}) %all-to-all-start.1) | async-done | bytes 131104 | tf_op jit(solution)/shard_map/while/body/eval_jaxpr/all_to_all | solution.py:110
  181.5 3.1 %collective-permute-done.3 = f32[64,256]{1,0:T(8,128)S(1)} collective-permute-done((f32[64,256]{1,0:T(8,128)S(1)}, f32[64,256]{1,0:T(8,128)S(1)}, u32[]{:S(2)}, u32[]{:S(2)}) %collective-permute-start.3) | collective-permute-done | bytes 65568 | tf_op jit(solution)/shard_map/while/body/eval_jaxpr/ppermute | solution.py:30
  188.2 3.9 %all-to-all-start = ((f32[32,8,128]{2,1,0:T(8,128)}), f32[32,8,128]{2,1,0:T(8,128)S(1)}, u32[]{:S(2)}, u32[]{:S(2)}) async-start(f32[32,8,128]{2,1,0:T(8,128)} %bitcast.80), calls=%async_computation | async-start | bytes 262144 | tf_op jit(solution)/shard_map/while/body/eval_jaxpr/all_to_all | solution.py:109
  193.5 9.5 %all-to-all-done = f32[32,8,128]{2,1,0:T(8,128)S(1)} async-done(((f32[32,8,128]{2,1,0:T(8,128)}), f32[32,8,128]{2,1,0:T(8,128)S(1)}, u32[]{:S(2)}, u32[]{:S(2)}) %all-to-all-start) | async-done | bytes 131104 | tf_op jit(solution)/shard_map/while/body/eval_jaxpr/all_to_all | solution.py:109
  203.7 3.9 %all-to-all-start.1 = ((f32[32,8,128]{2,1,0:T(8,128)}), f32[32,8,128]{2,1,0:T(8,128)S(1)}, u32[]{:S(2)}, u32[]{:S(2)}) async-start(f32[32,8,128]{2,1,0:T(8,128)} %broadcast_in_dim.22), calls=%async_computation.1 | async-start | bytes 262144 | tf_op jit(solution)/shard_map/while/body/eval_jaxpr/all_to_all | solution.py:110
  208.2 3.2 %factor.3 = f32[64,64]{1,0:T(8,128)S(1)} custom-call(f32[64,64]{1,0:T(8,128)} %pad_maximum_fusion.7.gram_ref), custom_call_target="tpu_custom_call" | custom-call | flops 16777216 | bytes 16777216 | tf_op jit(solution)/shard_map/while/body/eval_jaxpr/factor/pallas_call | solution.py:82
  211.8 6.2 %all-to-all-done.1 = f32[32,8,128]{2,1,0:T(8,128)S(1)} async-done(((f32[32,8,128]{2,1,0:T(8,128)}), f32[32,8,128]{2,1,0:T(8,128)S(1)}, u32[]{:S(2)}, u32[]{:S(2)}) %all-to-all-start.1) | async-done | bytes 131104 | tf_op jit(solution)/shard_map/while/body/eval_jaxpr/all_to_all | solution.py:110
  218.3 3.2 %collective-permute-start.22 = (f32[64,512]{1,0:T(8,128)S(1)}, f32[64,512]{1,0:T(8,128)S(1)}, u32[]{:S(2)}, u32[]{:S(2)}) collective-permute-start(f32[64,512]{1,0:T(8,128)S(1)} %get-tuple-element.111.refs_0_), channel_id=1, source_target_pairs={{0,192},{64,0},{128,64},{192,128},{1,193},{65,1},{129,65},{193,129... | collective-permute-start | bytes 393224 | tf_op jit(solution)/shard_map/ppermute | solution.py:30
  226.2 2.6 %collective-permute-start.17 = (f32[64,64]{1,0:T(8,128)S(1)}, f32[64,64]{1,0:T(8,128)S(1)}, u32[]{:S(2)}, u32[]{:S(2)}) collective-permute-start(f32[64,64]{1,0:T(8,128)S(1)} %fusion.20), channel_id=1, source_target_pairs={{0,128},{64,192},{128,0},{192,64},{1,129},{65,193},{129,1},{193,65... | collective-permute-start | bytes 49160 | tf_op jit(solution)/shard_map/ppermute | solution.py:30
  233.0 8.7 %finish.1 = (bf16[224,4096]{1,0:T(8,128)(2,1)}, f32[56,4096]{1,0:T(8,128)}, f32[56,4096]{1,0:T(8,128)}) custom-call(s32[1]{0:T(128)} %bitcast.6.me_ref, s32[1]{0:T(128)} %bitcast.7.core_ref, f32[64,64]{1,0:T(8,128)} %add_add_fusion.4.gram_ref, f32[64,224]{1,0:T(8,128)} %fusion.31.sketch_ref, bf16[224,4096]{1,0:T(8,128)(2,1)} %reduce-precision_convert_fusion.combined_ref, ...), custom_call_target="tpu_custom_call" | custom-call | tf_op jit(solution)/shard_map/finish/pallas_call | solution.py:203
  (169 shorter events, 77.6 us)
Async XLA Ops:
  2.8 35.5 %collective-permute-start.9 = (f32[112,1024]{1,0:T(8,128)}, f32[112,1024]{1,0:T(8,128)}, u32[]{:S(2)}, u32[]{:S(2)}) collective-permute-start(f32[112,1024]{1,0:T(8,128)} %get-tuple-element.103), channel_id=1, source_target_pairs={{0,192},{64,0},{128,64},{192,128},{1,193},{65,1},{129,65},{193,129... | collective-permute-start | bytes 1376264 | tf_op jit(solution)/shard_map/ppermute | solution.py:240
  7.3 11.6 %collective-permute-start.10 = (f32[112,1024]{1,0:T(8,128)}, f32[112,1024]{1,0:T(8,128)}, u32[]{:S(2)}, u32[]{:S(2)}) collective-permute-start(f32[112,1024]{1,0:T(8,128)} %get-tuple-element.105), channel_id=1, source_target_pairs={{0,64},{64,128},{128,192},{192,0},{1,65},{65,129},{129,193},{193,1... | collective-permute-start | bytes 1376264 | tf_op jit(solution)/shard_map/ppermute | solution.py:240
  7.3 18.3 %collective-permute-start.13 = (f32[112,1024]{1,0:T(8,128)}, f32[112,1024]{1,0:T(8,128)}, u32[]{:S(2)}, u32[]{:S(2)}) collective-permute-start(f32[112,1024]{1,0:T(8,128)} %get-tuple-element.109), channel_id=1, source_target_pairs={{0,192},{64,0},{128,64},{192,128},{1,193},{65,1},{129,65},{193,129... | collective-permute-start | bytes 1376264 | tf_op jit(solution)/shard_map/ppermute | solution.py:240
  20.0 18.3 %collective-permute-start.11 = (f32[112,1024]{1,0:T(8,128)S(1)}, f32[112,1024]{1,0:T(8,128)S(1)}, u32[]{:S(2)}, u32[]{:S(2)}) collective-permute-start(f32[112,1024]{1,0:T(8,128)S(1)} %add.100), channel_id=1, source_target_pairs={{0,64},{64,128},{128,192},{192,0},{1,65},{65,129},{129,193},{193,1... | collective-permute-start | bytes 1376264 | tf_op jit(solution)/shard_map/ppermute | solution.py:240
  20.6 14.0 %collective-permute-start.7 = (f32[64,224]{1,0:T(8,128)S(1)}, f32[64,224]{1,0:T(8,128)S(1)}, u32[]{:S(2)}, u32[]{:S(2)}) collective-permute-start(f32[64,224]{1,0:T(8,128)S(1)} %slice_add_fusion), channel_id=1, source_target_pairs={{0,64},{64,128},{128,192},{192,0},{1,65},{65,129},{129,193},{193,1... | collective-permute-start | bytes 172040 | tf_op jit(solution)/shard_map/ppermute | solution.py:30
  22.1 12.4 %collective-permute-start.8 = (f32[64,224]{1,0:T(8,128)S(1)}, f32[64,224]{1,0:T(8,128)S(1)}, u32[]{:S(2)}, u32[]{:S(2)}) collective-permute-start(f32[64,224]{1,0:T(8,128)S(1)} %slice_add_fusion), channel_id=1, source_target_pairs={{0,192},{64,0},{128,64},{192,128},{1,193},{65,1},{129,65},{193,129... | collective-permute-start | bytes 172040 | tf_op jit(solution)/shard_map/ppermute | solution.py:30
  25.6 12.7 %collective-permute-start.6 = (f32[64,224]{1,0:T(8,128)S(1)}, f32[64,224]{1,0:T(8,128)S(1)}, u32[]{:S(2)}, u32[]{:S(2)}) collective-permute-start(f32[64,224]{1,0:T(8,128)S(1)} %slice_add_fusion), channel_id=1, source_target_pairs={{0,128},{64,192},{128,0},{192,64},{1,129},{65,193},{129,1},{193,65... | collective-permute-start | bytes 172040 | tf_op jit(solution)/shard_map/ppermute | solution.py:30
  34.5 11.5 %collective-permute-start.12 = (f32[112,1024]{1,0:T(8,128)S(1)}, f32[112,1024]{1,0:T(8,128)S(1)}, u32[]{:S(2)}, u32[]{:S(2)}) collective-permute-start(f32[112,1024]{1,0:T(8,128)S(1)} %copy-done.13), channel_id=1, source_target_pairs={{0,64},{64,128},{128,192},{192,0},{1,65},{65,129},{129,193},{193,1... | collective-permute-start | bytes 1376264 | tf_op jit(solution)/shard_map/ppermute | solution.py:240
  34.5 11.5 %collective-permute-start.14 = (f32[112,1024]{1,0:T(8,128)S(1)}, f32[112,1024]{1,0:T(8,128)S(1)}, u32[]{:S(2)}, u32[]{:S(2)}) collective-permute-start(f32[112,1024]{1,0:T(8,128)S(1)} %add.103), channel_id=1, source_target_pairs={{0,192},{64,0},{128,64},{192,128},{1,193},{65,1},{129,65},{193,129... | collective-permute-start | bytes 1376264 | tf_op jit(solution)/shard_map/ppermute | solution.py:240
  49.0 22.1 %all-to-all-start.2 = ((f32[32,8,128]{2,1,0:T(8,128)}), f32[32,8,128]{2,1,0:T(8,128)S(1)}, u32[]{:S(2)}, u32[]{:S(2)}) async-start(f32[32,8,128]{2,1,0:T(8,128)} %bitcast.16), calls=%async_computation.2 | async-start | bytes 262144 | tf_op jit(solution)/shard_map/all_to_all | solution.py:109
  71.8 14.3 %all-to-all-start.3 = ((f32[32,8,128]{2,1,0:T(8,128)}), f32[32,8,128]{2,1,0:T(8,128)S(1)}, u32[]{:S(2)}, u32[]{:S(2)}) async-start(f32[32,8,128]{2,1,0:T(8,128)} %broadcast_in_dim.17), calls=%async_computation.3 | async-start | bytes 262144 | tf_op jit(solution)/shard_map/all_to_all | solution.py:110
  88.9 7.7 %collective-permute-start.3 = (f32[64,256]{1,0:T(8,128)S(1)}, f32[64,256]{1,0:T(8,128)S(1)}, u32[]{:S(2)}, u32[]{:S(2)}) collective-permute-start(f32[64,256]{1,0:T(8,128)S(1)} %pad_maximum_fusion.6), channel_id=1, source_target_pairs={{0,128},{64,192},{128,0},{192,64},{1,129},{65,193},{129,1},{193,65... | collective-permute-start | bytes 196616 | tf_op jit(solution)/shard_map/while/body/eval_jaxpr/ppermute | solution.py:30
  93.7 4.3 %collective-permute-start.2 = (f32[64,256]{1,0:T(8,128)S(1)}, f32[64,256]{1,0:T(8,128)S(1)}, u32[]{:S(2)}, u32[]{:S(2)}) collective-permute-start(f32[64,256]{1,0:T(8,128)S(1)} %pad_maximum_fusion.6), channel_id=1, source_target_pairs={{0,192},{64,0},{128,64},{192,128},{1,193},{65,1},{129,65},{193,129... | collective-permute-start | bytes 196616 | tf_op jit(solution)/shard_map/while/body/eval_jaxpr/ppermute | solution.py:30
  93.7 4.3 %collective-permute-start.1 = (f32[64,256]{1,0:T(8,128)S(1)}, f32[64,256]{1,0:T(8,128)S(1)}, u32[]{:S(2)}, u32[]{:S(2)}) collective-permute-start(f32[64,256]{1,0:T(8,128)S(1)} %pad_maximum_fusion.6), channel_id=1, source_target_pairs={{0,64},{64,128},{128,192},{192,0},{1,65},{65,129},{129,193},{193,1... | collective-permute-start | bytes 196616 | tf_op jit(solution)/shard_map/while/body/eval_jaxpr/ppermute | solution.py:30
  100.9 14.8 %all-to-all-start = ((f32[32,8,128]{2,1,0:T(8,128)}), f32[32,8,128]{2,1,0:T(8,128)S(1)}, u32[]{:S(2)}, u32[]{:S(2)}) async-start(f32[32,8,128]{2,1,0:T(8,128)} %bitcast.80), calls=%async_computation | async-start | bytes 262144 | tf_op jit(solution)/shard_map/while/body/eval_jaxpr/all_to_all | solution.py:109
  116.4 14.3 %all-to-all-start.1 = ((f32[32,8,128]{2,1,0:T(8,128)}), f32[32,8,128]{2,1,0:T(8,128)S(1)}, u32[]{:S(2)}, u32[]{:S(2)}) async-start(f32[32,8,128]{2,1,0:T(8,128)} %broadcast_in_dim.22), calls=%async_computation.1 | async-start | bytes 262144 | tf_op jit(solution)/shard_map/while/body/eval_jaxpr/all_to_all | solution.py:110
  133.8 5.9 %collective-permute-start.3 = (f32[64,256]{1,0:T(8,128)S(1)}, f32[64,256]{1,0:T(8,128)S(1)}, u32[]{:S(2)}, u32[]{:S(2)}) collective-permute-start(f32[64,256]{1,0:T(8,128)S(1)} %pad_maximum_fusion.6), channel_id=1, source_target_pairs={{0,128},{64,192},{128,0},{192,64},{1,129},{65,193},{129,1},{193,65... | collective-permute-start | bytes 196616 | tf_op jit(solution)/shard_map/while/body/eval_jaxpr/ppermute | solution.py:30
  136.5 4.6 %collective-permute-start.2 = (f32[64,256]{1,0:T(8,128)S(1)}, f32[64,256]{1,0:T(8,128)S(1)}, u32[]{:S(2)}, u32[]{:S(2)}) collective-permute-start(f32[64,256]{1,0:T(8,128)S(1)} %pad_maximum_fusion.6), channel_id=1, source_target_pairs={{0,192},{64,0},{128,64},{192,128},{1,193},{65,1},{129,65},{193,129... | collective-permute-start | bytes 196616 | tf_op jit(solution)/shard_map/while/body/eval_jaxpr/ppermute | solution.py:30
  138.0 4.3 %collective-permute-start.1 = (f32[64,256]{1,0:T(8,128)S(1)}, f32[64,256]{1,0:T(8,128)S(1)}, u32[]{:S(2)}, u32[]{:S(2)}) collective-permute-start(f32[64,256]{1,0:T(8,128)S(1)} %pad_maximum_fusion.6), channel_id=1, source_target_pairs={{0,64},{64,128},{128,192},{192,0},{1,65},{65,129},{129,193},{193,1... | collective-permute-start | bytes 196616 | tf_op jit(solution)/shard_map/while/body/eval_jaxpr/ppermute | solution.py:30
  145.2 14.8 %all-to-all-start = ((f32[32,8,128]{2,1,0:T(8,128)}), f32[32,8,128]{2,1,0:T(8,128)S(1)}, u32[]{:S(2)}, u32[]{:S(2)}) async-start(f32[32,8,128]{2,1,0:T(8,128)} %bitcast.80), calls=%async_computation | async-start | bytes 262144 | tf_op jit(solution)/shard_map/while/body/eval_jaxpr/all_to_all | solution.py:109
  160.7 14.3 %all-to-all-start.1 = ((f32[32,8,128]{2,1,0:T(8,128)}), f32[32,8,128]{2,1,0:T(8,128)S(1)}, u32[]{:S(2)}, u32[]{:S(2)}) async-start(f32[32,8,128]{2,1,0:T(8,128)} %broadcast_in_dim.22), calls=%async_computation.1 | async-start | bytes 262144 | tf_op jit(solution)/shard_map/while/body/eval_jaxpr/all_to_all | solution.py:110
  178.1 6.4 %collective-permute-start.3 = (f32[64,256]{1,0:T(8,128)S(1)}, f32[64,256]{1,0:T(8,128)S(1)}, u32[]{:S(2)}, u32[]{:S(2)}) collective-permute-start(f32[64,256]{1,0:T(8,128)S(1)} %pad_maximum_fusion.6), channel_id=1, source_target_pairs={{0,128},{64,192},{128,0},{192,64},{1,129},{65,193},{129,1},{193,65... | collective-permute-start | bytes 196616 | tf_op jit(solution)/shard_map/while/body/eval_jaxpr/ppermute | solution.py:30
  179.5 5.5 %collective-permute-start.2 = (f32[64,256]{1,0:T(8,128)S(1)}, f32[64,256]{1,0:T(8,128)S(1)}, u32[]{:S(2)}, u32[]{:S(2)}) collective-permute-start(f32[64,256]{1,0:T(8,128)S(1)} %pad_maximum_fusion.6), channel_id=1, source_target_pairs={{0,192},{64,0},{128,64},{192,128},{1,193},{65,1},{129,65},{193,129... | collective-permute-start | bytes 196616 | tf_op jit(solution)/shard_map/while/body/eval_jaxpr/ppermute | solution.py:30
  188.2 14.8 %all-to-all-start = ((f32[32,8,128]{2,1,0:T(8,128)}), f32[32,8,128]{2,1,0:T(8,128)S(1)}, u32[]{:S(2)}, u32[]{:S(2)}) async-start(f32[32,8,128]{2,1,0:T(8,128)} %bitcast.80), calls=%async_computation | async-start | bytes 262144 | tf_op jit(solution)/shard_map/while/body/eval_jaxpr/all_to_all | solution.py:109
  203.7 14.3 %all-to-all-start.1 = ((f32[32,8,128]{2,1,0:T(8,128)}), f32[32,8,128]{2,1,0:T(8,128)S(1)}, u32[]{:S(2)}, u32[]{:S(2)}) async-start(f32[32,8,128]{2,1,0:T(8,128)} %broadcast_in_dim.22), calls=%async_computation.1 | async-start | bytes 262144 | tf_op jit(solution)/shard_map/while/body/eval_jaxpr/all_to_all | solution.py:110
  218.2 4.9 %collective-permute-start.16 = (f32[64,512]{1,0:T(8,128)S(1)}, f32[64,512]{1,0:T(8,128)S(1)}, u32[]{:S(2)}, u32[]{:S(2)}) collective-permute-start(f32[64,512]{1,0:T(8,128)S(1)} %get-tuple-element.111.refs_0_), channel_id=1, source_target_pairs={{0,1},{1,0},{2,3},{3,2},{4,5},{5,4},{6,7},{7,6},{8,9},{9,8},{10,11... | collective-permute-start | bytes 393224 | tf_op jit(solution)/shard_map/ppermute | solution.py:103
  218.3 7.8 %collective-permute-start.22 = (f32[64,512]{1,0:T(8,128)S(1)}, f32[64,512]{1,0:T(8,128)S(1)}, u32[]{:S(2)}, u32[]{:S(2)}) collective-permute-start(f32[64,512]{1,0:T(8,128)S(1)} %get-tuple-element.111.refs_0_), channel_id=1, source_target_pairs={{0,192},{64,0},{128,64},{192,128},{1,193},{65,1},{129,65},{193,129... | collective-permute-start | bytes 393224 | tf_op jit(solution)/shard_map/ppermute | solution.py:30
  221.5 7.4 %collective-permute-start.21 = (f32[64,512]{1,0:T(8,128)S(1)}, f32[64,512]{1,0:T(8,128)S(1)}, u32[]{:S(2)}, u32[]{:S(2)}) collective-permute-start(f32[64,512]{1,0:T(8,128)S(1)} %get-tuple-element.111.refs_0_), channel_id=1, source_target_pairs={{0,128},{64,192},{128,0},{192,64},{1,129},{65,193},{129,1},{193,65... | collective-permute-start | bytes 393224 | tf_op jit(solution)/shard_map/ppermute | solution.py:30
  221.5 7.6 %collective-permute-start.20 = (f32[64,512]{1,0:T(8,128)S(1)}, f32[64,512]{1,0:T(8,128)S(1)}, u32[]{:S(2)}, u32[]{:S(2)}) collective-permute-start(f32[64,512]{1,0:T(8,128)S(1)} %get-tuple-element.111.refs_0_), channel_id=1, source_target_pairs={{0,64},{64,128},{128,192},{192,0},{1,65},{65,129},{129,193},{193,1... | collective-permute-start | bytes 393224 | tf_op jit(solution)/shard_map/ppermute | solution.py:30
  223.5 7.5 %collective-permute-start.19 = (f32[64,64]{1,0:T(8,128)S(1)}, f32[64,64]{1,0:T(8,128)S(1)}, u32[]{:S(2)}, u32[]{:S(2)}) collective-permute-start(f32[64,64]{1,0:T(8,128)S(1)} %fusion.20), channel_id=1, source_target_pairs={{0,192},{64,0},{128,64},{192,128},{1,193},{65,1},{129,65},{193,129... | collective-permute-start | bytes 49160 | tf_op jit(solution)/shard_map/ppermute | solution.py:30
  224.0 7.0 %collective-permute-start.18 = (f32[64,64]{1,0:T(8,128)S(1)}, f32[64,64]{1,0:T(8,128)S(1)}, u32[]{:S(2)}, u32[]{:S(2)}) collective-permute-start(f32[64,64]{1,0:T(8,128)S(1)} %fusion.20), channel_id=1, source_target_pairs={{0,64},{64,128},{128,192},{192,0},{1,65},{65,129},{129,193},{193,1... | collective-permute-start | bytes 49160 | tf_op jit(solution)/shard_map/ppermute | solution.py:30
  226.2 5.4 %collective-permute-start.17 = (f32[64,64]{1,0:T(8,128)S(1)}, f32[64,64]{1,0:T(8,128)S(1)}, u32[]{:S(2)}, u32[]{:S(2)}) collective-permute-start(f32[64,64]{1,0:T(8,128)S(1)} %fusion.20), channel_id=1, source_target_pairs={{0,128},{64,192},{128,0},{192,64},{1,129},{65,193},{129,1},{193,65... | collective-permute-start | bytes 49160 | tf_op jit(solution)/shard_map/ppermute | solution.py:30
  (30 other events, 208.1 us)

commit v2 on v1

--- a/solution.py
+++ b/solution.py
@@ -146,8 +146,11 @@
     return high, (v - high.astype(jnp.float32)).astype(jnp.bfloat16)
 
 
-def finish_kernel(me_ref, core_ref, gram_ref, sketch_ref, combined_ref, *refs):
-    near_refs, far_refs, rest = refs[:4], refs[4:8], refs[8:]
+def finish_kernel(me_ref, core_ref, *refs):
+    gram_refs, near_refs, refs = refs[:4], refs[4:8], refs[8:]
+    far_ref, others_ref, inverse_ref, image_ref, combined_ref = refs[:5]
+    far_refs = [far_ref] + [others_ref.at[i] for i in range(3)]
+    rest = refs[5:]
     params_ref, momentum_ref, error_out, params_out, momentum_out = rest[:5]
     left4, mine4, right, left, work = rest[5:]
     step = pl.program_id(0)
@@ -158,8 +161,10 @@
 
     @pl.when(step == 0)
     def _():
-        last = factor_into(gram_ref[...], work)
-        left[...] = dot(dot(last, sketch_ref[...], 1, 0), last, 0, 0) * (1.0 / islands)
+        a, b, c, d = [ref[...] for ref in gram_refs]
+        last = factor_into((a + c) + (b + d), work)
+        sketch = dot(inverse_ref[...], image_ref[...], 1, 0)
+        left[...] = dot(dot(last, sketch, 1, 0), last, 0, 0) * (1.0 / islands)
         high, low = low_high(left[...])
         left4[...] = jnp.concatenate([high, high, low, low], axis=1)
         own = pl.ds(pl.multiple_of(me_ref[0] * quarter, 8), quarter)
@@ -188,7 +193,7 @@
     params_out[...] = params_ref[...] - outer_rate * (mine + momentum_coef * moved)
 
 
-def finish(me, core, gram, sketch, combined, nears, fars, params, momentum):
+def finish(me, core, grams, nears, far, others, inverse, image, combined, params, momentum):
     rows, cols = combined.shape
     quarter = params.shape[0]
     rank, half = nears[0].shape
@@ -206,7 +211,7 @@
         grid_spec=pltpu.PrefetchScalarGridSpec(
             num_scalar_prefetch=2,
             grid=(islands,),
-            in_specs=[whole] * (3 + 2 * islands) + [block(quarter), block(quarter)],
+            in_specs=[whole] * (5 + 2 * islands) + [block(quarter), block(quarter)],
             out_specs=(block(rows), block(quarter), block(quarter)),
             scratch_shapes=[
                 pltpu.VMEM((rows, 4 * rank), jnp.bfloat16),
@@ -217,7 +222,19 @@
             ],
         ),
         name="finish",
-    )(me.reshape(1), core.reshape(1), gram, sketch, combined, *nears, *fars, params, momentum)
+    )(
+        me.reshape(1),
+        core.reshape(1),
+        *grams,
+        *nears,
+        far,
+        others,
+        inverse,
+        image,
+        combined,
+        params,
+        momentum,
+    )
 
 
 def start_sketch(basis, combined):
@@ -261,14 +278,6 @@
     from_above = hop(blocks[3][0], down)
     top_below = hop(blocks[1][0] + relay_up, up)
     bottom_above = hop(blocks[3][1] + relay_down, down)
-    total = jnp.concatenate(
-        [
-            (blocks[0][0] + from_above) + top_below,
-            (blocks[0][1] + from_below) + bottom_above,
-        ],
-        axis=0,
-    )
-
     both = grad.astype(jnp.float32) + buffer.astype(jnp.float32)
     combined = lax.reduce_precision(both, exponent_bits=8, mantissa_bits=7)
     combined = lax.optimization_barrier(combined.astype(jnp.bfloat16))
@@ -277,10 +286,36 @@
     basis = lax.dynamic_slice_in_dim(basis_init, me * width, width, 0)
     basis = jnp.where(core == 0, basis, jnp.roll(basis, half, axis=0)).T
     side = rank // 2
-
-    def gram_half(basis, right):
-        own = lax.dynamic_slice_in_dim(basis, core * side, side, 0)
-        return dot(right, own, 1, 1)
+    hold = lax.optimization_barrier
+
+    top = hold(blocks[0][0] + from_above)
+    bottom = hold(blocks[0][1] + from_below)
+    split = top.shape[0]
+    early = hold(dot(image[:, :split], top, 1, 0) + dot(image[:, split:], bottom, 1, 0))
+    top_image, bottom_image = image[:, :split], image[:, split:]
+
+    def late(columns):
+        return (
+            early[:, columns]
+            + dot(top_image, top_below[:, columns], 1, 0)
+            + dot(bottom_image, bottom_above[:, columns], 1, 0)
+        )
+
+    near_columns, far_columns = slice(0, half), slice(half, width)
+    far_part = late(far_columns)
+    near_part = hold(late(near_columns))
+    near = row_sum(near_part, far_part)
+    total_near, total_far = hold(
+        tuple(
+            jnp.concatenate(
+                [top[:, c] + top_below[:, c], bottom[:, c] + bottom_above[:, c]], axis=0
+            )
+            for c in (near_columns, far_columns)
+        )
+    )
+
+    def own_rows(basis):
+        return lax.dynamic_slice_in_dim(basis, core * side, side, 0)
 
     def gram_whole(own):
         other = swap(own)
@@ -288,36 +323,50 @@
         return jnp.concatenate([first, second], axis=1)
 
     def raw_sum(image):
-        return row_sum(dot(image, total[:, :half], 1, 0), dot(image, total[:, half:], 1, 0))
-
-    near = raw_sum(image)
+        far_part = dot(image, total_far, 1, 0)
+        return row_sum(hold(dot(image, total_near, 1, 0)), far_part)
 
     def sweep(_, carry):
-        near, basis = carry[:2]
+        near, basis_near, basis_far = carry[:3]
         far = swap(near)
-        right = jnp.concatenate([near, far], axis=1)
-        part = jnp.concatenate([dot(right, total, 1, 1), gram_half(basis, right)], axis=1)
-        summed = island_sum(part)
+        image = hold(dot(near, total_near, 1, 1))
+        gram = hold(dot(near, own_rows(basis_near), 1, 1))
+        image = image + dot(far, total_far, 1, 1)
+        gram = gram + dot(far, own_rows(basis_far), 1, 1)
+        summed = island_sum(jnp.concatenate([image, gram], axis=1))
         image = summed[:, :rows]
         raw = raw_sum(image)
         inverse = inverse_factor(gram_whole(summed[:, rows:]))
-        basis = dot(inverse, right, 1, 0)
+        basis_near = dot(inverse, near, 1, 0)
+        basis_far = dot(inverse, far, 1, 0)
         near = dot(inverse, raw, 1, 0)
-        return near, basis, image, inverse
+        return near, basis_near, basis_far, image, inverse
 
     square = jnp.zeros((rank, rank), jnp.float32)
-    near, basis, image, inverse = lax.fori_loop(
-        1, ITERS, sweep, (near, basis, jnp.zeros_like(image), square)
+    near, basis_near, basis_far, image, inverse = lax.fori_loop(
+        1,
+        ITERS,
+        sweep,
+        (near, basis[:, :half], basis[:, half:], jnp.zeros_like(image), square),
     )
     nears = island_parts(near)
     far = swap(near)
-    others = swap(jnp.stack(nears[1:]))
-    fars = [far] + [others[i] for i in range(islands - 1)]
-    right = jnp.concatenate([near, fars[0]], axis=1)
-    gram = island_sum(dot(basis, right, 1, 1))
-    sketch = dot(inverse, image, 1, 0)
+    gram = hold(dot(basis_near, near, 1, 1)) + dot(basis_far, far, 1, 1)
+    grams = island_parts(gram)
+    stacked = jnp.stack(nears[1:])
+    others = swap(stacked)
     new_error, new_params, new_momentum = finish(
-        me, core, gram, sketch, combined, nears, fars, params, momentum
+        me,
+        core,
+        grams,
+        nears,
+        far,
+        others,
+        inverse,
+        image,
+        combined,
+        params,
+        momentum,
     )
     return (new_error[None], new_params, new_momentum)
 

time: 246 us -> 250 us (1.016)
  waiting for transfers between devices: 102 us -> 111 us
  matrix products: 15.9 us -> 12.9 us
    ppermute x18, waiting for transfers between devices: 12.6 us -> 28.7 us  [island_parts(): return [v] + [lax.ppermute(v, 'x', ring(4, s)) for s in (1, 2, 3)]]
    all_to_all x4, waiting for transfers between devices: 28.6 us -> 39.8 us  [row_sum(): full = lax.all_to_all(jnp.broadcast_to(own, parts.shape), ROW, 0, 0)]
    ppermute x12, waiting for transfers between devices: 12.5 us -> 4.05 us  [swap(): return lax.ppermute(v, 'c', ring(2, 1))]
    all_to_all x4, waiting for transfers between devices: 39.1 us -> 32.3 us  [row_sum(): own = jnp.sum(lax.all_to_all(parts, ROW, 0, 0), axis=0)]
    ppermute x6, waiting for transfers between devices: 9.36 us -> 5.79 us  [hop(): return lax.ppermute(v, 'x', pairs)]
    ppermute x18, starting transfers between devices: 31.2 us -> 27.7 us  [island_parts(): return [v] + [lax.ppermute(v, 'x', ring(4, s)) for s in (1, 2, 3)]]
    add x2 -> x8, other arithmetic: 1.17 us -> 4.02 us  [the longest x4 2.69 us: row_sum(): near = near + swap(far)]
    dot_general x22 -> x35, matrix products: 13.7 us -> 12.2 us  [dot(): lax.dot_general(a, b, (((ca,), (cb,)), ((), ())), precision=lax.Precision...]
  transfers between devices with their start and end apart: 44 -> 44, of which waited for: 33 -> 29; matrix products, arithmetic and copies ran while one was open for 7% -> 7% of each run, Pallas kernels for 7% -> 7%
where the time goes in v2:
time: 250 us; the launch traced here: 248 us
  waiting for transfers between devices  111 us (44%)
  starting transfers between devices  78.6 us (31%)
  Pallas kernels  26.9 us (11%)
  other arithmetic  13.1 us (5%)
  matrix products  12.9 us (5%)
  local copies, waits for them, and re-layouts  4.45 us (2%)
    all_to_all x4, waiting for transfers between devices, row_sum(): full = lax.all_to_all(jnp.broadcast_to(own, parts.shape), ROW, 0, 0)  39.8 us
    all_to_all x4, waiting for transfers between devices, row_sum(): own = jnp.sum(lax.all_to_all(parts, ROW, 0, 0), axis=0)  32.3 us
    ppermute x18, waiting for transfers between devices, island_parts(): return [v] + [lax.ppermute(v, 'x', ring(4, s)) for s in (1, 2, 3)]  28.7 us
    ppermute x18, starting transfers between devices, island_parts(): return [v] + [lax.ppermute(v, 'x', ring(4, s)) for s in (1, 2, 3)]  27.7 us
    all_to_all x4, starting transfers between devices, row_sum(): own = jnp.sum(lax.all_to_all(parts, ROW, 0, 0), axis=0)  24.4 us
    all_to_all x4, starting transfers between devices, row_sum(): full = lax.all_to_all(jnp.broadcast_to(own, parts.shape), ROW, 0, 0)  15.6 us
    dot_general x35, matrix products, dot(): lax.dot_general(a, b, (((ca,), (cb,)), ((), ())), precision=lax.Precision...  12.2 us
    pallas_call x3, Pallas kernels, inverse_factor(): pl.pallas_call(factor_kernel, out_shape=jax.ShapeDtypeStruct((n, n), jnp....  9.5 us
  transfers between devices with their start and end apart: 44, of which 29 were waited for; matrix products, arithmetic and copies ran while one was open for 7% of the time, Pallas kernels for 7%

profile of v2, /device:TPU:2, one launch (start us, length us, event | category | flops | bytes accessed | tf_op | source)
XLA Modules:
  0.0 248.1 jit_solution(9747055210773825767)
XLA Ops:
  2.4 2.2 reduce-precision_convert_fusion.refs_12_
  17.9 3.3 %collective-permute-start.13 = (f32[112,1024]{1,0:T(8,128)}, f32[112,1024]{1,0:T(8,128)}, u32[]{:S(2)}, u32[]{:S(2)}) collective-permute-start(f32[112,1024]{1,0:T(8,128)} %get-tuple-element.134), channel_id=1, source_target_pairs={{0,192},{64,0},{128,64},{192,128},{1,193},{65,1},{129,65},{193,129... | collective-permute-start | bytes 1376264 | tf_op jit(solution)/shard_map/ppermute | solution.py:257
  25.5 11.7 %collective-permute-done.6 = f32[64,224]{1,0:T(8,128)S(1)} collective-permute-done((f32[64,224]{1,0:T(8,128)S(1)}, f32[64,224]{1,0:T(8,128)S(1)}, u32[]{:S(2)}, u32[]{:S(2)}) %collective-permute-start.6) | collective-permute-done | bytes 57376 | tf_op jit(solution)/shard_map/ppermute | solution.py:30
  43.7 4.8 %collective-permute-done.12 = f32[112,1024]{1,0:T(8,128)S(1)} collective-permute-done((f32[112,1024]{1,0:T(8,128)S(1)}, f32[112,1024]{1,0:T(8,128)S(1)}, u32[]{:S(2)}, u32[]{:S(2)}) %collective-permute-start.12) | collective-permute-done | bytes 458784 | tf_op jit(solution)/shard_map/ppermute | solution.py:257
  52.2 12.9 %all-to-all-start.2 = ((f32[32,8,128]{2,1,0:T(8,128)}), f32[32,8,128]{2,1,0:T(8,128)S(1)}, u32[]{:S(2)}, u32[]{:S(2)}) async-start(f32[32,8,128]{2,1,0:T(8,128)} %bitcast.18), calls=%async_computation.2 | async-start | bytes 262144 | tf_op jit(solution)/shard_map/all_to_all | solution.py:109
  65.2 10.5 %all-to-all-done.2 = f32[32,8,128]{2,1,0:T(8,128)S(1)} async-done(((f32[32,8,128]{2,1,0:T(8,128)}), f32[32,8,128]{2,1,0:T(8,128)S(1)}, u32[]{:S(2)}, u32[]{:S(2)}) %all-to-all-start.2) | async-done | bytes 131104 | tf_op jit(solution)/shard_map/all_to_all | solution.py:109
  76.4 4.0 %all-to-all-start.3 = ((f32[32,8,128]{2,1,0:T(8,128)}), f32[32,8,128]{2,1,0:T(8,128)S(1)}, u32[]{:S(2)}, u32[]{:S(2)}) async-start(f32[32,8,128]{2,1,0:T(8,128)} %broadcast_in_dim.17), calls=%async_computation.3 | async-start | bytes 262144 | tf_op jit(solution)/shard_map/all_to_all | solution.py:110
  80.6 10.3 %all-to-all-done.3 = f32[32,8,128]{2,1,0:T(8,128)S(1)} async-done(((f32[32,8,128]{2,1,0:T(8,128)}), f32[32,8,128]{2,1,0:T(8,128)S(1)}, u32[]{:S(2)}, u32[]{:S(2)}) %all-to-all-start.3) | async-done | bytes 131104 | tf_op jit(solution)/shard_map/all_to_all | solution.py:110
  90.9 129.2 %while.20 = (s32[]{:T(128)}, f32[64,512]{1,0:T(8,128)S(1)}, f32[64,512]{1,0:T(8,128)S(1)}, f32[64,512]{1,0:T(8,128)S(1)}, f32[64,224]{1,0:T(8,128)}, /*index=5*/...) while((s32[]{:T(128)}, f32[64,512]{1,0:T(8,128)S(1)}, ...), condition=%wide.region_3.4_spmd, body=%wide.region_1.3_spmd.sunk | while | flops 469933056 | bytes 24887784 | solution.py:346
  93.1 2.7 %collective-permute-start.3 = (f32[64,256]{1,0:T(8,128)S(1)}, f32[64,256]{1,0:T(8,128)S(1)}, u32[]{:S(2)}, u32[]{:S(2)}) collective-permute-start(f32[64,256]{1,0:T(8,128)S(1)} %pad_maximum_fusion.7), channel_id=1, source_target_pairs={{0,128},{64,192},{128,0},{192,64},{1,129},{65,193},{129,1},{193,65... | collective-permute-start | bytes 196616 | tf_op jit(solution)/shard_map/while/body/eval_jaxpr/ppermute | solution.py:30
  104.0 3.9 %all-to-all-start = ((f32[32,8,128]{2,1,0:T(8,128)}), f32[32,8,128]{2,1,0:T(8,128)S(1)}, u32[]{:S(2)}, u32[]{:S(2)}) async-start(f32[32,8,128]{2,1,0:T(8,128)} %bitcast.106), calls=%async_computation | async-start | bytes 262144 | tf_op jit(solution)/shard_map/while/body/eval_jaxpr/all_to_all | solution.py:109
  108.7 3.2 %factor.3 = f32[64,64]{1,0:T(8,128)S(1)} custom-call(f32[64,64]{1,0:T(8,128)} %pad_maximum_fusion.8.gram_ref), custom_call_target="tpu_custom_call" | custom-call | flops 16777216 | bytes 16777216 | tf_op jit(solution)/shard_map/while/body/eval_jaxpr/factor/pallas_call | solution.py:82
  111.9 7.3 %all-to-all-done = f32[32,8,128]{2,1,0:T(8,128)S(1)} async-done(((f32[32,8,128]{2,1,0:T(8,128)}), f32[32,8,128]{2,1,0:T(8,128)S(1)}, u32[]{:S(2)}, u32[]{:S(2)}) %all-to-all-start) | async-done | bytes 131104 | tf_op jit(solution)/shard_map/while/body/eval_jaxpr/all_to_all | solution.py:109
  119.8 3.9 %all-to-all-start.1 = ((f32[32,8,128]{2,1,0:T(8,128)}), f32[32,8,128]{2,1,0:T(8,128)S(1)}, u32[]{:S(2)}, u32[]{:S(2)}) async-start(f32[32,8,128]{2,1,0:T(8,128)} %broadcast_in_dim.22), calls=%async_computation.1 | async-start | bytes 262144 | tf_op jit(solution)/shard_map/while/body/eval_jaxpr/all_to_all | solution.py:110
  124.2 9.9 %all-to-all-done.1 = f32[32,8,128]{2,1,0:T(8,128)S(1)} async-done(((f32[32,8,128]{2,1,0:T(8,128)}), f32[32,8,128]{2,1,0:T(8,128)S(1)}, u32[]{:S(2)}, u32[]{:S(2)}) %all-to-all-start.1) | async-done | bytes 131104 | tf_op jit(solution)/shard_map/while/body/eval_jaxpr/all_to_all | solution.py:110
  140.5 2.3 collective-permute-done.3
  146.9 3.9 %all-to-all-start = ((f32[32,8,128]{2,1,0:T(8,128)}), f32[32,8,128]{2,1,0:T(8,128)S(1)}, u32[]{:S(2)}, u32[]{:S(2)}) async-start(f32[32,8,128]{2,1,0:T(8,128)} %bitcast.106), calls=%async_computation | async-start | bytes 262144 | tf_op jit(solution)/shard_map/while/body/eval_jaxpr/all_to_all | solution.py:109
  151.5 3.2 %factor.3 = f32[64,64]{1,0:T(8,128)S(1)} custom-call(f32[64,64]{1,0:T(8,128)} %pad_maximum_fusion.8.gram_ref), custom_call_target="tpu_custom_call" | custom-call | flops 16777216 | bytes 16777216 | tf_op jit(solution)/shard_map/while/body/eval_jaxpr/factor/pallas_call | solution.py:82
  154.7 7.3 %all-to-all-done = f32[32,8,128]{2,1,0:T(8,128)S(1)} async-done(((f32[32,8,128]{2,1,0:T(8,128)}), f32[32,8,128]{2,1,0:T(8,128)S(1)}, u32[]{:S(2)}, u32[]{:S(2)}) %all-to-all-start) | async-done | bytes 131104 | tf_op jit(solution)/shard_map/while/body/eval_jaxpr/all_to_all | solution.py:109
  162.7 3.9 %all-to-all-start.1 = ((f32[32,8,128]{2,1,0:T(8,128)}), f32[32,8,128]{2,1,0:T(8,128)S(1)}, u32[]{:S(2)}, u32[]{:S(2)}) async-start(f32[32,8,128]{2,1,0:T(8,128)} %broadcast_in_dim.22), calls=%async_computation.1 | async-start | bytes 262144 | tf_op jit(solution)/shard_map/while/body/eval_jaxpr/all_to_all | solution.py:110
  167.1 9.9 %all-to-all-done.1 = f32[32,8,128]{2,1,0:T(8,128)S(1)} async-done(((f32[32,8,128]{2,1,0:T(8,128)}), f32[32,8,128]{2,1,0:T(8,128)S(1)}, u32[]{:S(2)}, u32[]{:S(2)}) %all-to-all-start.1) | async-done | bytes 131104 | tf_op jit(solution)/shard_map/while/body/eval_jaxpr/all_to_all | solution.py:110
  189.7 3.9 %all-to-all-start = ((f32[32,8,128]{2,1,0:T(8,128)}), f32[32,8,128]{2,1,0:T(8,128)S(1)}, u32[]{:S(2)}, u32[]{:S(2)}) async-start(f32[32,8,128]{2,1,0:T(8,128)} %bitcast.106), calls=%async_computation | async-start | bytes 262144 | tf_op jit(solution)/shard_map/while/body/eval_jaxpr/all_to_all | solution.py:109
  194.4 3.2 %factor.3 = f32[64,64]{1,0:T(8,128)S(1)} custom-call(f32[64,64]{1,0:T(8,128)} %pad_maximum_fusion.8.gram_ref), custom_call_target="tpu_custom_call" | custom-call | flops 16777216 | bytes 16777216 | tf_op jit(solution)/shard_map/while/body/eval_jaxpr/factor/pallas_call | solution.py:82
  197.6 7.3 %all-to-all-done = f32[32,8,128]{2,1,0:T(8,128)S(1)} async-done(((f32[32,8,128]{2,1,0:T(8,128)}), f32[32,8,128]{2,1,0:T(8,128)S(1)}, u32[]{:S(2)}, u32[]{:S(2)}) %all-to-all-start) | async-done | bytes 131104 | tf_op jit(solution)/shard_map/while/body/eval_jaxpr/all_to_all | solution.py:109
  205.5 3.9 %all-to-all-start.1 = ((f32[32,8,128]{2,1,0:T(8,128)}), f32[32,8,128]{2,1,0:T(8,128)S(1)}, u32[]{:S(2)}, u32[]{:S(2)}) async-start(f32[32,8,128]{2,1,0:T(8,128)} %broadcast_in_dim.22), calls=%async_computation.1 | async-start | bytes 262144 | tf_op jit(solution)/shard_map/while/body/eval_jaxpr/all_to_all | solution.py:110
  209.9 9.9 %all-to-all-done.1 = f32[32,8,128]{2,1,0:T(8,128)S(1)} async-done(((f32[32,8,128]{2,1,0:T(8,128)}), f32[32,8,128]{2,1,0:T(8,128)S(1)}, u32[]{:S(2)}, u32[]{:S(2)}) %all-to-all-start.1) | async-done | bytes 131104 | tf_op jit(solution)/shard_map/while/body/eval_jaxpr/all_to_all | solution.py:110
  220.1 3.0 %collective-permute-start.22 = (f32[64,512]{1,0:T(8,128)S(1)}, f32[64,512]{1,0:T(8,128)S(1)}, u32[]{:S(2)}, u32[]{:S(2)}) collective-permute-start(f32[64,512]{1,0:T(8,128)S(1)} %get-tuple-element.138.refs_4_), channel_id=1, source_target_pairs={{0,192},{64,0},{128,64},{192,128},{1,193},{65,1},{129,65},{193,129... | collective-permute-start | bytes 393224 | tf_op jit(solution)/shard_map/ppermute | solution.py:30
  223.1 2.5 %collective-permute-start.20 = (f32[64,512]{1,0:T(8,128)S(1)}, f32[64,512]{1,0:T(8,128)S(1)}, u32[]{:S(2)}, u32[]{:S(2)}) collective-permute-start(f32[64,512]{1,0:T(8,128)S(1)} %get-tuple-element.138.refs_4_), channel_id=1, source_target_pairs={{0,64},{64,128},{128,192},{192,0},{1,65},{65,129},{129,193},{193,1... | collective-permute-start | bytes 393224 | tf_op jit(solution)/shard_map/ppermute | solution.py:30
  225.6 3.9 %collective-permute-done.21.refs_6_ = f32[64,512]{1,0:T(8,128)S(1)} collective-permute-done((f32[64,512]{1,0:T(8,128)S(1)}, f32[64,512]{1,0:T(8,128)S(1)}, u32[]{:S(2)}, u32[]{:S(2)}) %collective-permute-start.21) | collective-permute-done | bytes 131104 | tf_op jit(solution)/shard_map/ppermute | solution.py:30
  230.2 2.6 %collective-permute-start.19 = (f32[64,64]{1,0:T(8,128)S(1)}, f32[64,64]{1,0:T(8,128)S(1)}, u32[]{:S(2)}, u32[]{:S(2)}) collective-permute-start(f32[64,64]{1,0:T(8,128)S(1)} %convolution_add_fusion.2.refs_0_), channel_id=1, source_target_pairs={{0,192},{64,0},{128,64},{192,128},{1,193},{65,1},{129,65},{193,129... | collective-permute-start | bytes 49160 | tf_op jit(solution)/shard_map/ppermute | solution.py:30
  235.0 3.3 %collective-permute-done.18.refs_2_ = f32[64,64]{1,0:T(8,128)S(1)} collective-permute-done((f32[64,64]{1,0:T(8,128)S(1)}, f32[64,64]{1,0:T(8,128)S(1)}, u32[]{:S(2)}, u32[]{:S(2)}) %collective-permute-start.18) | collective-permute-done | bytes 16416 | tf_op jit(solution)/shard_map/ppermute | solution.py:30
  239.1 8.9 %finish.1 = (bf16[224,4096]{1,0:T(8,128)(2,1)}, f32[56,4096]{1,0:T(8,128)}, f32[56,4096]{1,0:T(8,128)}) custom-call(s32[1]{0:T(128)} %bitcast.8.me_ref, s32[1]{0:T(128)} %bitcast.9.core_ref, f32[64,64]{1,0:T(8,128)} %copy-done.13, f32[64,64]{1,0:T(8,128)} %copy-done.16, f32[64,64]{1,0:T(8,128)} %copy-done.15, f32[64,64]{1,0:T(8,128)} %copy-done.14, ...), custom_call_target="tpu_custom_call" | custom-call | tf_op jit(solution)/shard_map/finish/pallas_call | solution.py:208
  (187 shorter events, 73.7 us)
Async XLA Ops:
  5.9 12.0 %collective-permute-start.7 = (f32[64,224]{1,0:T(8,128)S(1)}, f32[64,224]{1,0:T(8,128)S(1)}, u32[]{:S(2)}, u32[]{:S(2)}) collective-permute-start(f32[64,224]{1,0:T(8,128)S(1)} %slice_add_fusion.6), channel_id=1, source_target_pairs={{0,64},{64,128},{128,192},{192,0},{1,65},{65,129},{129,193},{193,1... | collective-permute-start | bytes 172040 | tf_op jit(solution)/shard_map/ppermute | solution.py:30
  7.5 13.7 %collective-permute-start.8 = (f32[64,224]{1,0:T(8,128)S(1)}, f32[64,224]{1,0:T(8,128)S(1)}, u32[]{:S(2)}, u32[]{:S(2)}) collective-permute-start(f32[64,224]{1,0:T(8,128)S(1)} %slice_add_fusion.6), channel_id=1, source_target_pairs={{0,192},{64,0},{128,64},{192,128},{1,193},{65,1},{129,65},{193,129... | collective-permute-start | bytes 172040 | tf_op jit(solution)/shard_map/ppermute | solution.py:30
  10.4 28.0 %collective-permute-start.10 = (f32[112,1024]{1,0:T(8,128)}, f32[112,1024]{1,0:T(8,128)S(1)}, u32[]{:S(2)}, u32[]{:S(2)}) collective-permute-start(f32[112,1024]{1,0:T(8,128)} %get-tuple-element.130), channel_id=1, source_target_pairs={{0,64},{64,128},{128,192},{192,0},{1,65},{65,129},{129,193},{193,1... | collective-permute-start | bytes 1376264 | tf_op jit(solution)/shard_map/ppermute | solution.py:257
  13.7 23.5 %collective-permute-start.9 = (f32[112,1024]{1,0:T(8,128)}, f32[112,1024]{1,0:T(8,128)S(1)}, u32[]{:S(2)}, u32[]{:S(2)}) collective-permute-start(f32[112,1024]{1,0:T(8,128)} %get-tuple-element.128), channel_id=1, source_target_pairs={{0,192},{64,0},{128,64},{192,128},{1,193},{65,1},{129,65},{193,129... | collective-permute-start | bytes 1376264 | tf_op jit(solution)/shard_map/ppermute | solution.py:257
  17.9 20.6 %collective-permute-start.11 = (f32[112,1024]{1,0:T(8,128)}, f32[112,1024]{1,0:T(8,128)}, u32[]{:S(2)}, u32[]{:S(2)}) collective-permute-start(f32[112,1024]{1,0:T(8,128)} %get-tuple-element.132), channel_id=1, source_target_pairs={{0,64},{64,128},{128,192},{192,0},{1,65},{65,129},{129,193},{193,1... | collective-permute-start | bytes 1376264 | tf_op jit(solution)/shard_map/ppermute | solution.py:257
  17.9 21.8 %collective-permute-start.13 = (f32[112,1024]{1,0:T(8,128)}, f32[112,1024]{1,0:T(8,128)}, u32[]{:S(2)}, u32[]{:S(2)}) collective-permute-start(f32[112,1024]{1,0:T(8,128)} %get-tuple-element.134), channel_id=1, source_target_pairs={{0,192},{64,0},{128,64},{192,128},{1,193},{65,1},{129,65},{193,129... | collective-permute-start | bytes 1376264 | tf_op jit(solution)/shard_map/ppermute | solution.py:257
  21.2 16.0 %collective-permute-start.6 = (f32[64,224]{1,0:T(8,128)S(1)}, f32[64,224]{1,0:T(8,128)S(1)}, u32[]{:S(2)}, u32[]{:S(2)}) collective-permute-start(f32[64,224]{1,0:T(8,128)S(1)} %slice_add_fusion.6), channel_id=1, source_target_pairs={{0,128},{64,192},{128,0},{192,64},{1,129},{65,193},{129,1},{193,65... | collective-permute-start | bytes 172040 | tf_op jit(solution)/shard_map/ppermute | solution.py:30
  39.6 9.0 %collective-permute-start.12 = (f32[112,1024]{1,0:T(8,128)S(1)}, f32[112,1024]{1,0:T(8,128)S(1)}, u32[]{:S(2)}, u32[]{:S(2)}) collective-permute-start(f32[112,1024]{1,0:T(8,128)S(1)} %add.128), channel_id=1, source_target_pairs={{0,64},{64,128},{128,192},{192,0},{1,65},{65,129},{129,193},{193,1... | collective-permute-start | bytes 1376264 | tf_op jit(solution)/shard_map/ppermute | solution.py:257
  40.8 9.0 %collective-permute-start.14 = (f32[112,1024]{1,0:T(8,128)S(1)}, f32[112,1024]{1,0:T(8,128)S(1)}, u32[]{:S(2)}, u32[]{:S(2)}) collective-permute-start(f32[112,1024]{1,0:T(8,128)S(1)} %add.130), channel_id=1, source_target_pairs={{0,192},{64,0},{128,64},{192,128},{1,193},{65,1},{129,65},{193,129... | collective-permute-start | bytes 1376264 | tf_op jit(solution)/shard_map/ppermute | solution.py:257
  52.2 23.5 %all-to-all-start.2 = ((f32[32,8,128]{2,1,0:T(8,128)}), f32[32,8,128]{2,1,0:T(8,128)S(1)}, u32[]{:S(2)}, u32[]{:S(2)}) async-start(f32[32,8,128]{2,1,0:T(8,128)} %bitcast.18), calls=%async_computation.2 | async-start | bytes 262144 | tf_op jit(solution)/shard_map/all_to_all | solution.py:109
  76.4 14.5 %all-to-all-start.3 = ((f32[32,8,128]{2,1,0:T(8,128)}), f32[32,8,128]{2,1,0:T(8,128)S(1)}, u32[]{:S(2)}, u32[]{:S(2)}) async-start(f32[32,8,128]{2,1,0:T(8,128)} %broadcast_in_dim.17), calls=%async_computation.3 | async-start | bytes 262144 | tf_op jit(solution)/shard_map/all_to_all | solution.py:110
  93.1 6.5 %collective-permute-start.3 = (f32[64,256]{1,0:T(8,128)S(1)}, f32[64,256]{1,0:T(8,128)S(1)}, u32[]{:S(2)}, u32[]{:S(2)}) collective-permute-start(f32[64,256]{1,0:T(8,128)S(1)} %pad_maximum_fusion.7), channel_id=1, source_target_pairs={{0,128},{64,192},{128,0},{192,64},{1,129},{65,193},{129,1},{193,65... | collective-permute-start | bytes 196616 | tf_op jit(solution)/shard_map/while/body/eval_jaxpr/ppermute | solution.py:30
  101.3 6.6 %collective-permute-start.4 = (f32[64,32]{1,0:T(8,128)S(1)}, f32[64,32]{1,0:T(8,128)S(1)}, u32[]{:S(2)}, u32[]{:S(2)}) collective-permute-start(f32[64,32]{1,0:T(8,128)S(1)} %slice.173), channel_id=1, source_target_pairs={{0,1},{1,0},{2,3},{3,2},{4,5},{5,4},{6,7},{7,6},{8,9},{9,8},{10,11... | collective-permute-start | bytes 24584 | tf_op jit(solution)/shard_map/while/body/eval_jaxpr/ppermute | solution.py:103
  104.0 15.1 %all-to-all-start = ((f32[32,8,128]{2,1,0:T(8,128)}), f32[32,8,128]{2,1,0:T(8,128)S(1)}, u32[]{:S(2)}, u32[]{:S(2)}) async-start(f32[32,8,128]{2,1,0:T(8,128)} %bitcast.106), calls=%async_computation | async-start | bytes 262144 | tf_op jit(solution)/shard_map/while/body/eval_jaxpr/all_to_all | solution.py:109
  119.8 14.3 %all-to-all-start.1 = ((f32[32,8,128]{2,1,0:T(8,128)}), f32[32,8,128]{2,1,0:T(8,128)S(1)}, u32[]{:S(2)}, u32[]{:S(2)}) async-start(f32[32,8,128]{2,1,0:T(8,128)} %broadcast_in_dim.22), calls=%async_computation.1 | async-start | bytes 262144 | tf_op jit(solution)/shard_map/while/body/eval_jaxpr/all_to_all | solution.py:110
  136.7 6.1 %collective-permute-start.3 = (f32[64,256]{1,0:T(8,128)S(1)}, f32[64,256]{1,0:T(8,128)S(1)}, u32[]{:S(2)}, u32[]{:S(2)}) collective-permute-start(f32[64,256]{1,0:T(8,128)S(1)} %pad_maximum_fusion.7), channel_id=1, source_target_pairs={{0,128},{64,192},{128,0},{192,64},{1,129},{65,193},{129,1},{193,65... | collective-permute-start | bytes 196616 | tf_op jit(solution)/shard_map/while/body/eval_jaxpr/ppermute | solution.py:30
  138.4 5.4 %collective-permute-start.2 = (f32[64,256]{1,0:T(8,128)S(1)}, f32[64,256]{1,0:T(8,128)S(1)}, u32[]{:S(2)}, u32[]{:S(2)}) collective-permute-start(f32[64,256]{1,0:T(8,128)S(1)} %pad_maximum_fusion.7), channel_id=1, source_target_pairs={{0,192},{64,0},{128,64},{192,128},{1,193},{65,1},{129,65},{193,129... | collective-permute-start | bytes 196616 | tf_op jit(solution)/shard_map/while/body/eval_jaxpr/ppermute | solution.py:30
  144.2 6.6 %collective-permute-start.4 = (f32[64,32]{1,0:T(8,128)S(1)}, f32[64,32]{1,0:T(8,128)S(1)}, u32[]{:S(2)}, u32[]{:S(2)}) collective-permute-start(f32[64,32]{1,0:T(8,128)S(1)} %slice.173), channel_id=1, source_target_pairs={{0,1},{1,0},{2,3},{3,2},{4,5},{5,4},{6,7},{7,6},{8,9},{9,8},{10,11... | collective-permute-start | bytes 24584 | tf_op jit(solution)/shard_map/while/body/eval_jaxpr/ppermute | solution.py:103
  146.9 15.1 %all-to-all-start = ((f32[32,8,128]{2,1,0:T(8,128)}), f32[32,8,128]{2,1,0:T(8,128)S(1)}, u32[]{:S(2)}, u32[]{:S(2)}) async-start(f32[32,8,128]{2,1,0:T(8,128)} %bitcast.106), calls=%async_computation | async-start | bytes 262144 | tf_op jit(solution)/shard_map/while/body/eval_jaxpr/all_to_all | solution.py:109
  162.7 14.3 %all-to-all-start.1 = ((f32[32,8,128]{2,1,0:T(8,128)}), f32[32,8,128]{2,1,0:T(8,128)S(1)}, u32[]{:S(2)}, u32[]{:S(2)}) async-start(f32[32,8,128]{2,1,0:T(8,128)} %broadcast_in_dim.22), calls=%async_computation.1 | async-start | bytes 262144 | tf_op jit(solution)/shard_map/while/body/eval_jaxpr/all_to_all | solution.py:110
  179.6 5.9 %collective-permute-start.3 = (f32[64,256]{1,0:T(8,128)S(1)}, f32[64,256]{1,0:T(8,128)S(1)}, u32[]{:S(2)}, u32[]{:S(2)}) collective-permute-start(f32[64,256]{1,0:T(8,128)S(1)} %pad_maximum_fusion.7), channel_id=1, source_target_pairs={{0,128},{64,192},{128,0},{192,64},{1,129},{65,193},{129,1},{193,65... | collective-permute-start | bytes 196616 | tf_op jit(solution)/shard_map/while/body/eval_jaxpr/ppermute | solution.py:30
  181.7 5.1 %collective-permute-start.2 = (f32[64,256]{1,0:T(8,128)S(1)}, f32[64,256]{1,0:T(8,128)S(1)}, u32[]{:S(2)}, u32[]{:S(2)}) collective-permute-start(f32[64,256]{1,0:T(8,128)S(1)} %pad_maximum_fusion.7), channel_id=1, source_target_pairs={{0,192},{64,0},{128,64},{192,128},{1,193},{65,1},{129,65},{193,129... | collective-permute-start | bytes 196616 | tf_op jit(solution)/shard_map/while/body/eval_jaxpr/ppermute | solution.py:30
  187.0 6.6 %collective-permute-start.4 = (f32[64,32]{1,0:T(8,128)S(1)}, f32[64,32]{1,0:T(8,128)S(1)}, u32[]{:S(2)}, u32[]{:S(2)}) collective-permute-start(f32[64,32]{1,0:T(8,128)S(1)} %slice.173), channel_id=1, source_target_pairs={{0,1},{1,0},{2,3},{3,2},{4,5},{5,4},{6,7},{7,6},{8,9},{9,8},{10,11... | collective-permute-start | bytes 24584 | tf_op jit(solution)/shard_map/while/body/eval_jaxpr/ppermute | solution.py:103
  189.7 15.1 %all-to-all-start = ((f32[32,8,128]{2,1,0:T(8,128)}), f32[32,8,128]{2,1,0:T(8,128)S(1)}, u32[]{:S(2)}, u32[]{:S(2)}) async-start(f32[32,8,128]{2,1,0:T(8,128)} %bitcast.106), calls=%async_computation | async-start | bytes 262144 | tf_op jit(solution)/shard_map/while/body/eval_jaxpr/all_to_all | solution.py:109
  205.5 14.3 %all-to-all-start.1 = ((f32[32,8,128]{2,1,0:T(8,128)}), f32[32,8,128]{2,1,0:T(8,128)S(1)}, u32[]{:S(2)}, u32[]{:S(2)}) async-start(f32[32,8,128]{2,1,0:T(8,128)} %broadcast_in_dim.22), calls=%async_computation.1 | async-start | bytes 262144 | tf_op jit(solution)/shard_map/while/body/eval_jaxpr/all_to_all | solution.py:110
  220.1 5.5 %collective-permute-start.22 = (f32[64,512]{1,0:T(8,128)S(1)}, f32[64,512]{1,0:T(8,128)S(1)}, u32[]{:S(2)}, u32[]{:S(2)}) collective-permute-start(f32[64,512]{1,0:T(8,128)S(1)} %get-tuple-element.138.refs_4_), channel_id=1, source_target_pairs={{0,192},{64,0},{128,64},{192,128},{1,193},{65,1},{129,65},{193,129... | collective-permute-start | bytes 393224 | tf_op jit(solution)/shard_map/ppermute | solution.py:30
  223.1 6.5 %collective-permute-start.21 = (f32[64,512]{1,0:T(8,128)S(1)}, f32[64,512]{1,0:T(8,128)S(1)}, u32[]{:S(2)}, u32[]{:S(2)}) collective-permute-start(f32[64,512]{1,0:T(8,128)S(1)} %get-tuple-element.138.refs_4_), channel_id=1, source_target_pairs={{0,128},{64,192},{128,0},{192,64},{1,129},{65,193},{129,1},{193,65... | collective-permute-start | bytes 393224 | tf_op jit(solution)/shard_map/ppermute | solution.py:30
  223.1 6.4 %collective-permute-start.20 = (f32[64,512]{1,0:T(8,128)S(1)}, f32[64,512]{1,0:T(8,128)S(1)}, u32[]{:S(2)}, u32[]{:S(2)}) collective-permute-start(f32[64,512]{1,0:T(8,128)S(1)} %get-tuple-element.138.refs_4_), channel_id=1, source_target_pairs={{0,64},{64,128},{128,192},{192,0},{1,65},{65,129},{129,193},{193,1... | collective-permute-start | bytes 393224 | tf_op jit(solution)/shard_map/ppermute | solution.py:30
  229.6 8.7 %collective-permute-start.23 = (f32[3,64,512]{2,1,0:T(8,128)S(1)}, f32[3,64,512]{2,1,0:T(8,128)S(1)}, u32[]{:S(2)}, u32[]{:S(2)}) collective-permute-start(f32[3,64,512]{2,1,0:T(8,128)S(1)} %pad_maximum_fusion.4), channel_id=1, source_target_pairs={{0,1},{1,0},{2,3},{3,2},{4,5},{5,4},{6,7},{7,6},{8,9},{9,8},{10,11... | collective-permute-start | bytes 1179656 | tf_op jit(solution)/shard_map/ppermute | solution.py:103
  230.2 4.7 %collective-permute-start.19 = (f32[64,64]{1,0:T(8,128)S(1)}, f32[64,64]{1,0:T(8,128)S(1)}, u32[]{:S(2)}, u32[]{:S(2)}) collective-permute-start(f32[64,64]{1,0:T(8,128)S(1)} %convolution_add_fusion.2.refs_0_), channel_id=1, source_target_pairs={{0,192},{64,0},{128,64},{192,128},{1,193},{65,1},{129,65},{193,129... | collective-permute-start | bytes 49160 | tf_op jit(solution)/shard_map/ppermute | solution.py:30
  232.8 5.4 %collective-permute-start.18 = (f32[64,64]{1,0:T(8,128)S(1)}, f32[64,64]{1,0:T(8,128)S(1)}, u32[]{:S(2)}, u32[]{:S(2)}) collective-permute-start(f32[64,64]{1,0:T(8,128)S(1)} %convolution_add_fusion.2.refs_0_), channel_id=1, source_target_pairs={{0,128},{64,192},{128,0},{192,64},{1,129},{65,193},{129,1},{193,65... | collective-permute-start | bytes 49160 | tf_op jit(solution)/shard_map/ppermute | solution.py:30
  232.8 5.4 %collective-permute-start.17 = (f32[64,64]{1,0:T(8,128)S(1)}, f32[64,64]{1,0:T(8,128)S(1)}, u32[]{:S(2)}, u32[]{:S(2)}) collective-permute-start(f32[64,64]{1,0:T(8,128)S(1)} %convolution_add_fusion.2.refs_0_), channel_id=1, source_target_pairs={{0,64},{64,128},{128,192},{192,0},{1,65},{65,129},{129,193},{193,1... | collective-permute-start | bytes 49160 | tf_op jit(solution)/shard_map/ppermute | solution.py:30
  (33 other events, 287.7 us)

commit v3 on v2

--- a/solution.py
+++ b/solution.py
@@ -237,18 +237,19 @@
     )
 
 
-def start_sketch(basis, combined):
-    rank = basis.shape[1]
+def split_basis(basis):
     rest, pieces = basis, []
     for _ in range(3):
         piece = lax.reduce_precision(rest, exponent_bits=8, mantissa_bits=7)
         pieces.append(piece.astype(jnp.bfloat16))
         rest = rest - piece
+    return jnp.concatenate(pieces, axis=1)
+
+
+def start_sketch(pieces, combined):
+    rank = pieces.shape[1] // 3
     wide = lax.dot_general(
-        jnp.concatenate(pieces, axis=1),
-        combined,
-        (((0,), (1,)), ((), ())),
-        preferred_element_type=jnp.float32,
+        pieces, combined, (((0,), (1,)), ((), ())), preferred_element_type=jnp.float32
     )
     return wide[2 * rank :] + wide[rank : 2 * rank] + wide[:rank]
 
@@ -276,17 +277,20 @@
     relay_down = hop(blocks[2][1], down)
     from_below = hop(blocks[1][1], up)
     from_above = hop(blocks[3][0], down)
-    top_below = hop(blocks[1][0] + relay_up, up)
-    bottom_above = hop(blocks[3][1] + relay_down, down)
     both = grad.astype(jnp.float32) + buffer.astype(jnp.float32)
     combined = lax.reduce_precision(both, exponent_bits=8, mantissa_bits=7)
-    combined = lax.optimization_barrier(combined.astype(jnp.bfloat16))
-    part = start_sketch(basis_init, combined)
+    hold = lax.optimization_barrier
+    combined = hold(combined.astype(jnp.bfloat16))
+    pieces, up_sum, down_sum = hold(
+        (split_basis(basis_init), blocks[1][0] + relay_up, blocks[3][1] + relay_down)
+    )
+    top_below = hop(up_sum, up)
+    bottom_above = hop(down_sum, down)
+    part = start_sketch(pieces, combined)
     image = island_sum(part)
     basis = lax.dynamic_slice_in_dim(basis_init, me * width, width, 0)
     basis = jnp.where(core == 0, basis, jnp.roll(basis, half, axis=0)).T
     side = rank // 2
-    hold = lax.optimization_barrier
 
     top = hold(blocks[0][0] + from_above)
     bottom = hold(blocks[0][1] + from_below)

time: 250 us -> 250 us (level)
  other arithmetic: 13.1 us -> 16 us
  starting transfers between devices: 78.6 us -> 75.7 us
    ppermute x6, waiting for transfers between devices: 5.79 us -> 17.9 us  [hop(): return lax.ppermute(v, 'x', pairs)]
    ppermute x18, waiting for transfers between devices: 28.7 us -> 16.9 us  [island_parts(): return [v] + [lax.ppermute(v, 'x', ring(4, s)) for s in (1, 2, 3)]]
  transfers between devices with their start and end apart: 44 -> 44, of which waited for: 29 -> 29; matrix products, arithmetic and copies ran while one was open for 7% -> 10% of each run, Pallas kernels for 7% -> 6%
where the time goes in v3:
time: 250 us; the launch traced here: 248 us
  waiting for transfers between devices  111 us (44%)
  starting transfers between devices  75.7 us (30%)
  Pallas kernels  27 us (11%)
  other arithmetic  16 us (6%)
  matrix products  12.9 us (5%)
  local copies, waits for them, and re-layouts  3.71 us (1%)
    all_to_all x4, waiting for transfers between devices, row_sum(): full = lax.all_to_all(jnp.broadcast_to(own, parts.shape), ROW, 0, 0)  39.9 us
    all_to_all x4, waiting for transfers between devices, row_sum(): own = jnp.sum(lax.all_to_all(parts, ROW, 0, 0), axis=0)  32.3 us
    ppermute x18, starting transfers between devices, island_parts(): return [v] + [lax.ppermute(v, 'x', ring(4, s)) for s in (1, 2, 3)]  28.4 us
    all_to_all x4, starting transfers between devices, row_sum(): own = jnp.sum(lax.all_to_all(parts, ROW, 0, 0), axis=0)  23.1 us
    ppermute x6, waiting for transfers between devices, hop(): return lax.ppermute(v, 'x', pairs)  17.9 us
    ppermute x18, waiting for transfers between devices, island_parts(): return [v] + [lax.ppermute(v, 'x', ring(4, s)) for s in (1, 2, 3)]  16.9 us
    all_to_all x4, starting transfers between devices, row_sum(): full = lax.all_to_all(jnp.broadcast_to(own, parts.shape), ROW, 0, 0)  15.6 us
    dot_general x35, matrix products, dot(): lax.dot_general(a, b, (((ca,), (cb,)), ((), ())), precision=lax.Precision...  12.1 us
  transfers between devices with their start and end apart: 44, of which 29 were waited for; matrix products, arithmetic and copies ran while one was open for 10% of the time, Pallas kernels for 6%

profile of v3, /device:TPU:2, one launch (start us, length us, event | category | flops | bytes accessed | tf_op | source)
XLA Modules:
  0.0 247.7 jit_solution(1136812728047914024)
XLA Ops:
  11.4 3.5 %reduce-precision_convert_fusion.refs_12_ = bf16[224,4096]{1,0:T(8,128)(2,1)} fusion(bf16[1,224,4096]{2,1,0:T(8,128)(2,1)} %param.8, bf16[1,224,4096]{2,1,0:T(8,128)(2,1)S(1)} %copy-done), kind=kLoop, calls=%fused_computation.13 | loop fusion | flops 4587520 | bytes 5505024 | tf_op jit(solution)/shard_map/convert_element_type | solution.py:283
  15.4 9.8 %collective-permute-done.7 = f32[112,1024]{1,0:T(8,128)} collective-permute-done((f32[112,1024]{1,0:T(8,128)}, f32[112,1024]{1,0:T(8,128)}, u32[]{:S(2)}, u32[]{:S(2)}) %collective-permute-start.7) | collective-permute-done | bytes 458784 | tf_op jit(solution)/shard_map/ppermute | solution.py:258
  30.8 3.3 %collective-permute-start.8 = (f32[64,224]{1,0:T(8,128)S(1)}, f32[64,224]{1,0:T(8,128)S(1)}, u32[]{:S(2)}, u32[]{:S(2)}) collective-permute-start(f32[64,224]{1,0:T(8,128)S(1)} %slice_add_fusion.6), channel_id=1, source_target_pairs={{0,128},{64,192},{128,0},{192,64},{1,129},{65,193},{129,1},{193,65... | collective-permute-start | bytes 172040 | tf_op jit(solution)/shard_map/ppermute | solution.py:30
  42.8 7.6 %collective-permute-done.13 = f32[112,1024]{1,0:T(8,128)S(1)} collective-permute-done((f32[112,1024]{1,0:T(8,128)S(1)}, f32[112,1024]{1,0:T(8,128)S(1)}, u32[]{:S(2)}, u32[]{:S(2)}) %collective-permute-start.13) | collective-permute-done | bytes 458784 | tf_op jit(solution)/shard_map/ppermute | solution.py:258
  53.6 11.5 %all-to-all-start.2 = ((f32[32,8,128]{2,1,0:T(8,128)}), f32[32,8,128]{2,1,0:T(8,128)S(1)}, u32[]{:S(2)}, u32[]{:S(2)}) async-start(f32[32,8,128]{2,1,0:T(8,128)} %bitcast.18), calls=%async_computation.2 | async-start | bytes 262144 | tf_op jit(solution)/shard_map/all_to_all | solution.py:109
  65.2 10.5 %all-to-all-done.2 = f32[32,8,128]{2,1,0:T(8,128)S(1)} async-done(((f32[32,8,128]{2,1,0:T(8,128)}), f32[32,8,128]{2,1,0:T(8,128)S(1)}, u32[]{:S(2)}, u32[]{:S(2)}) %all-to-all-start.2) | async-done | bytes 131104 | tf_op jit(solution)/shard_map/all_to_all | solution.py:109
  76.4 4.0 %all-to-all-start.3 = ((f32[32,8,128]{2,1,0:T(8,128)}), f32[32,8,128]{2,1,0:T(8,128)S(1)}, u32[]{:S(2)}, u32[]{:S(2)}) async-start(f32[32,8,128]{2,1,0:T(8,128)} %broadcast_in_dim.17), calls=%async_computation.3 | async-start | bytes 262144 | tf_op jit(solution)/shard_map/all_to_all | solution.py:110
  80.6 10.3 %all-to-all-done.3 = f32[32,8,128]{2,1,0:T(8,128)S(1)} async-done(((f32[32,8,128]{2,1,0:T(8,128)}), f32[32,8,128]{2,1,0:T(8,128)S(1)}, u32[]{:S(2)}, u32[]{:S(2)}) %all-to-all-start.3) | async-done | bytes 131104 | tf_op jit(solution)/shard_map/all_to_all | solution.py:110
  90.8 129.5 %while.20 = (s32[]{:T(128)}, f32[64,512]{1,0:T(8,128)S(1)}, f32[64,512]{1,0:T(8,128)S(1)}, f32[64,512]{1,0:T(8,128)S(1)}, f32[64,224]{1,0:T(8,128)}, /*index=5*/...) while((s32[]{:T(128)}, f32[64,512]{1,0:T(8,128)S(1)}, ...), condition=%wide.region_3.4_spmd, body=%wide.region_1.3_spmd.sunk | while | flops 469933056 | bytes 24887784 | solution.py:350
  93.1 3.2 %collective-permute-start.3 = (f32[64,256]{1,0:T(8,128)S(1)}, f32[64,256]{1,0:T(8,128)S(1)}, u32[]{:S(2)}, u32[]{:S(2)}) collective-permute-start(f32[64,256]{1,0:T(8,128)S(1)} %pad_maximum_fusion.8), channel_id=1, source_target_pairs={{0,128},{64,192},{128,0},{192,64},{1,129},{65,193},{129,1},{193,65... | collective-permute-start | bytes 196616 | tf_op jit(solution)/shard_map/while/body/eval_jaxpr/ppermute | solution.py:30
  103.4 3.9 %all-to-all-start = ((f32[32,8,128]{2,1,0:T(8,128)}), f32[32,8,128]{2,1,0:T(8,128)S(1)}, u32[]{:S(2)}, u32[]{:S(2)}) async-start(f32[32,8,128]{2,1,0:T(8,128)} %bitcast.107), calls=%async_computation | async-start | bytes 262144 | tf_op jit(solution)/shard_map/while/body/eval_jaxpr/all_to_all | solution.py:109
  108.1 3.2 %factor.3 = f32[64,64]{1,0:T(8,128)S(1)} custom-call(f32[64,64]{1,0:T(8,128)} %pad_maximum_fusion.9.gram_ref), custom_call_target="tpu_custom_call" | custom-call | flops 16777216 | bytes 16777216 | tf_op jit(solution)/shard_map/while/body/eval_jaxpr/factor/pallas_call | solution.py:82
  111.3 7.3 %all-to-all-done = f32[32,8,128]{2,1,0:T(8,128)S(1)} async-done(((f32[32,8,128]{2,1,0:T(8,128)}), f32[32,8,128]{2,1,0:T(8,128)S(1)}, u32[]{:S(2)}, u32[]{:S(2)}) %all-to-all-start) | async-done | bytes 131104 | tf_op jit(solution)/shard_map/while/body/eval_jaxpr/all_to_all | solution.py:109
  119.2 3.9 %all-to-all-start.1 = ((f32[32,8,128]{2,1,0:T(8,128)}), f32[32,8,128]{2,1,0:T(8,128)S(1)}, u32[]{:S(2)}, u32[]{:S(2)}) async-start(f32[32,8,128]{2,1,0:T(8,128)} %broadcast_in_dim.22), calls=%async_computation.1 | async-start | bytes 262144 | tf_op jit(solution)/shard_map/while/body/eval_jaxpr/all_to_all | solution.py:110
  123.6 9.9 %all-to-all-done.1 = f32[32,8,128]{2,1,0:T(8,128)S(1)} async-done(((f32[32,8,128]{2,1,0:T(8,128)}), f32[32,8,128]{2,1,0:T(8,128)S(1)}, u32[]{:S(2)}, u32[]{:S(2)}) %all-to-all-start.1) | async-done | bytes 131104 | tf_op jit(solution)/shard_map/while/body/eval_jaxpr/all_to_all | solution.py:110
  136.1 2.6 %collective-permute-start.3 = (f32[64,256]{1,0:T(8,128)S(1)}, f32[64,256]{1,0:T(8,128)S(1)}, u32[]{:S(2)}, u32[]{:S(2)}) collective-permute-start(f32[64,256]{1,0:T(8,128)S(1)} %pad_maximum_fusion.8), channel_id=1, source_target_pairs={{0,128},{64,192},{128,0},{192,64},{1,129},{65,193},{129,1},{193,65... | collective-permute-start | bytes 196616 | tf_op jit(solution)/shard_map/while/body/eval_jaxpr/ppermute | solution.py:30
  147.4 3.9 %all-to-all-start = ((f32[32,8,128]{2,1,0:T(8,128)}), f32[32,8,128]{2,1,0:T(8,128)S(1)}, u32[]{:S(2)}, u32[]{:S(2)}) async-start(f32[32,8,128]{2,1,0:T(8,128)} %bitcast.107), calls=%async_computation | async-start | bytes 262144 | tf_op jit(solution)/shard_map/while/body/eval_jaxpr/all_to_all | solution.py:109
  152.0 3.2 %factor.3 = f32[64,64]{1,0:T(8,128)S(1)} custom-call(f32[64,64]{1,0:T(8,128)} %pad_maximum_fusion.9.gram_ref), custom_call_target="tpu_custom_call" | custom-call | flops 16777216 | bytes 16777216 | tf_op jit(solution)/shard_map/while/body/eval_jaxpr/factor/pallas_call | solution.py:82
  155.2 7.3 %all-to-all-done = f32[32,8,128]{2,1,0:T(8,128)S(1)} async-done(((f32[32,8,128]{2,1,0:T(8,128)}), f32[32,8,128]{2,1,0:T(8,128)S(1)}, u32[]{:S(2)}, u32[]{:S(2)}) %all-to-all-start) | async-done | bytes 131104 | tf_op jit(solution)/shard_map/while/body/eval_jaxpr/all_to_all | solution.py:109
  163.2 3.9 %all-to-all-start.1 = ((f32[32,8,128]{2,1,0:T(8,128)}), f32[32,8,128]{2,1,0:T(8,128)S(1)}, u32[]{:S(2)}, u32[]{:S(2)}) async-start(f32[32,8,128]{2,1,0:T(8,128)} %broadcast_in_dim.22), calls=%async_computation.1 | async-start | bytes 262144 | tf_op jit(solution)/shard_map/while/body/eval_jaxpr/all_to_all | solution.py:110
  167.6 9.9 %all-to-all-done.1 = f32[32,8,128]{2,1,0:T(8,128)S(1)} async-done(((f32[32,8,128]{2,1,0:T(8,128)}), f32[32,8,128]{2,1,0:T(8,128)S(1)}, u32[]{:S(2)}, u32[]{:S(2)}) %all-to-all-start.1) | async-done | bytes 131104 | tf_op jit(solution)/shard_map/while/body/eval_jaxpr/all_to_all | solution.py:110
  183.7 2.8 %collective-permute-done.3 = f32[64,256]{1,0:T(8,128)S(1)} collective-permute-done((f32[64,256]{1,0:T(8,128)S(1)}, f32[64,256]{1,0:T(8,128)S(1)}, u32[]{:S(2)}, u32[]{:S(2)}) %collective-permute-start.3) | collective-permute-done | bytes 65568 | tf_op jit(solution)/shard_map/while/body/eval_jaxpr/ppermute | solution.py:30
  190.0 3.9 %all-to-all-start = ((f32[32,8,128]{2,1,0:T(8,128)}), f32[32,8,128]{2,1,0:T(8,128)S(1)}, u32[]{:S(2)}, u32[]{:S(2)}) async-start(f32[32,8,128]{2,1,0:T(8,128)} %bitcast.107), calls=%async_computation | async-start | bytes 262144 | tf_op jit(solution)/shard_map/while/body/eval_jaxpr/all_to_all | solution.py:109
  194.6 3.2 %factor.3 = f32[64,64]{1,0:T(8,128)S(1)} custom-call(f32[64,64]{1,0:T(8,128)} %pad_maximum_fusion.9.gram_ref), custom_call_target="tpu_custom_call" | custom-call | flops 16777216 | bytes 16777216 | tf_op jit(solution)/shard_map/while/body/eval_jaxpr/factor/pallas_call | solution.py:82
  197.8 7.3 %all-to-all-done = f32[32,8,128]{2,1,0:T(8,128)S(1)} async-done(((f32[32,8,128]{2,1,0:T(8,128)}), f32[32,8,128]{2,1,0:T(8,128)S(1)}, u32[]{:S(2)}, u32[]{:S(2)}) %all-to-all-start) | async-done | bytes 131104 | tf_op jit(solution)/shard_map/while/body/eval_jaxpr/all_to_all | solution.py:109
  205.8 3.9 %all-to-all-start.1 = ((f32[32,8,128]{2,1,0:T(8,128)}), f32[32,8,128]{2,1,0:T(8,128)S(1)}, u32[]{:S(2)}, u32[]{:S(2)}) async-start(f32[32,8,128]{2,1,0:T(8,128)} %broadcast_in_dim.22), calls=%async_computation.1 | async-start | bytes 262144 | tf_op jit(solution)/shard_map/while/body/eval_jaxpr/all_to_all | solution.py:110
  210.2 9.9 %all-to-all-done.1 = f32[32,8,128]{2,1,0:T(8,128)S(1)} async-done(((f32[32,8,128]{2,1,0:T(8,128)}), f32[32,8,128]{2,1,0:T(8,128)S(1)}, u32[]{:S(2)}, u32[]{:S(2)}) %all-to-all-start.1) | async-done | bytes 131104 | tf_op jit(solution)/shard_map/while/body/eval_jaxpr/all_to_all | solution.py:110
  220.4 3.2 %collective-permute-start.22 = (f32[64,512]{1,0:T(8,128)S(1)}, f32[64,512]{1,0:T(8,128)S(1)}, u32[]{:S(2)}, u32[]{:S(2)}) collective-permute-start(f32[64,512]{1,0:T(8,128)S(1)} %get-tuple-element.144.refs_4_), channel_id=1, source_target_pairs={{0,192},{64,0},{128,64},{192,128},{1,193},{65,1},{129,65},{193,129... | collective-permute-start | bytes 393224 | tf_op jit(solution)/shard_map/ppermute | solution.py:30
  226.1 3.9 %collective-permute-done.21.refs_6_ = f32[64,512]{1,0:T(8,128)S(1)} collective-permute-done((f32[64,512]{1,0:T(8,128)S(1)}, f32[64,512]{1,0:T(8,128)S(1)}, u32[]{:S(2)}, u32[]{:S(2)}) %collective-permute-start.21) | collective-permute-done | bytes 131104 | tf_op jit(solution)/shard_map/ppermute | solution.py:30
  232.9 2.5 %collective-permute-start.17 = (f32[64,64]{1,0:T(8,128)S(1)}, f32[64,64]{1,0:T(8,128)S(1)}, u32[]{:S(2)}, u32[]{:S(2)}) collective-permute-start(f32[64,64]{1,0:T(8,128)S(1)} %convolution_add_fusion.2.refs_0_), channel_id=1, source_target_pairs={{0,64},{64,128},{128,192},{192,0},{1,65},{65,129},{129,193},{193,1... | collective-permute-start | bytes 49160 | tf_op jit(solution)/shard_map/ppermute | solution.py:30
  235.5 2.5 collective-permute-done.18.refs_2_
  238.7 8.9 %finish.1 = (bf16[224,4096]{1,0:T(8,128)(2,1)}, f32[56,4096]{1,0:T(8,128)}, f32[56,4096]{1,0:T(8,128)}) custom-call(s32[1]{0:T(128)} %bitcast.8.me_ref, s32[1]{0:T(128)} %bitcast.9.core_ref, f32[64,64]{1,0:T(8,128)} %copy-done.14, f32[64,64]{1,0:T(8,128)} %copy-done.17, f32[64,64]{1,0:T(8,128)} %copy-done.16, f32[64,64]{1,0:T(8,128)} %copy-done.15, ...), custom_call_target="tpu_custom_call" | custom-call | tf_op jit(solution)/shard_map/finish/pallas_call | solution.py:208
  (190 shorter events, 72.0 us)
Async XLA Ops:
  2.8 34.4 %collective-permute-start.11 = (f32[112,1024]{1,0:T(8,128)}, f32[112,1024]{1,0:T(8,128)}, u32[]{:S(2)}, u32[]{:S(2)}) collective-permute-start(f32[112,1024]{1,0:T(8,128)} %get-tuple-element.136), channel_id=1, source_target_pairs={{0,192},{64,0},{128,64},{192,128},{1,193},{65,1},{129,65},{193,129... | collective-permute-start | bytes 1376264 | tf_op jit(solution)/shard_map/ppermute | solution.py:258
  7.2 19.9 %collective-permute-start.6 = (f32[112,1024]{1,0:T(8,128)}, f32[112,1024]{1,0:T(8,128)S(1)}, u32[]{:S(2)}, u32[]{:S(2)}) collective-permute-start(f32[112,1024]{1,0:T(8,128)} %get-tuple-element.131), channel_id=1, source_target_pairs={{0,64},{64,128},{128,192},{192,0},{1,65},{65,129},{129,193},{193,1... | collective-permute-start | bytes 1376264 | tf_op jit(solution)/shard_map/ppermute | solution.py:258
  7.2 18.0 %collective-permute-start.7 = (f32[112,1024]{1,0:T(8,128)}, f32[112,1024]{1,0:T(8,128)}, u32[]{:S(2)}, u32[]{:S(2)}) collective-permute-start(f32[112,1024]{1,0:T(8,128)} %get-tuple-element.133), channel_id=1, source_target_pairs={{0,192},{64,0},{128,64},{192,128},{1,193},{65,1},{129,65},{193,129... | collective-permute-start | bytes 1376264 | tf_op jit(solution)/shard_map/ppermute | solution.py:258
  11.4 27.1 %collective-permute-start.12 = (f32[112,1024]{1,0:T(8,128)}, f32[112,1024]{1,0:T(8,128)}, u32[]{:S(2)}, u32[]{:S(2)}) collective-permute-start(f32[112,1024]{1,0:T(8,128)} %get-tuple-element.138), channel_id=1, source_target_pairs={{0,64},{64,128},{128,192},{192,0},{1,65},{65,129},{129,193},{193,1... | collective-permute-start | bytes 1376264 | tf_op jit(solution)/shard_map/ppermute | solution.py:258
  28.7 13.2 %collective-permute-start.9 = (f32[64,224]{1,0:T(8,128)S(1)}, f32[64,224]{1,0:T(8,128)S(1)}, u32[]{:S(2)}, u32[]{:S(2)}) collective-permute-start(f32[64,224]{1,0:T(8,128)S(1)} %slice_add_fusion.6), channel_id=1, source_target_pairs={{0,64},{64,128},{128,192},{192,0},{1,65},{65,129},{129,193},{193,1... | collective-permute-start | bytes 172040 | tf_op jit(solution)/shard_map/ppermute | solution.py:30
  30.2 11.7 %collective-permute-start.10 = (f32[64,224]{1,0:T(8,128)S(1)}, f32[64,224]{1,0:T(8,128)S(1)}, u32[]{:S(2)}, u32[]{:S(2)}) collective-permute-start(f32[64,224]{1,0:T(8,128)S(1)} %slice_add_fusion.6), channel_id=1, source_target_pairs={{0,192},{64,0},{128,64},{192,128},{1,193},{65,1},{129,65},{193,129... | collective-permute-start | bytes 172040 | tf_op jit(solution)/shard_map/ppermute | solution.py:30
  30.8 11.1 %collective-permute-start.8 = (f32[64,224]{1,0:T(8,128)S(1)}, f32[64,224]{1,0:T(8,128)S(1)}, u32[]{:S(2)}, u32[]{:S(2)}) collective-permute-start(f32[64,224]{1,0:T(8,128)S(1)} %slice_add_fusion.6), channel_id=1, source_target_pairs={{0,128},{64,192},{128,0},{192,64},{1,129},{65,193},{129,1},{193,65... | collective-permute-start | bytes 172040 | tf_op jit(solution)/shard_map/ppermute | solution.py:30
  39.8 10.6 %collective-permute-start.13 = (f32[112,1024]{1,0:T(8,128)S(1)}, f32[112,1024]{1,0:T(8,128)S(1)}, u32[]{:S(2)}, u32[]{:S(2)}) collective-permute-start(f32[112,1024]{1,0:T(8,128)S(1)} %copy-done.11), channel_id=1, source_target_pairs={{0,64},{64,128},{128,192},{192,0},{1,65},{65,129},{129,193},{193,1... | collective-permute-start | bytes 1376264 | tf_op jit(solution)/shard_map/ppermute | solution.py:258
  40.6 10.6 %collective-permute-start.14 = (f32[112,1024]{1,0:T(8,128)S(1)}, f32[112,1024]{1,0:T(8,128)S(1)}, u32[]{:S(2)}, u32[]{:S(2)}) collective-permute-start(f32[112,1024]{1,0:T(8,128)S(1)} %copy-done.9), channel_id=1, source_target_pairs={{0,192},{64,0},{128,64},{192,128},{1,193},{65,1},{129,65},{193,129... | collective-permute-start | bytes 1376264 | tf_op jit(solution)/shard_map/ppermute | solution.py:258
  53.6 22.1 %all-to-all-start.2 = ((f32[32,8,128]{2,1,0:T(8,128)}), f32[32,8,128]{2,1,0:T(8,128)S(1)}, u32[]{:S(2)}, u32[]{:S(2)}) async-start(f32[32,8,128]{2,1,0:T(8,128)} %bitcast.18), calls=%async_computation.2 | async-start | bytes 262144 | tf_op jit(solution)/shard_map/all_to_all | solution.py:109
  76.4 14.5 %all-to-all-start.3 = ((f32[32,8,128]{2,1,0:T(8,128)}), f32[32,8,128]{2,1,0:T(8,128)S(1)}, u32[]{:S(2)}, u32[]{:S(2)}) async-start(f32[32,8,128]{2,1,0:T(8,128)} %broadcast_in_dim.17), calls=%async_computation.3 | async-start | bytes 262144 | tf_op jit(solution)/shard_map/all_to_all | solution.py:110
  93.1 6.6 %collective-permute-start.3 = (f32[64,256]{1,0:T(8,128)S(1)}, f32[64,256]{1,0:T(8,128)S(1)}, u32[]{:S(2)}, u32[]{:S(2)}) collective-permute-start(f32[64,256]{1,0:T(8,128)S(1)} %pad_maximum_fusion.8), channel_id=1, source_target_pairs={{0,128},{64,192},{128,0},{192,64},{1,129},{65,193},{129,1},{193,65... | collective-permute-start | bytes 196616 | tf_op jit(solution)/shard_map/while/body/eval_jaxpr/ppermute | solution.py:30
  100.7 6.6 %collective-permute-start.4 = (f32[64,32]{1,0:T(8,128)S(1)}, f32[64,32]{1,0:T(8,128)S(1)}, u32[]{:S(2)}, u32[]{:S(2)}) collective-permute-start(f32[64,32]{1,0:T(8,128)S(1)} %slice.173), channel_id=1, source_target_pairs={{0,1},{1,0},{2,3},{3,2},{4,5},{5,4},{6,7},{7,6},{8,9},{9,8},{10,11... | collective-permute-start | bytes 24584 | tf_op jit(solution)/shard_map/while/body/eval_jaxpr/ppermute | solution.py:103
  103.4 15.1 %all-to-all-start = ((f32[32,8,128]{2,1,0:T(8,128)}), f32[32,8,128]{2,1,0:T(8,128)S(1)}, u32[]{:S(2)}, u32[]{:S(2)}) async-start(f32[32,8,128]{2,1,0:T(8,128)} %bitcast.107), calls=%async_computation | async-start | bytes 262144 | tf_op jit(solution)/shard_map/while/body/eval_jaxpr/all_to_all | solution.py:109
  119.2 14.3 %all-to-all-start.1 = ((f32[32,8,128]{2,1,0:T(8,128)}), f32[32,8,128]{2,1,0:T(8,128)S(1)}, u32[]{:S(2)}, u32[]{:S(2)}) async-start(f32[32,8,128]{2,1,0:T(8,128)} %broadcast_in_dim.22), calls=%async_computation.1 | async-start | bytes 262144 | tf_op jit(solution)/shard_map/while/body/eval_jaxpr/all_to_all | solution.py:110
  136.1 5.9 %collective-permute-start.3 = (f32[64,256]{1,0:T(8,128)S(1)}, f32[64,256]{1,0:T(8,128)S(1)}, u32[]{:S(2)}, u32[]{:S(2)}) collective-permute-start(f32[64,256]{1,0:T(8,128)S(1)} %pad_maximum_fusion.8), channel_id=1, source_target_pairs={{0,128},{64,192},{128,0},{192,64},{1,129},{65,193},{129,1},{193,65... | collective-permute-start | bytes 196616 | tf_op jit(solution)/shard_map/while/body/eval_jaxpr/ppermute | solution.py:30
  144.7 6.6 %collective-permute-start.4 = (f32[64,32]{1,0:T(8,128)S(1)}, f32[64,32]{1,0:T(8,128)S(1)}, u32[]{:S(2)}, u32[]{:S(2)}) collective-permute-start(f32[64,32]{1,0:T(8,128)S(1)} %slice.173), channel_id=1, source_target_pairs={{0,1},{1,0},{2,3},{3,2},{4,5},{5,4},{6,7},{7,6},{8,9},{9,8},{10,11... | collective-permute-start | bytes 24584 | tf_op jit(solution)/shard_map/while/body/eval_jaxpr/ppermute | solution.py:103
  147.4 15.1 %all-to-all-start = ((f32[32,8,128]{2,1,0:T(8,128)}), f32[32,8,128]{2,1,0:T(8,128)S(1)}, u32[]{:S(2)}, u32[]{:S(2)}) async-start(f32[32,8,128]{2,1,0:T(8,128)} %bitcast.107), calls=%async_computation | async-start | bytes 262144 | tf_op jit(solution)/shard_map/while/body/eval_jaxpr/all_to_all | solution.py:109
  163.2 14.3 %all-to-all-start.1 = ((f32[32,8,128]{2,1,0:T(8,128)}), f32[32,8,128]{2,1,0:T(8,128)S(1)}, u32[]{:S(2)}, u32[]{:S(2)}) async-start(f32[32,8,128]{2,1,0:T(8,128)} %broadcast_in_dim.22), calls=%async_computation.1 | async-start | bytes 262144 | tf_op jit(solution)/shard_map/while/body/eval_jaxpr/all_to_all | solution.py:110
  180.1 6.4 %collective-permute-start.3 = (f32[64,256]{1,0:T(8,128)S(1)}, f32[64,256]{1,0:T(8,128)S(1)}, u32[]{:S(2)}, u32[]{:S(2)}) collective-permute-start(f32[64,256]{1,0:T(8,128)S(1)} %pad_maximum_fusion.8), channel_id=1, source_target_pairs={{0,128},{64,192},{128,0},{192,64},{1,129},{65,193},{129,1},{193,65... | collective-permute-start | bytes 196616 | tf_op jit(solution)/shard_map/while/body/eval_jaxpr/ppermute | solution.py:30
  181.6 5.3 %collective-permute-start.2 = (f32[64,256]{1,0:T(8,128)S(1)}, f32[64,256]{1,0:T(8,128)S(1)}, u32[]{:S(2)}, u32[]{:S(2)}) collective-permute-start(f32[64,256]{1,0:T(8,128)S(1)} %pad_maximum_fusion.8), channel_id=1, source_target_pairs={{0,192},{64,0},{128,64},{192,128},{1,193},{65,1},{129,65},{193,129... | collective-permute-start | bytes 196616 | tf_op jit(solution)/shard_map/while/body/eval_jaxpr/ppermute | solution.py:30
  187.3 6.6 %collective-permute-start.4 = (f32[64,32]{1,0:T(8,128)S(1)}, f32[64,32]{1,0:T(8,128)S(1)}, u32[]{:S(2)}, u32[]{:S(2)}) collective-permute-start(f32[64,32]{1,0:T(8,128)S(1)} %slice.173), channel_id=1, source_target_pairs={{0,1},{1,0},{2,3},{3,2},{4,5},{5,4},{6,7},{7,6},{8,9},{9,8},{10,11... | collective-permute-start | bytes 24584 | tf_op jit(solution)/shard_map/while/body/eval_jaxpr/ppermute | solution.py:103
  190.0 15.1 %all-to-all-start = ((f32[32,8,128]{2,1,0:T(8,128)}), f32[32,8,128]{2,1,0:T(8,128)S(1)}, u32[]{:S(2)}, u32[]{:S(2)}) async-start(f32[32,8,128]{2,1,0:T(8,128)} %bitcast.107), calls=%async_computation | async-start | bytes 262144 | tf_op jit(solution)/shard_map/while/body/eval_jaxpr/all_to_all | solution.py:109
  205.8 14.3 %all-to-all-start.1 = ((f32[32,8,128]{2,1,0:T(8,128)}), f32[32,8,128]{2,1,0:T(8,128)S(1)}, u32[]{:S(2)}, u32[]{:S(2)}) async-start(f32[32,8,128]{2,1,0:T(8,128)} %broadcast_in_dim.22), calls=%async_computation.1 | async-start | bytes 262144 | tf_op jit(solution)/shard_map/while/body/eval_jaxpr/all_to_all | solution.py:110
  220.4 5.7 %collective-permute-start.22 = (f32[64,512]{1,0:T(8,128)S(1)}, f32[64,512]{1,0:T(8,128)S(1)}, u32[]{:S(2)}, u32[]{:S(2)}) collective-permute-start(f32[64,512]{1,0:T(8,128)S(1)} %get-tuple-element.144.refs_4_), channel_id=1, source_target_pairs={{0,192},{64,0},{128,64},{192,128},{1,193},{65,1},{129,65},{193,129... | collective-permute-start | bytes 393224 | tf_op jit(solution)/shard_map/ppermute | solution.py:30
  223.5 6.5 %collective-permute-start.21 = (f32[64,512]{1,0:T(8,128)S(1)}, f32[64,512]{1,0:T(8,128)S(1)}, u32[]{:S(2)}, u32[]{:S(2)}) collective-permute-start(f32[64,512]{1,0:T(8,128)S(1)} %get-tuple-element.144.refs_4_), channel_id=1, source_target_pairs={{0,128},{64,192},{128,0},{192,64},{1,129},{65,193},{129,1},{193,65... | collective-permute-start | bytes 393224 | tf_op jit(solution)/shard_map/ppermute | solution.py:30
  223.6 6.5 %collective-permute-start.20 = (f32[64,512]{1,0:T(8,128)S(1)}, f32[64,512]{1,0:T(8,128)S(1)}, u32[]{:S(2)}, u32[]{:S(2)}) collective-permute-start(f32[64,512]{1,0:T(8,128)S(1)} %get-tuple-element.144.refs_4_), channel_id=1, source_target_pairs={{0,64},{64,128},{128,192},{192,0},{1,65},{65,129},{129,193},{193,1... | collective-permute-start | bytes 393224 | tf_op jit(solution)/shard_map/ppermute | solution.py:30
  225.1 5.3 %collective-permute-start.16 = (f32[64,512]{1,0:T(8,128)S(1)}, f32[64,512]{1,0:T(8,128)S(1)}, u32[]{:S(2)}, u32[]{:S(2)}) collective-permute-start(f32[64,512]{1,0:T(8,128)S(1)} %get-tuple-element.144.refs_4_), channel_id=1, source_target_pairs={{0,1},{1,0},{2,3},{3,2},{4,5},{5,4},{6,7},{7,6},{8,9},{9,8},{10,11... | collective-permute-start | bytes 393224 | tf_op jit(solution)/shard_map/ppermute | solution.py:103
  230.1 7.9 %collective-permute-start.23 = (f32[3,64,512]{2,1,0:T(8,128)S(1)}, f32[3,64,512]{2,1,0:T(8,128)S(1)}, u32[]{:S(2)}, u32[]{:S(2)}) collective-permute-start(f32[3,64,512]{2,1,0:T(8,128)S(1)} %pad_maximum_fusion.5), channel_id=1, source_target_pairs={{0,1},{1,0},{2,3},{3,2},{4,5},{5,4},{6,7},{7,6},{8,9},{9,8},{10,11... | collective-permute-start | bytes 1179656 | tf_op jit(solution)/shard_map/ppermute | solution.py:103
  230.7 4.7 %collective-permute-start.19 = (f32[64,64]{1,0:T(8,128)S(1)}, f32[64,64]{1,0:T(8,128)S(1)}, u32[]{:S(2)}, u32[]{:S(2)}) collective-permute-start(f32[64,64]{1,0:T(8,128)S(1)} %convolution_add_fusion.2.refs_0_), channel_id=1, source_target_pairs={{0,192},{64,0},{128,64},{192,128},{1,193},{65,1},{129,65},{193,129... | collective-permute-start | bytes 49160 | tf_op jit(solution)/shard_map/ppermute | solution.py:30
  232.5 5.4 %collective-permute-start.18 = (f32[64,64]{1,0:T(8,128)S(1)}, f32[64,64]{1,0:T(8,128)S(1)}, u32[]{:S(2)}, u32[]{:S(2)}) collective-permute-start(f32[64,64]{1,0:T(8,128)S(1)} %convolution_add_fusion.2.refs_0_), channel_id=1, source_target_pairs={{0,128},{64,192},{128,0},{192,64},{1,129},{65,193},{129,1},{193,65... | collective-permute-start | bytes 49160 | tf_op jit(solution)/shard_map/ppermute | solution.py:30
  232.9 5.0 %collective-permute-start.17 = (f32[64,64]{1,0:T(8,128)S(1)}, f32[64,64]{1,0:T(8,128)S(1)}, u32[]{:S(2)}, u32[]{:S(2)}) collective-permute-start(f32[64,64]{1,0:T(8,128)S(1)} %convolution_add_fusion.2.refs_0_), channel_id=1, source_target_pairs={{0,64},{64,128},{128,192},{192,0},{1,65},{65,129},{129,193},{193,1... | collective-permute-start | bytes 49160 | tf_op jit(solution)/shard_map/ppermute | solution.py:30
  (34 other events, 292.0 us)

commit v4 on v2

--- a/solution.py
+++ b/solution.py
@@ -152,9 +152,9 @@
     far_refs = [far_ref] + [others_ref.at[i] for i in range(3)]
     rest = refs[5:]
     params_ref, momentum_ref, error_out, params_out, momentum_out = rest[:5]
-    left4, mine4, right, left, work = rest[5:]
+    left4, mine4, right4, left, work = rest[5:]
     step = pl.program_id(0)
-    width = right.shape[1]
+    width = right4.shape[1]
     half = width // 2
     quarter = params_ref.shape[0]
     islands = len(near_refs)
@@ -177,17 +177,16 @@
 
         @pl.when(step == s)
         def _(s=s):
-            right[:, pl.ds(near, half)] = near_refs[s][...]
-            right[:, pl.ds(far, half)] = far_refs[s][...]
-
-    high, low = low_high(right[...])
-    right4 = jnp.concatenate([high, low, high, low], axis=0)
-    approx = jnp.dot(left4[...], right4, preferred_element_type=jnp.float32)
+            for ref, at in ((near_refs[s], near), (far_refs[s], far)):
+                high, low = low_high(ref[...])
+                right4[:, pl.ds(at, half)] = jnp.concatenate([high, low, high, low], axis=0)
+
+    approx = jnp.dot(left4[...], right4[...], preferred_element_type=jnp.float32)
     island = lax.rem(me_ref[0] + islands - step, islands)
     columns = pl.ds(pl.multiple_of(island * width, width), width)
     combined = combined_ref[:, columns].astype(jnp.float32)
     error_out[...] = (combined - approx).astype(jnp.bfloat16)
-    mine = jnp.dot(mine4[...], right4, preferred_element_type=jnp.float32)
+    mine = jnp.dot(mine4[...], right4[...], preferred_element_type=jnp.float32)
     moved = momentum_coef * momentum_ref[...] + mine
     momentum_out[...] = moved
     params_out[...] = params_ref[...] - outer_rate * (mine + momentum_coef * moved)
@@ -216,7 +215,7 @@
             scratch_shapes=[
                 pltpu.VMEM((rows, 4 * rank), jnp.bfloat16),
                 pltpu.VMEM((quarter, 4 * rank), jnp.bfloat16),
-                pltpu.VMEM((rank, width), jnp.float32),
+                pltpu.VMEM((4 * rank, width), jnp.bfloat16),
                 pltpu.VMEM((rows, rank), jnp.float32),
                 pltpu.VMEM((rank, 2 * rank), jnp.float32),
             ],

time: 250 us -> 250 us (level)
  no operation moved by 1% of the time
where the time goes in v4:
time: 250 us; the launch traced here: 248 us
  waiting for transfers between devices  111 us (44%)
  starting transfers between devices  78.6 us (31%)
  Pallas kernels  26.9 us (11%)
  other arithmetic  13.1 us (5%)
  matrix products  12.9 us (5%)
  local copies, waits for them, and re-layouts  4.45 us (2%)
    all_to_all x4, waiting for transfers between devices, row_sum(): full = lax.all_to_all(jnp.broadcast_to(own, parts.shape), ROW, 0, 0)  39.8 us
    all_to_all x4, waiting for transfers between devices, row_sum(): own = jnp.sum(lax.all_to_all(parts, ROW, 0, 0), axis=0)  32.3 us
    ppermute x18, waiting for transfers between devices, island_parts(): return [v] + [lax.ppermute(v, 'x', ring(4, s)) for s in (1, 2, 3)]  28.7 us
    ppermute x18, starting transfers between devices, island_parts(): return [v] + [lax.ppermute(v, 'x', ring(4, s)) for s in (1, 2, 3)]  27.7 us
    all_to_all x4, starting transfers between devices, row_sum(): own = jnp.sum(lax.all_to_all(parts, ROW, 0, 0), axis=0)  24.4 us
    all_to_all x4, starting transfers between devices, row_sum(): full = lax.all_to_all(jnp.broadcast_to(own, parts.shape), ROW, 0, 0)  15.6 us
    dot_general x35, matrix products, dot(): lax.dot_general(a, b, (((ca,), (cb,)), ((), ())), precision=lax.Precision...  12.2 us
    pallas_call x3, Pallas kernels, inverse_factor(): pl.pallas_call(factor_kernel, out_shape=jax.ShapeDtypeStruct((n, n), jnp....  9.5 us
  transfers between devices with their start and end apart: 44, of which 29 were waited for; matrix products, arithmetic and copies ran while one was open for 7% of the time, Pallas kernels for 7%

profile of v4, /device:TPU:2, one launch (start us, length us, event | category | flops | bytes accessed | tf_op | source)
XLA Modules:
  0.0 248.1 jit_solution(5132644021205224742)
XLA Ops:
  2.4 2.2 reduce-precision_convert_fusion.refs_12_
  17.9 3.3 %collective-permute-start.13 = (f32[112,1024]{1,0:T(8,128)}, f32[112,1024]{1,0:T(8,128)}, u32[]{:S(2)}, u32[]{:S(2)}) collective-permute-start(f32[112,1024]{1,0:T(8,128)} %get-tuple-element.134), channel_id=1, source_target_pairs={{0,192},{64,0},{128,64},{192,128},{1,193},{65,1},{129,65},{193,129... | collective-permute-start | bytes 1376264 | tf_op jit(solution)/shard_map/ppermute | solution.py:256
  25.5 11.7 %collective-permute-done.6 = f32[64,224]{1,0:T(8,128)S(1)} collective-permute-done((f32[64,224]{1,0:T(8,128)S(1)}, f32[64,224]{1,0:T(8,128)S(1)}, u32[]{:S(2)}, u32[]{:S(2)}) %collective-permute-start.6) | collective-permute-done | bytes 57376 | tf_op jit(solution)/shard_map/ppermute | solution.py:30
  43.7 4.8 %collective-permute-done.12 = f32[112,1024]{1,0:T(8,128)S(1)} collective-permute-done((f32[112,1024]{1,0:T(8,128)S(1)}, f32[112,1024]{1,0:T(8,128)S(1)}, u32[]{:S(2)}, u32[]{:S(2)}) %collective-permute-start.12) | collective-permute-done | bytes 458784 | tf_op jit(solution)/shard_map/ppermute | solution.py:256
  52.2 12.9 %all-to-all-start.2 = ((f32[32,8,128]{2,1,0:T(8,128)}), f32[32,8,128]{2,1,0:T(8,128)S(1)}, u32[]{:S(2)}, u32[]{:S(2)}) async-start(f32[32,8,128]{2,1,0:T(8,128)} %bitcast.18), calls=%async_computation.2 | async-start | bytes 262144 | tf_op jit(solution)/shard_map/all_to_all | solution.py:109
  65.2 10.5 %all-to-all-done.2 = f32[32,8,128]{2,1,0:T(8,128)S(1)} async-done(((f32[32,8,128]{2,1,0:T(8,128)}), f32[32,8,128]{2,1,0:T(8,128)S(1)}, u32[]{:S(2)}, u32[]{:S(2)}) %all-to-all-start.2) | async-done | bytes 131104 | tf_op jit(solution)/shard_map/all_to_all | solution.py:109
  76.4 4.0 %all-to-all-start.3 = ((f32[32,8,128]{2,1,0:T(8,128)}), f32[32,8,128]{2,1,0:T(8,128)S(1)}, u32[]{:S(2)}, u32[]{:S(2)}) async-start(f32[32,8,128]{2,1,0:T(8,128)} %broadcast_in_dim.17), calls=%async_computation.3 | async-start | bytes 262144 | tf_op jit(solution)/shard_map/all_to_all | solution.py:110
  80.6 10.3 %all-to-all-done.3 = f32[32,8,128]{2,1,0:T(8,128)S(1)} async-done(((f32[32,8,128]{2,1,0:T(8,128)}), f32[32,8,128]{2,1,0:T(8,128)S(1)}, u32[]{:S(2)}, u32[]{:S(2)}) %all-to-all-start.3) | async-done | bytes 131104 | tf_op jit(solution)/shard_map/all_to_all | solution.py:110
  90.9 129.2 %while.20 = (s32[]{:T(128)}, f32[64,512]{1,0:T(8,128)S(1)}, f32[64,512]{1,0:T(8,128)S(1)}, f32[64,512]{1,0:T(8,128)S(1)}, f32[64,224]{1,0:T(8,128)}, /*index=5*/...) while((s32[]{:T(128)}, f32[64,512]{1,0:T(8,128)S(1)}, ...), condition=%wide.region_3.4_spmd, body=%wide.region_1.3_spmd.sunk | while | flops 469933056 | bytes 24887784 | solution.py:345
  93.1 2.7 %collective-permute-start.3 = (f32[64,256]{1,0:T(8,128)S(1)}, f32[64,256]{1,0:T(8,128)S(1)}, u32[]{:S(2)}, u32[]{:S(2)}) collective-permute-start(f32[64,256]{1,0:T(8,128)S(1)} %pad_maximum_fusion.7), channel_id=1, source_target_pairs={{0,128},{64,192},{128,0},{192,64},{1,129},{65,193},{129,1},{193,65... | collective-permute-start | bytes 196616 | tf_op jit(solution)/shard_map/while/body/eval_jaxpr/ppermute | solution.py:30
  104.0 3.9 %all-to-all-start = ((f32[32,8,128]{2,1,0:T(8,128)}), f32[32,8,128]{2,1,0:T(8,128)S(1)}, u32[]{:S(2)}, u32[]{:S(2)}) async-start(f32[32,8,128]{2,1,0:T(8,128)} %bitcast.106), calls=%async_computation | async-start | bytes 262144 | tf_op jit(solution)/shard_map/while/body/eval_jaxpr/all_to_all | solution.py:109
  108.7 3.2 %factor.3 = f32[64,64]{1,0:T(8,128)S(1)} custom-call(f32[64,64]{1,0:T(8,128)} %pad_maximum_fusion.8.gram_ref), custom_call_target="tpu_custom_call" | custom-call | flops 16777216 | bytes 16777216 | tf_op jit(solution)/shard_map/while/body/eval_jaxpr/factor/pallas_call | solution.py:82
  111.9 7.3 %all-to-all-done = f32[32,8,128]{2,1,0:T(8,128)S(1)} async-done(((f32[32,8,128]{2,1,0:T(8,128)}), f32[32,8,128]{2,1,0:T(8,128)S(1)}, u32[]{:S(2)}, u32[]{:S(2)}) %all-to-all-start) | async-done | bytes 131104 | tf_op jit(solution)/shard_map/while/body/eval_jaxpr/all_to_all | solution.py:109
  119.8 3.9 %all-to-all-start.1 = ((f32[32,8,128]{2,1,0:T(8,128)}), f32[32,8,128]{2,1,0:T(8,128)S(1)}, u32[]{:S(2)}, u32[]{:S(2)}) async-start(f32[32,8,128]{2,1,0:T(8,128)} %broadcast_in_dim.22), calls=%async_computation.1 | async-start | bytes 262144 | tf_op jit(solution)/shard_map/while/body/eval_jaxpr/all_to_all | solution.py:110
  124.2 9.9 %all-to-all-done.1 = f32[32,8,128]{2,1,0:T(8,128)S(1)} async-done(((f32[32,8,128]{2,1,0:T(8,128)}), f32[32,8,128]{2,1,0:T(8,128)S(1)}, u32[]{:S(2)}, u32[]{:S(2)}) %all-to-all-start.1) | async-done | bytes 131104 | tf_op jit(solution)/shard_map/while/body/eval_jaxpr/all_to_all | solution.py:110
  140.5 2.3 collective-permute-done.3
  146.9 3.9 %all-to-all-start = ((f32[32,8,128]{2,1,0:T(8,128)}), f32[32,8,128]{2,1,0:T(8,128)S(1)}, u32[]{:S(2)}, u32[]{:S(2)}) async-start(f32[32,8,128]{2,1,0:T(8,128)} %bitcast.106), calls=%async_computation | async-start | bytes 262144 | tf_op jit(solution)/shard_map/while/body/eval_jaxpr/all_to_all | solution.py:109
  151.5 3.2 %factor.3 = f32[64,64]{1,0:T(8,128)S(1)} custom-call(f32[64,64]{1,0:T(8,128)} %pad_maximum_fusion.8.gram_ref), custom_call_target="tpu_custom_call" | custom-call | flops 16777216 | bytes 16777216 | tf_op jit(solution)/shard_map/while/body/eval_jaxpr/factor/pallas_call | solution.py:82
  154.7 7.3 %all-to-all-done = f32[32,8,128]{2,1,0:T(8,128)S(1)} async-done(((f32[32,8,128]{2,1,0:T(8,128)}), f32[32,8,128]{2,1,0:T(8,128)S(1)}, u32[]{:S(2)}, u32[]{:S(2)}) %all-to-all-start) | async-done | bytes 131104 | tf_op jit(solution)/shard_map/while/body/eval_jaxpr/all_to_all | solution.py:109
  162.7 3.9 %all-to-all-start.1 = ((f32[32,8,128]{2,1,0:T(8,128)}), f32[32,8,128]{2,1,0:T(8,128)S(1)}, u32[]{:S(2)}, u32[]{:S(2)}) async-start(f32[32,8,128]{2,1,0:T(8,128)} %broadcast_in_dim.22), calls=%async_computation.1 | async-start | bytes 262144 | tf_op jit(solution)/shard_map/while/body/eval_jaxpr/all_to_all | solution.py:110
  167.1 9.9 %all-to-all-done.1 = f32[32,8,128]{2,1,0:T(8,128)S(1)} async-done(((f32[32,8,128]{2,1,0:T(8,128)}), f32[32,8,128]{2,1,0:T(8,128)S(1)}, u32[]{:S(2)}, u32[]{:S(2)}) %all-to-all-start.1) | async-done | bytes 131104 | tf_op jit(solution)/shard_map/while/body/eval_jaxpr/all_to_all | solution.py:110
  189.7 3.9 %all-to-all-start = ((f32[32,8,128]{2,1,0:T(8,128)}), f32[32,8,128]{2,1,0:T(8,128)S(1)}, u32[]{:S(2)}, u32[]{:S(2)}) async-start(f32[32,8,128]{2,1,0:T(8,128)} %bitcast.106), calls=%async_computation | async-start | bytes 262144 | tf_op jit(solution)/shard_map/while/body/eval_jaxpr/all_to_all | solution.py:109
  194.4 3.2 %factor.3 = f32[64,64]{1,0:T(8,128)S(1)} custom-call(f32[64,64]{1,0:T(8,128)} %pad_maximum_fusion.8.gram_ref), custom_call_target="tpu_custom_call" | custom-call | flops 16777216 | bytes 16777216 | tf_op jit(solution)/shard_map/while/body/eval_jaxpr/factor/pallas_call | solution.py:82
  197.6 7.3 %all-to-all-done = f32[32,8,128]{2,1,0:T(8,128)S(1)} async-done(((f32[32,8,128]{2,1,0:T(8,128)}), f32[32,8,128]{2,1,0:T(8,128)S(1)}, u32[]{:S(2)}, u32[]{:S(2)}) %all-to-all-start) | async-done | bytes 131104 | tf_op jit(solution)/shard_map/while/body/eval_jaxpr/all_to_all | solution.py:109
  205.5 3.9 %all-to-all-start.1 = ((f32[32,8,128]{2,1,0:T(8,128)}), f32[32,8,128]{2,1,0:T(8,128)S(1)}, u32[]{:S(2)}, u32[]{:S(2)}) async-start(f32[32,8,128]{2,1,0:T(8,128)} %broadcast_in_dim.22), calls=%async_computation.1 | async-start | bytes 262144 | tf_op jit(solution)/shard_map/while/body/eval_jaxpr/all_to_all | solution.py:110
  209.9 9.9 %all-to-all-done.1 = f32[32,8,128]{2,1,0:T(8,128)S(1)} async-done(((f32[32,8,128]{2,1,0:T(8,128)}), f32[32,8,128]{2,1,0:T(8,128)S(1)}, u32[]{:S(2)}, u32[]{:S(2)}) %all-to-all-start.1) | async-done | bytes 131104 | tf_op jit(solution)/shard_map/while/body/eval_jaxpr/all_to_all | solution.py:110
  220.1 3.0 %collective-permute-start.22 = (f32[64,512]{1,0:T(8,128)S(1)}, f32[64,512]{1,0:T(8,128)S(1)}, u32[]{:S(2)}, u32[]{:S(2)}) collective-permute-start(f32[64,512]{1,0:T(8,128)S(1)} %get-tuple-element.138.refs_4_), channel_id=1, source_target_pairs={{0,192},{64,0},{128,64},{192,128},{1,193},{65,1},{129,65},{193,129... | collective-permute-start | bytes 393224 | tf_op jit(solution)/shard_map/ppermute | solution.py:30
  223.1 2.5 %collective-permute-start.20 = (f32[64,512]{1,0:T(8,128)S(1)}, f32[64,512]{1,0:T(8,128)S(1)}, u32[]{:S(2)}, u32[]{:S(2)}) collective-permute-start(f32[64,512]{1,0:T(8,128)S(1)} %get-tuple-element.138.refs_4_), channel_id=1, source_target_pairs={{0,64},{64,128},{128,192},{192,0},{1,65},{65,129},{129,193},{193,1... | collective-permute-start | bytes 393224 | tf_op jit(solution)/shard_map/ppermute | solution.py:30
  225.6 3.9 %collective-permute-done.21.refs_6_ = f32[64,512]{1,0:T(8,128)S(1)} collective-permute-done((f32[64,512]{1,0:T(8,128)S(1)}, f32[64,512]{1,0:T(8,128)S(1)}, u32[]{:S(2)}, u32[]{:S(2)}) %collective-permute-start.21) | collective-permute-done | bytes 131104 | tf_op jit(solution)/shard_map/ppermute | solution.py:30
  230.2 2.6 %collective-permute-start.19 = (f32[64,64]{1,0:T(8,128)S(1)}, f32[64,64]{1,0:T(8,128)S(1)}, u32[]{:S(2)}, u32[]{:S(2)}) collective-permute-start(f32[64,64]{1,0:T(8,128)S(1)} %convolution_add_fusion.2.refs_0_), channel_id=1, source_target_pairs={{0,192},{64,0},{128,64},{192,128},{1,193},{65,1},{129,65},{193,129... | collective-permute-start | bytes 49160 | tf_op jit(solution)/shard_map/ppermute | solution.py:30
  235.0 3.3 %collective-permute-done.18.refs_2_ = f32[64,64]{1,0:T(8,128)S(1)} collective-permute-done((f32[64,64]{1,0:T(8,128)S(1)}, f32[64,64]{1,0:T(8,128)S(1)}, u32[]{:S(2)}, u32[]{:S(2)}) %collective-permute-start.18) | collective-permute-done | bytes 16416 | tf_op jit(solution)/shard_map/ppermute | solution.py:30
  239.1 8.9 %finish.1 = (bf16[224,4096]{1,0:T(8,128)(2,1)}, f32[56,4096]{1,0:T(8,128)}, f32[56,4096]{1,0:T(8,128)}) custom-call(s32[1]{0:T(128)} %bitcast.8.me_ref, s32[1]{0:T(128)} %bitcast.9.core_ref, f32[64,64]{1,0:T(8,128)} %copy-done.13, f32[64,64]{1,0:T(8,128)} %copy-done.16, f32[64,64]{1,0:T(8,128)} %copy-done.15, f32[64,64]{1,0:T(8,128)} %copy-done.14, ...), custom_call_target="tpu_custom_call" | custom-call | tf_op jit(solution)/shard_map/finish/pallas_call | solution.py:207
  (187 shorter events, 73.7 us)
Async XLA Ops:
  5.9 12.0 %collective-permute-start.7 = (f32[64,224]{1,0:T(8,128)S(1)}, f32[64,224]{1,0:T(8,128)S(1)}, u32[]{:S(2)}, u32[]{:S(2)}) collective-permute-start(f32[64,224]{1,0:T(8,128)S(1)} %slice_add_fusion.6), channel_id=1, source_target_pairs={{0,64},{64,128},{128,192},{192,0},{1,65},{65,129},{129,193},{193,1... | collective-permute-start | bytes 172040 | tf_op jit(solution)/shard_map/ppermute | solution.py:30
  7.5 13.7 %collective-permute-start.8 = (f32[64,224]{1,0:T(8,128)S(1)}, f32[64,224]{1,0:T(8,128)S(1)}, u32[]{:S(2)}, u32[]{:S(2)}) collective-permute-start(f32[64,224]{1,0:T(8,128)S(1)} %slice_add_fusion.6), channel_id=1, source_target_pairs={{0,192},{64,0},{128,64},{192,128},{1,193},{65,1},{129,65},{193,129... | collective-permute-start | bytes 172040 | tf_op jit(solution)/shard_map/ppermute | solution.py:30
  10.4 28.0 %collective-permute-start.10 = (f32[112,1024]{1,0:T(8,128)}, f32[112,1024]{1,0:T(8,128)S(1)}, u32[]{:S(2)}, u32[]{:S(2)}) collective-permute-start(f32[112,1024]{1,0:T(8,128)} %get-tuple-element.130), channel_id=1, source_target_pairs={{0,64},{64,128},{128,192},{192,0},{1,65},{65,129},{129,193},{193,1... | collective-permute-start | bytes 1376264 | tf_op jit(solution)/shard_map/ppermute | solution.py:256
  13.7 23.5 %collective-permute-start.9 = (f32[112,1024]{1,0:T(8,128)}, f32[112,1024]{1,0:T(8,128)S(1)}, u32[]{:S(2)}, u32[]{:S(2)}) collective-permute-start(f32[112,1024]{1,0:T(8,128)} %get-tuple-element.128), channel_id=1, source_target_pairs={{0,192},{64,0},{128,64},{192,128},{1,193},{65,1},{129,65},{193,129... | collective-permute-start | bytes 1376264 | tf_op jit(solution)/shard_map/ppermute | solution.py:256
  17.9 20.6 %collective-permute-start.11 = (f32[112,1024]{1,0:T(8,128)}, f32[112,1024]{1,0:T(8,128)}, u32[]{:S(2)}, u32[]{:S(2)}) collective-permute-start(f32[112,1024]{1,0:T(8,128)} %get-tuple-element.132), channel_id=1, source_target_pairs={{0,64},{64,128},{128,192},{192,0},{1,65},{65,129},{129,193},{193,1... | collective-permute-start | bytes 1376264 | tf_op jit(solution)/shard_map/ppermute | solution.py:256
  17.9 21.8 %collective-permute-start.13 = (f32[112,1024]{1,0:T(8,128)}, f32[112,1024]{1,0:T(8,128)}, u32[]{:S(2)}, u32[]{:S(2)}) collective-permute-start(f32[112,1024]{1,0:T(8,128)} %get-tuple-element.134), channel_id=1, source_target_pairs={{0,192},{64,0},{128,64},{192,128},{1,193},{65,1},{129,65},{193,129... | collective-permute-start | bytes 1376264 | tf_op jit(solution)/shard_map/ppermute | solution.py:256
  21.2 16.0 %collective-permute-start.6 = (f32[64,224]{1,0:T(8,128)S(1)}, f32[64,224]{1,0:T(8,128)S(1)}, u32[]{:S(2)}, u32[]{:S(2)}) collective-permute-start(f32[64,224]{1,0:T(8,128)S(1)} %slice_add_fusion.6), channel_id=1, source_target_pairs={{0,128},{64,192},{128,0},{192,64},{1,129},{65,193},{129,1},{193,65... | collective-permute-start | bytes 172040 | tf_op jit(solution)/shard_map/ppermute | solution.py:30
  39.6 9.0 %collective-permute-start.12 = (f32[112,1024]{1,0:T(8,128)S(1)}, f32[112,1024]{1,0:T(8,128)S(1)}, u32[]{:S(2)}, u32[]{:S(2)}) collective-permute-start(f32[112,1024]{1,0:T(8,128)S(1)} %add.128), channel_id=1, source_target_pairs={{0,64},{64,128},{128,192},{192,0},{1,65},{65,129},{129,193},{193,1... | collective-permute-start | bytes 1376264 | tf_op jit(solution)/shard_map/ppermute | solution.py:256
  40.8 9.0 %collective-permute-start.14 = (f32[112,1024]{1,0:T(8,128)S(1)}, f32[112,1024]{1,0:T(8,128)S(1)}, u32[]{:S(2)}, u32[]{:S(2)}) collective-permute-start(f32[112,1024]{1,0:T(8,128)S(1)} %add.130), channel_id=1, source_target_pairs={{0,192},{64,0},{128,64},{192,128},{1,193},{65,1},{129,65},{193,129... | collective-permute-start | bytes 1376264 | tf_op jit(solution)/shard_map/ppermute | solution.py:256
  52.2 23.5 %all-to-all-start.2 = ((f32[32,8,128]{2,1,0:T(8,128)}), f32[32,8,128]{2,1,0:T(8,128)S(1)}, u32[]{:S(2)}, u32[]{:S(2)}) async-start(f32[32,8,128]{2,1,0:T(8,128)} %bitcast.18), calls=%async_computation.2 | async-start | bytes 262144 | tf_op jit(solution)/shard_map/all_to_all | solution.py:109
  76.4 14.5 %all-to-all-start.3 = ((f32[32,8,128]{2,1,0:T(8,128)}), f32[32,8,128]{2,1,0:T(8,128)S(1)}, u32[]{:S(2)}, u32[]{:S(2)}) async-start(f32[32,8,128]{2,1,0:T(8,128)} %broadcast_in_dim.17), calls=%async_computation.3 | async-start | bytes 262144 | tf_op jit(solution)/shard_map/all_to_all | solution.py:110
  93.1 6.5 %collective-permute-start.3 = (f32[64,256]{1,0:T(8,128)S(1)}, f32[64,256]{1,0:T(8,128)S(1)}, u32[]{:S(2)}, u32[]{:S(2)}) collective-permute-start(f32[64,256]{1,0:T(8,128)S(1)} %pad_maximum_fusion.7), channel_id=1, source_target_pairs={{0,128},{64,192},{128,0},{192,64},{1,129},{65,193},{129,1},{193,65... | collective-permute-start | bytes 196616 | tf_op jit(solution)/shard_map/while/body/eval_jaxpr/ppermute | solution.py:30
  101.3 6.6 %collective-permute-start.4 = (f32[64,32]{1,0:T(8,128)S(1)}, f32[64,32]{1,0:T(8,128)S(1)}, u32[]{:S(2)}, u32[]{:S(2)}) collective-permute-start(f32[64,32]{1,0:T(8,128)S(1)} %slice.173), channel_id=1, source_target_pairs={{0,1},{1,0},{2,3},{3,2},{4,5},{5,4},{6,7},{7,6},{8,9},{9,8},{10,11... | collective-permute-start | bytes 24584 | tf_op jit(solution)/shard_map/while/body/eval_jaxpr/ppermute | solution.py:103
  104.0 15.1 %all-to-all-start = ((f32[32,8,128]{2,1,0:T(8,128)}), f32[32,8,128]{2,1,0:T(8,128)S(1)}, u32[]{:S(2)}, u32[]{:S(2)}) async-start(f32[32,8,128]{2,1,0:T(8,128)} %bitcast.106), calls=%async_computation | async-start | bytes 262144 | tf_op jit(solution)/shard_map/while/body/eval_jaxpr/all_to_all | solution.py:109
  119.8 14.3 %all-to-all-start.1 = ((f32[32,8,128]{2,1,0:T(8,128)}), f32[32,8,128]{2,1,0:T(8,128)S(1)}, u32[]{:S(2)}, u32[]{:S(2)}) async-start(f32[32,8,128]{2,1,0:T(8,128)} %broadcast_in_dim.22), calls=%async_computation.1 | async-start | bytes 262144 | tf_op jit(solution)/shard_map/while/body/eval_jaxpr/all_to_all | solution.py:110
  136.7 6.1 %collective-permute-start.3 = (f32[64,256]{1,0:T(8,128)S(1)}, f32[64,256]{1,0:T(8,128)S(1)}, u32[]{:S(2)}, u32[]{:S(2)}) collective-permute-start(f32[64,256]{1,0:T(8,128)S(1)} %pad_maximum_fusion.7), channel_id=1, source_target_pairs={{0,128},{64,192},{128,0},{192,64},{1,129},{65,193},{129,1},{193,65... | collective-permute-start | bytes 196616 | tf_op jit(solution)/shard_map/while/body/eval_jaxpr/ppermute | solution.py:30
  138.4 5.4 %collective-permute-start.2 = (f32[64,256]{1,0:T(8,128)S(1)}, f32[64,256]{1,0:T(8,128)S(1)}, u32[]{:S(2)}, u32[]{:S(2)}) collective-permute-start(f32[64,256]{1,0:T(8,128)S(1)} %pad_maximum_fusion.7), channel_id=1, source_target_pairs={{0,192},{64,0},{128,64},{192,128},{1,193},{65,1},{129,65},{193,129... | collective-permute-start | bytes 196616 | tf_op jit(solution)/shard_map/while/body/eval_jaxpr/ppermute | solution.py:30
  144.2 6.6 %collective-permute-start.4 = (f32[64,32]{1,0:T(8,128)S(1)}, f32[64,32]{1,0:T(8,128)S(1)}, u32[]{:S(2)}, u32[]{:S(2)}) collective-permute-start(f32[64,32]{1,0:T(8,128)S(1)} %slice.173), channel_id=1, source_target_pairs={{0,1},{1,0},{2,3},{3,2},{4,5},{5,4},{6,7},{7,6},{8,9},{9,8},{10,11... | collective-permute-start | bytes 24584 | tf_op jit(solution)/shard_map/while/body/eval_jaxpr/ppermute | solution.py:103
  146.9 15.1 %all-to-all-start = ((f32[32,8,128]{2,1,0:T(8,128)}), f32[32,8,128]{2,1,0:T(8,128)S(1)}, u32[]{:S(2)}, u32[]{:S(2)}) async-start(f32[32,8,128]{2,1,0:T(8,128)} %bitcast.106), calls=%async_computation | async-start | bytes 262144 | tf_op jit(solution)/shard_map/while/body/eval_jaxpr/all_to_all | solution.py:109
  162.7 14.3 %all-to-all-start.1 = ((f32[32,8,128]{2,1,0:T(8,128)}), f32[32,8,128]{2,1,0:T(8,128)S(1)}, u32[]{:S(2)}, u32[]{:S(2)}) async-start(f32[32,8,128]{2,1,0:T(8,128)} %broadcast_in_dim.22), calls=%async_computation.1 | async-start | bytes 262144 | tf_op jit(solution)/shard_map/while/body/eval_jaxpr/all_to_all | solution.py:110
  179.6 5.9 %collective-permute-start.3 = (f32[64,256]{1,0:T(8,128)S(1)}, f32[64,256]{1,0:T(8,128)S(1)}, u32[]{:S(2)}, u32[]{:S(2)}) collective-permute-start(f32[64,256]{1,0:T(8,128)S(1)} %pad_maximum_fusion.7), channel_id=1, source_target_pairs={{0,128},{64,192},{128,0},{192,64},{1,129},{65,193},{129,1},{193,65... | collective-permute-start | bytes 196616 | tf_op jit(solution)/shard_map/while/body/eval_jaxpr/ppermute | solution.py:30
  181.7 5.1 %collective-permute-start.2 = (f32[64,256]{1,0:T(8,128)S(1)}, f32[64,256]{1,0:T(8,128)S(1)}, u32[]{:S(2)}, u32[]{:S(2)}) collective-permute-start(f32[64,256]{1,0:T(8,128)S(1)} %pad_maximum_fusion.7), channel_id=1, source_target_pairs={{0,192},{64,0},{128,64},{192,128},{1,193},{65,1},{129,65},{193,129... | collective-permute-start | bytes 196616 | tf_op jit(solution)/shard_map/while/body/eval_jaxpr/ppermute | solution.py:30
  187.0 6.6 %collective-permute-start.4 = (f32[64,32]{1,0:T(8,128)S(1)}, f32[64,32]{1,0:T(8,128)S(1)}, u32[]{:S(2)}, u32[]{:S(2)}) collective-permute-start(f32[64,32]{1,0:T(8,128)S(1)} %slice.173), channel_id=1, source_target_pairs={{0,1},{1,0},{2,3},{3,2},{4,5},{5,4},{6,7},{7,6},{8,9},{9,8},{10,11... | collective-permute-start | bytes 24584 | tf_op jit(solution)/shard_map/while/body/eval_jaxpr/ppermute | solution.py:103
  189.7 15.1 %all-to-all-start = ((f32[32,8,128]{2,1,0:T(8,128)}), f32[32,8,128]{2,1,0:T(8,128)S(1)}, u32[]{:S(2)}, u32[]{:S(2)}) async-start(f32[32,8,128]{2,1,0:T(8,128)} %bitcast.106), calls=%async_computation | async-start | bytes 262144 | tf_op jit(solution)/shard_map/while/body/eval_jaxpr/all_to_all | solution.py:109
  205.5 14.3 %all-to-all-start.1 = ((f32[32,8,128]{2,1,0:T(8,128)}), f32[32,8,128]{2,1,0:T(8,128)S(1)}, u32[]{:S(2)}, u32[]{:S(2)}) async-start(f32[32,8,128]{2,1,0:T(8,128)} %broadcast_in_dim.22), calls=%async_computation.1 | async-start | bytes 262144 | tf_op jit(solution)/shard_map/while/body/eval_jaxpr/all_to_all | solution.py:110
  220.1 5.5 %collective-permute-start.22 = (f32[64,512]{1,0:T(8,128)S(1)}, f32[64,512]{1,0:T(8,128)S(1)}, u32[]{:S(2)}, u32[]{:S(2)}) collective-permute-start(f32[64,512]{1,0:T(8,128)S(1)} %get-tuple-element.138.refs_4_), channel_id=1, source_target_pairs={{0,192},{64,0},{128,64},{192,128},{1,193},{65,1},{129,65},{193,129... | collective-permute-start | bytes 393224 | tf_op jit(solution)/shard_map/ppermute | solution.py:30
  223.1 6.5 %collective-permute-start.21 = (f32[64,512]{1,0:T(8,128)S(1)}, f32[64,512]{1,0:T(8,128)S(1)}, u32[]{:S(2)}, u32[]{:S(2)}) collective-permute-start(f32[64,512]{1,0:T(8,128)S(1)} %get-tuple-element.138.refs_4_), channel_id=1, source_target_pairs={{0,128},{64,192},{128,0},{192,64},{1,129},{65,193},{129,1},{193,65... | collective-permute-start | bytes 393224 | tf_op jit(solution)/shard_map/ppermute | solution.py:30
  223.1 6.4 %collective-permute-start.20 = (f32[64,512]{1,0:T(8,128)S(1)}, f32[64,512]{1,0:T(8,128)S(1)}, u32[]{:S(2)}, u32[]{:S(2)}) collective-permute-start(f32[64,512]{1,0:T(8,128)S(1)} %get-tuple-element.138.refs_4_), channel_id=1, source_target_pairs={{0,64},{64,128},{128,192},{192,0},{1,65},{65,129},{129,193},{193,1... | collective-permute-start | bytes 393224 | tf_op jit(solution)/shard_map/ppermute | solution.py:30
  229.6 8.7 %collective-permute-start.23 = (f32[3,64,512]{2,1,0:T(8,128)S(1)}, f32[3,64,512]{2,1,0:T(8,128)S(1)}, u32[]{:S(2)}, u32[]{:S(2)}) collective-permute-start(f32[3,64,512]{2,1,0:T(8,128)S(1)} %pad_maximum_fusion.4), channel_id=1, source_target_pairs={{0,1},{1,0},{2,3},{3,2},{4,5},{5,4},{6,7},{7,6},{8,9},{9,8},{10,11... | collective-permute-start | bytes 1179656 | tf_op jit(solution)/shard_map/ppermute | solution.py:103
  230.2 4.7 %collective-permute-start.19 = (f32[64,64]{1,0:T(8,128)S(1)}, f32[64,64]{1,0:T(8,128)S(1)}, u32[]{:S(2)}, u32[]{:S(2)}) collective-permute-start(f32[64,64]{1,0:T(8,128)S(1)} %convolution_add_fusion.2.refs_0_), channel_id=1, source_target_pairs={{0,192},{64,0},{128,64},{192,128},{1,193},{65,1},{129,65},{193,129... | collective-permute-start | bytes 49160 | tf_op jit(solution)/shard_map/ppermute | solution.py:30
  232.8 5.4 %collective-permute-start.18 = (f32[64,64]{1,0:T(8,128)S(1)}, f32[64,64]{1,0:T(8,128)S(1)}, u32[]{:S(2)}, u32[]{:S(2)}) collective-permute-start(f32[64,64]{1,0:T(8,128)S(1)} %convolution_add_fusion.2.refs_0_), channel_id=1, source_target_pairs={{0,128},{64,192},{128,0},{192,64},{1,129},{65,193},{129,1},{193,65... | collective-permute-start | bytes 49160 | tf_op jit(solution)/shard_map/ppermute | solution.py:30
  232.8 5.4 %collective-permute-start.17 = (f32[64,64]{1,0:T(8,128)S(1)}, f32[64,64]{1,0:T(8,128)S(1)}, u32[]{:S(2)}, u32[]{:S(2)}) collective-permute-start(f32[64,64]{1,0:T(8,128)S(1)} %convolution_add_fusion.2.refs_0_), channel_id=1, source_target_pairs={{0,64},{64,128},{128,192},{192,0},{1,65},{65,129},{129,193},{193,1... | collective-permute-start | bytes 49160 | tf_op jit(solution)/shard_map/ppermute | solution.py:30
  (33 other events, 287.7 us)
